TPU v7x, 256 devices: a whole 4x4x8 slice. The times are simulated.
256 devices in a mesh: row: 16 (over z, core), col: 8 (over x_hi, y), feat: 2 (over x_lo).
Axes of the slice: x: 4 (x_hi: 2, x_lo: 2; x = x_hi * 2 + x_lo), y: 4, z: 8, core: 2. Of those that a mesh axis runs over, the one named last changes fastest.
Arguments:
- features: bfloat16 [65536, 256], P(('col', 'row'), 'feat'), may hold values from -6 to 6
- tile_rows: int32 [16, 8, 256], P('row', 'col'), may hold values from 0 to 31, as said below
- tile_cols: int32 [16, 8, 256], P('row', 'col'), may hold values from 0 to 63
- tile_count: int32 [16, 8], P('row', 'col'), may hold values from 64 to 256, as said below
- tile_values: bfloat16 [16, 8, 256, 128, 128], P('row', 'col'), may hold values from -0.21875 to 0.21875
- weights: bfloat16 [256, 256], replicated, may hold values from -0.375 to 0.375
- cotangent: bfloat16 [65536, 256], P(('row', 'col'), 'feat'), may hold values from -6 to 6
Outputs:
- activated: bfloat16 [65536, 256], P(('row', 'col'), 'feat')
- feature_grad: bfloat16 [65536, 256], P(('col', 'row'), 'feat')
- weight_grad: float32 [256, 256], P('feat')
Inputs may be any that keep to these rules, and one draw needn't show every extreme that they name: `tile_rows`: block rows of a cell, unevenly loaded. `tile_count`: some cell has all 256 slots live.
All inputs are finite; a program needn't handle non-finite values.
Results may differ from a plain program's by a relative error of at most 0.027.
Values may be sent and summed in bfloat16 or wider, within the bound.
A program may use at most 128 MiB of HBM per device.

v0:
```python
import jax
import jax.numpy as jnp
from jax import lax
from jax.sharding import PartitionSpec as P


def shards(features, tile_rows, tile_cols, tile_count, tile_values, weights, cotangent):
    width = tile_values.shape[-1]
    slots = tile_values.shape[2]
    local_tiles = tile_values[0, 0]
    block_rows = tile_rows[0, 0]
    block_cols = tile_cols[0, 0]
    live_mask = (jnp.arange(slots) < tile_count[0, 0]).astype(jnp.float32)
    n_rowdev = lax.axis_size("row")
    n_coldev = lax.axis_size("col")
    local_blocks = features.shape[0] // width
    feat_half = features.shape[1]
    feat_index = lax.axis_index("feat")
    row_blocks = local_blocks * n_coldev
    col_blocks = local_blocks * n_rowdev
    node_total = features.shape[0] * n_rowdev * n_coldev
    panel = lax.all_gather(features, "row", axis=0, tiled=True)
    gathered = panel.reshape(col_blocks, width, feat_half)[block_cols]
    products = jnp.einsum("tij,tjf->tif", local_tiles, gathered, preferred_element_type=jnp.float32)
    products = products * live_mask[:, None, None]
    partial_value = (
        jnp.zeros((row_blocks, width, feat_half), jnp.float32).at[block_rows].add(products)
    )
    summed = lax.psum_scatter(
        partial_value.reshape(row_blocks * width, feat_half).astype(jnp.bfloat16),
        "col",
        scatter_dimension=0,
        tiled=True,
    )
    weight_rows = lax.dynamic_slice_in_dim(weights, feat_index * feat_half, feat_half, 0)
    mix_term = jnp.dot(summed, weight_rows, preferred_element_type=jnp.float32)
    hidden = lax.psum_scatter(
        mix_term.astype(jnp.bfloat16), "feat", scatter_dimension=1, tiled=True
    ).astype(jnp.float32)
    negative = jnp.minimum(hidden, 0.0)
    activated = jnp.where(hidden > 0, hidden, jnp.expm1(negative)).astype(jnp.bfloat16)
    slope_factor = jnp.where(hidden > 0, 1.0, jnp.exp(negative))
    grad_out = (cotangent.astype(jnp.float32) * slope_factor).astype(jnp.bfloat16)
    grad_whole = lax.all_gather(grad_out, "feat", axis=1, tiled=True)
    weight_term = lax.dot_general(
        summed, grad_whole, (((0,), (0,)), ((), ())), preferred_element_type=jnp.float32
    )
    weight_grad = lax.psum(weight_term, ("row", "col")) * node_total ** (-0.5)
    spread = lax.dot_general(
        grad_whole, weight_rows, (((1,), (1,)), ((), ())), preferred_element_type=jnp.float32
    ).astype(jnp.bfloat16)
    spread_panel = lax.all_gather(spread, "col", axis=0, tiled=True)
    spread_blocks = spread_panel.reshape(row_blocks, width, feat_half)[block_rows]
    back_products = jnp.einsum(
        "tji,tjf->tif", local_tiles, spread_blocks, preferred_element_type=jnp.float32
    )
    back_products = back_products * live_mask[:, None, None]
    back_partial = (
        jnp.zeros((col_blocks, width, feat_half), jnp.float32).at[block_cols].add(back_products)
    )
    back_summed = lax.psum_scatter(
        back_partial.reshape(col_blocks * width, feat_half).astype(jnp.bfloat16),
        "row",
        scatter_dimension=0,
        tiled=True,
    )
    return (activated, back_summed, weight_grad)


def solution(mesh):
    return jax.shard_map(
        shards,
        mesh=mesh,
        in_specs=(
            P(("col", "row"), "feat"),
            P("row", "col", None),
            P("row", "col", None),
            P("row", "col"),
            P("row", "col", None, None, None),
            P(),
            P(("row", "col"), "feat"),
        ),
        out_specs=(P(("row", "col"), "feat"), P(("col", "row"), "feat"), P("feat", None)),
        check_vma=False,
    )
```

profile of v0, /device:TPU:1, one launch (start us, length us, event | category | flops | bytes accessed | tf_op | source)
XLA Modules:
  0.0 1464.9 jit_solution(11761849151452895008)
XLA Ops:
  10.0 43.8 %all-gather.3.cloned.1.call-done = bf16[8192,128]{1,0:T(8,128)(2,1)} async-done(((bf16[512,128]{1,0:T(8,128)(2,1)}), bf16[8192,128]{1,0:T(8,128)(2,1)}) %all-gather.3.cloned.1.call-update) | async-done | bytes 2097168 | tf_op jit(solution)/shard_map/all_gather | solution.py:22
  53.8 10.2 gather_fusion
  64.0 13.0 multiply_bitcast_fusion.1
  77.0 17.5 %copy.17 = f32[256,128,128]{2,1,0:T(8,128)} copy(f32[256,128,128]{1,2,0:T(8,128)} %multiply_bitcast_fusion.1) | data formatting | bytes 33554432 | tf_op jit(solution)/shard_map/mul | solution.py:25
  94.7 33.2 %scatter_fusion = f32[32,128,128]{2,1,0:T(8,128)S(1)} fusion(f32[32,128,128]{2,1,0:T(8,128)S(1)} %broadcast_in_dim.8, s32[256]{0:T(256)S(1)} %bitcast.37, f32[256,128,128]{2,1,0:T(8,128)} %copy.17), kind=kCustom, calls=%fused_computation.2 | custom fusion | flops 4194304 | bytes 50332672 | tf_op jit(solution)/shard_map/scatter-add | solution.py:27
  127.9 1.1 convert_element_type.38
  129.1 72.8 %reduce-scatter.6.cloned.1.call-done = bf16[512,128]{1,0:T(8,128)(2,1)} async-done(((bf16[4096,128]{1,0:T(8,128)(2,1)}), bf16[512,128]{1,0:T(8,128)(2,1)}) %reduce-scatter.6.cloned.1.call-update) | async-done | bytes 131088 | tf_op jit(solution)/shard_map/reduce_scatter | solution.py:29
  201.9 1.1 convolution_convert_fusion
  203.0 0.8 copy.22
  204.0 18.4 %reduce-scatter.10.cloned.1.call-done = bf16[128,512]{1,0:T(8,128)(2,1)} async-done(((bf16[256,512]{1,0:T(8,128)(2,1)}), bf16[128,512]{1,0:T(8,128)(2,1)}) %reduce-scatter.10.cloned.1.call-update) | async-done | bytes 131088
  222.3 1.0 copy.23
  224.2 5.1 all_gather.10
  229.3 0.9 convolution_convert_fusion.1
  230.3 1.8 fusion.12
  232.3 49.8 %all-gather.5.cloned.1.call-done = bf16[4096,128]{1,0:T(8,128)(2,1)} async-done(((bf16[512,128]{1,0:T(8,128)(2,1)}), bf16[4096,128]{1,0:T(8,128)(2,1)}) %all-gather.5.cloned.1.call-update) | async-done | bytes 1048592 | tf_op jit(solution)/shard_map/all_gather | solution.py:52
  282.1 9.8 gather_fusion.1
  292.0 15.4 %multiply_bitcast_fusion = f32[256,128,128]{1,2,0:T(8,128)} fusion(bf16[256,128,128]{2,1,0:T(8,128)(2,1)} %gather_fusion.1, bf16[1,1,256,128,128]{4,3,2,1,0:T(8,128)(2,1)} %param.11, f32[256]{0:T(256)S(1)} %compare_convert_fusion), kind=kOutput, calls=%fused_computation.4 | convolution fusion | flops 1077936128 | bytes 33555456 | tf_op jit(solution)/shard_map/tji,tjf->tif/dot_general | solution.py:54
  307.4 17.5 %copy.19 = f32[256,128,128]{2,1,0:T(8,128)} copy(f32[256,128,128]{1,2,0:T(8,128)} %multiply_bitcast_fusion) | data formatting | bytes 33554432 | tf_op jit(solution)/shard_map/mul | solution.py:57
  324.8 2.4 broadcast_in_dim.9
  327.3 51.9 %scatter_fusion.1 = f32[64,128,128]{2,1,0:T(8,128)} fusion(f32[64,128,128]{2,1,0:T(8,128)} %broadcast_in_dim.9, s32[256]{0:T(256)S(1)} %bitcast.36, f32[256,128,128]{2,1,0:T(8,128)} %copy.19), kind=kCustom, calls=%fused_computation.3 | custom fusion | flops 4194304 | bytes 50332672 | tf_op jit(solution)/shard_map/scatter-add | solution.py:59
  379.1 3.9 convert_element_type.46
  383.1 1013.4 %all-reduce.2.cloned.1.call-done = f32[128,256]{1,0:T(8,128)} async-done(((f32[128,256]{1,0:T(8,128)}), f32[128,256]{1,0:T(8,128)}) %all-reduce.2.cloned.1.call-update) | async-done | bytes 131088 | tf_op jit(solution)/shard_map/psum | solution.py:48
  1396.5 1.6 broadcast_multiply_fusion
  1398.1 60.0 %reduce-scatter.8.cloned.1.call-done = bf16[512,128]{1,0:T(8,128)(2,1)} async-done(((bf16[8192,128]{1,0:T(8,128)(2,1)}), bf16[512,128]{1,0:T(8,128)(2,1)}) %reduce-scatter.8.cloned.1.call-update) | async-done | bytes 131088 | tf_op jit(solution)/shard_map/reduce_scatter | solution.py:61
  (25 shorter events, 3.6 us)
Async XLA Ops:
  7.2 194.8 %copy-start = (bf16[256,256]{1,0:T(8,128)(2,1)S(1)}, bf16[256,256]{1,0:T(8,128)(2,1)}, u32[]{:S(2)}) copy-start(bf16[256,256]{1,0:T(8,128)(2,1)} %param.12) | copy-start | bytes 393220
  7.2 46.6 %all-gather.3.cloned.1.call-start = ((), (), s32[]{:S(2)}) async-start(), calls=%async_computation.3 | async-start | bytes 2228224 | tf_op jit(solution)/shard_map/all_gather | solution.py:22
  7.9 194.0 %reduce-scatter.6.cloned.1.call-start = ((), (), s32[]{:S(2)}) async-start(), calls=%async_computation.4 | async-start | bytes 1179648 | tf_op jit(solution)/shard_map/reduce_scatter | solution.py:29
  94.7 128.7 %copy-start.2 = (bf16[512,128]{1,0:T(8,128)(2,1)S(1)}, bf16[512,128]{1,0:T(8,128)(2,1)}, u32[]{:S(2)}) copy-start(bf16[512,128]{1,0:T(8,128)(2,1)} %param.13) | copy-start | bytes 393220
  129.1 93.3 %reduce-scatter.10.cloned.1.call-start = ((), (), s32[]{:S(2)}) async-start(), calls=%async_computation.8 | async-start | bytes 393216
  203.9 78.2 %all-gather.5.cloned.1.call-start = ((), (), s32[]{:S(2)}) async-start(), calls=%async_computation.5 | async-start | bytes 1179648 | tf_op jit(solution)/shard_map/all_gather | solution.py:52
  230.2 1166.3 %all-reduce.2.cloned.1.call-start = ((), (), s32[]{:S(2)}) async-start(), calls=%async_computation.7 | async-start | bytes 262144 | tf_op jit(solution)/shard_map/psum | solution.py:48
  232.1 1226.0 %reduce-scatter.8.cloned.1.call-start = ((), (), s32[]{:S(2)}) async-start(), calls=%async_computation.6 | async-start | bytes 2228224 | tf_op jit(solution)/shard_map/reduce_scatter | solution.py:61
  327.3 1130.8 %copy-start.1 = (bf16[256,256]{1,0:T(8,128)(2,1)S(1)}, bf16[256,256]{1,0:T(8,128)(2,1)}, u32[]{:S(2)}) copy-start(bf16[256,256]{1,0:T(8,128)(2,1)} %param.12) | copy-start | bytes 393220
Sparse Core Ops, SparseCore 0:
  9.8 43.9 all-gather.2
  129.2 72.6 reduce-scatter.5
  204.6 17.7 reduce-scatter.9
  230.3 51.7 all-gather.4
  285.2 1111.2 all-reduce.1
  1399.6 58.4 reduce-scatter.7
where the time goes:
time: 1470 us; the launch traced here: 1460 us
  waiting for transfers between devices  1260 us (86%)
  other arithmetic  93.8 us (6%)
  local copies, waits for them, and re-layouts  59.5 us (4%)
  matrix products  32.2 us (2%)
  between operations  14.8 us (1%)
    psum x1, waiting for transfers between devices, shards(): weight_grad = lax.psum(weight_term, ('row', 'col')) * node_total ** (-0.5)  1010 us
    reduce_scatter x1, waiting for transfers between devices, shards(): lax.psum_scatter(partial_value.reshape(row_blocks * width, feat_half).ast...  72.8 us
    reduce_scatter x1, waiting for transfers between devices, shards(): lax.psum_scatter(back_partial.reshape(col_blocks * width, feat_half).asty...  60 us
    scatter-add x1, other arithmetic, shards(): jnp.zeros((col_blocks, width, feat_half), jnp.float32).at[block_cols]  51.9 us
    all_gather x1, waiting for transfers between devices, shards(): spread_panel = lax.all_gather(spread, 'col', axis=0, tiled=True)  49.8 us
    all_gather x1, waiting for transfers between devices, shards(): panel = lax.all_gather(features, 'row', axis=0, tiled=True)  43.8 us
    scatter-add x1, other arithmetic, shards(): jnp.zeros((row_blocks, width, feat_half), jnp.float32).at[block_rows]  33.2 us
  transfers between devices with their start and end apart: 6, of which 6 were waited for; matrix products, arithmetic and copies ran while one was open for 7% of the time, Pallas kernels for 0%

commit v1 on v0

--- a/solution.py
+++ b/solution.py
@@ -45,7 +45,11 @@
     weight_term = lax.dot_general(
         summed, grad_whole, (((0,), (0,)), ((), ())), preferred_element_type=jnp.float32
     )
-    weight_grad = lax.psum(weight_term, ("row", "col")) * node_total ** (-0.5)
+    n_feat = lax.axis_size("feat")
+    slots = jnp.zeros((n_feat,) + weight_term.shape, jnp.float32)
+    slots = lax.dynamic_update_slice_in_dim(slots, weight_term[None], feat_index, 0)
+    slots = lax.psum(slots, ("row", "col", "feat"))
+    weight_grad = lax.dynamic_index_in_dim(slots, feat_index, 0, keepdims=False) * node_total ** (-0.5)
     spread = lax.dot_general(
         grad_whole, weight_rows, (((1,), (1,)), ((), ())), preferred_element_type=jnp.float32
     ).astype(jnp.bfloat16)

time: 1470 us -> 607 us (0.41)
  waiting for transfers between devices: 1260 us -> 397 us
    psum x1, waiting for transfers between devices: 1010 us -> 153 us  [shards(): slots = lax.psum(slots, ('row', 'col', 'feat'))]
  transfers between devices with their start and end apart: 6 -> 6, of which waited for: 6 -> 6; matrix products, arithmetic and copies ran while one was open for 7% -> 17% of each run, Pallas kernels for 0% -> 0%
where the time goes in v1:
time: 607 us; the launch traced here: 603 us
  waiting for transfers between devices  397 us (65%)
  other arithmetic  93.4 us (15%)
  local copies, waits for them, and re-layouts  60.2 us (10%)
  matrix products  31.5 us (5%)
  between operations  14.9 us (2%)
    psum x1, waiting for transfers between devices, shards(): slots = lax.psum(slots, ('row', 'col', 'feat'))  153 us
    reduce_scatter x1, waiting for transfers between devices, shards(): lax.psum_scatter(partial_value.reshape(row_blocks * width, feat_half).ast...  72.8 us
    reduce_scatter x1, waiting for transfers between devices, shards(): lax.psum_scatter(back_partial.reshape(col_blocks * width, feat_half).asty...  57.9 us
    scatter-add x1, other arithmetic, shards(): jnp.zeros((col_blocks, width, feat_half), jnp.float32).at[block_cols]  52.1 us
    all_gather x1, waiting for transfers between devices, shards(): spread_panel = lax.all_gather(spread, 'col', axis=0, tiled=True)  49.7 us
    all_gather x1, waiting for transfers between devices, shards(): panel = lax.all_gather(features, 'row', axis=0, tiled=True)  44.5 us
    scatter-add x1, other arithmetic, shards(): jnp.zeros((row_blocks, width, feat_half), jnp.float32).at[block_rows]  33.2 us
    unnamed x7, waiting for transfers between devices  19.1 us
  transfers between devices with their start and end apart: 6, of which 6 were waited for; matrix products, arithmetic and copies ran while one was open for 17% of the time, Pallas kernels for 0%

profile of v1, /device:TPU:1, one launch (start us, length us, event | category | flops | bytes accessed | tf_op | source)
XLA Modules:
  0.0 603.0 jit_solution(15216501221385841070)
XLA Ops:
  9.3 44.5 %all-gather.3.cloned.1.call-done = bf16[8192,128]{1,0:T(8,128)(2,1)} async-done(((bf16[512,128]{1,0:T(8,128)(2,1)}), bf16[8192,128]{1,0:T(8,128)(2,1)}) %all-gather.3.cloned.1.call-update) | async-done | bytes 2097168 | tf_op jit(solution)/shard_map/all_gather | solution.py:22
  53.8 10.2 %gather_fusion = bf16[256,128,128]{2,1,0:T(8,128)(2,1)} fusion(bf16[64,128,128]{2,1,0:T(8,128)(2,1)} %bitcast.36, s32[1024]{0:T(1024)S(1)} %pad_clamp_fusion.1), kind=kCustom, calls=%fused_computation | custom fusion | bytes 16778240 | tf_op jit(solution)/shard_map/gather | solution.py:23
  64.0 13.0 %multiply_bitcast_fusion.1 = f32[256,128,128]{1,2,0:T(8,128)} fusion(bf16[256,128,128]{2,1,0:T(8,128)(2,1)} %gather_fusion, bf16[1,1,256,128,128]{4,3,2,1,0:T(8,128)(2,1)} %param.11, f32[256]{0:T(256)S(1)} %compare_convert_fusion), kind=kOutput, calls=%fused_computation.5 | convolution fusion | flops 1077936128 | bytes 33555456 | tf_op jit(solution)/shard_map/tij,tjf->tif/dot_general | solution.py:24
  77.0 17.4 %copy.17 = f32[256,128,128]{2,1,0:T(8,128)} copy(f32[256,128,128]{1,2,0:T(8,128)} %multiply_bitcast_fusion.1) | data formatting | bytes 33554432 | tf_op jit(solution)/shard_map/mul | solution.py:25
  94.7 33.2 %scatter_fusion = f32[32,128,128]{2,1,0:T(8,128)S(1)} fusion(f32[32,128,128]{2,1,0:T(8,128)S(1)} %broadcast_in_dim.22, s32[256]{0:T(256)S(1)} %bitcast.43, f32[256,128,128]{2,1,0:T(8,128)} %copy.17), kind=kCustom, calls=%fused_computation.2 | custom fusion | flops 4194304 | bytes 50332672 | tf_op jit(solution)/shard_map/scatter-add | solution.py:27
  127.9 1.1 convert_element_type.38
  129.2 72.8 %reduce-scatter.6.cloned.1.call-done = bf16[512,128]{1,0:T(8,128)(2,1)} async-done(((bf16[4096,128]{1,0:T(8,128)(2,1)}), bf16[512,128]{1,0:T(8,128)(2,1)}) %reduce-scatter.6.cloned.1.call-update) | async-done | bytes 131088 | tf_op jit(solution)/shard_map/reduce_scatter | solution.py:29
  202.0 1.1 convolution_convert_fusion
  203.1 0.8 copy.22
  204.0 18.4 %reduce-scatter.10.cloned.1.call-done = bf16[128,512]{1,0:T(8,128)(2,1)} async-done(((bf16[256,512]{1,0:T(8,128)(2,1)}), bf16[128,512]{1,0:T(8,128)(2,1)}) %reduce-scatter.10.cloned.1.call-update) | async-done | bytes 131088
  222.4 1.0 copy.23
  224.2 5.1 all_gather.10
  229.3 0.9 convolution_convert_fusion.1
  230.3 1.1 fusion.2
  232.4 49.7 %all-gather.5.cloned.1.call-done = bf16[4096,128]{1,0:T(8,128)(2,1)} async-done(((bf16[512,128]{1,0:T(8,128)(2,1)}), bf16[4096,128]{1,0:T(8,128)(2,1)}) %all-gather.5.cloned.1.call-update) | async-done | bytes 1048592 | tf_op jit(solution)/shard_map/all_gather | solution.py:56
  282.2 9.8 %gather_fusion.1 = bf16[256,128,128]{2,1,0:T(8,128)(2,1)} fusion(bf16[32,128,128]{2,1,0:T(8,128)(2,1)} %bitcast.35, s32[1024]{0:T(1024)S(1)} %pad_clamp_fusion), kind=kCustom, calls=%fused_computation.1 | custom fusion | bytes 16778240 | tf_op jit(solution)/shard_map/gather | solution.py:57
  292.0 15.4 %multiply_bitcast_fusion = f32[256,128,128]{1,2,0:T(8,128)} fusion(bf16[256,128,128]{2,1,0:T(8,128)(2,1)} %gather_fusion.1, bf16[1,1,256,128,128]{4,3,2,1,0:T(8,128)(2,1)} %param.11, f32[256]{0:T(256)S(1)} %compare_convert_fusion), kind=kOutput, calls=%fused_computation.4 | convolution fusion | flops 1077936128 | bytes 33555456 | tf_op jit(solution)/shard_map/tji,tjf->tif/dot_general | solution.py:58
  307.4 17.5 %copy.19 = f32[256,128,128]{2,1,0:T(8,128)} copy(f32[256,128,128]{1,2,0:T(8,128)} %multiply_bitcast_fusion) | data formatting | bytes 33554432 | tf_op jit(solution)/shard_map/mul | solution.py:61
  324.9 2.5 broadcast_in_dim.23
  327.4 52.1 %scatter_fusion.1 = f32[64,128,128]{2,1,0:T(8,128)} fusion(f32[64,128,128]{2,1,0:T(8,128)} %broadcast_in_dim.23, s32[256]{0:T(256)S(1)} %bitcast.42, f32[256,128,128]{2,1,0:T(8,128)} %copy.19), kind=kCustom, calls=%fused_computation.3 | custom fusion | flops 4194304 | bytes 50332672 | tf_op jit(solution)/shard_map/scatter-add | solution.py:63
  379.4 3.9 convert_element_type.46
  383.4 153.3 %all-reduce.2.cloned.1.call-done = f32[2,128,256]{2,1,0:T(8,128)} async-done(((f32[2,128,256]{2,1,0:T(8,128)}), f32[2,128,256]{2,1,0:T(8,128)}) %all-reduce.2.cloned.1.call-update) | async-done | bytes 262160 | tf_op jit(solution)/shard_map/psum | solution.py:51
  536.7 1.6 multiply_bitcast_fusion.2
  538.3 57.9 %reduce-scatter.8.cloned.1.call-done = bf16[512,128]{1,0:T(8,128)(2,1)} async-done(((bf16[8192,128]{1,0:T(8,128)(2,1)}), bf16[512,128]{1,0:T(8,128)(2,1)}) %reduce-scatter.8.cloned.1.call-update) | async-done | bytes 131088 | tf_op jit(solution)/shard_map/reduce_scatter | solution.py:65
  (27 shorter events, 3.7 us)
Async XLA Ops:
  7.2 194.8 %copy-start = (bf16[256,256]{1,0:T(8,128)(2,1)S(1)}, bf16[256,256]{1,0:T(8,128)(2,1)}, u32[]{:S(2)}) copy-start(bf16[256,256]{1,0:T(8,128)(2,1)} %param.12) | copy-start | bytes 393220
  7.2 46.6 %all-gather.3.cloned.1.call-start = ((), (), s32[]{:S(2)}) async-start(), calls=%async_computation.3 | async-start | bytes 2228224 | tf_op jit(solution)/shard_map/all_gather | solution.py:22
  7.9 194.1 %reduce-scatter.6.cloned.1.call-start = ((), (), s32[]{:S(2)}) async-start(), calls=%async_computation.4 | async-start | bytes 1179648 | tf_op jit(solution)/shard_map/reduce_scatter | solution.py:29
  94.7 128.7 %copy-start.3 = (bf16[512,128]{1,0:T(8,128)(2,1)S(1)}, bf16[512,128]{1,0:T(8,128)(2,1)}, u32[]{:S(2)}) copy-start(bf16[512,128]{1,0:T(8,128)(2,1)} %param.13) | copy-start | bytes 393220
  129.1 93.3 %reduce-scatter.10.cloned.1.call-start = ((), (), s32[]{:S(2)}) async-start(), calls=%async_computation.8 | async-start | bytes 393216
  204.0 78.2 %all-gather.5.cloned.1.call-start = ((), (), s32[]{:S(2)}) async-start(), calls=%async_computation.5 | async-start | bytes 1179648 | tf_op jit(solution)/shard_map/all_gather | solution.py:56
  230.3 306.5 %all-reduce.2.cloned.1.call-start = ((), (), s32[]{:S(2)}) async-start(), calls=%async_computation.7 | async-start | bytes 524288 | tf_op jit(solution)/shard_map/psum | solution.py:51
  231.5 0.7 copy-start.2
  232.2 363.9 %reduce-scatter.8.cloned.1.call-start = ((), (), s32[]{:S(2)}) async-start(), calls=%async_computation.6 | async-start | bytes 2228224 | tf_op jit(solution)/shard_map/reduce_scatter | solution.py:65
  327.4 268.8 %copy-start.1 = (bf16[256,256]{1,0:T(8,128)(2,1)S(1)}, bf16[256,256]{1,0:T(8,128)(2,1)}, u32[]{:S(2)}) copy-start(bf16[256,256]{1,0:T(8,128)(2,1)} %param.12) | copy-start | bytes 393220
Sparse Core Ops, SparseCore 0:
  9.8 43.9 all-gather.2
  129.2 72.7 reduce-scatter.5
  204.6 17.7 reduce-scatter.9
  230.4 51.7 all-gather.4
  287.5 249.1 all-reduce.1
  539.7 56.4 reduce-scatter.7

commit v2 on v1

--- a/solution.py
+++ b/solution.py
@@ -1,16 +1,83 @@
+import functools
+
 import jax
 import jax.numpy as jnp
 from jax import lax
+from jax.experimental import pallas as pl
+from jax.experimental.pallas import tpu as pltpu
 from jax.sharding import PartitionSpec as P
+
+GROUP = 8
+
+
+def tile_kernel(transpose, rows_ref, cols_ref, count_ref, tiles_ref, panel_ref, out_ref, acc_ref):
+    step = pl.program_id(0)
+    width = tiles_ref.shape[-1]
+    count = count_ref[0]
+
+    @pl.when(step == 0)
+    def _():
+        acc_ref[...] = jnp.zeros_like(acc_ref)
+
+    for j in range(GROUP):
+        slot = step * GROUP + j
+
+        @pl.when(slot < count)
+        def _():
+            src = rows_ref[slot] if transpose else cols_ref[slot]
+            dst = cols_ref[slot] if transpose else rows_ref[slot]
+            block = panel_ref[pl.ds(pl.multiple_of(src * width, width), width), :]
+            tile = tiles_ref[j]
+            if transpose:
+                term = lax.dot_general(tile, block, (((0,), (0,)), ((), ())),
+                                       preferred_element_type=jnp.float32)
+            else:
+                term = jnp.dot(tile, block, preferred_element_type=jnp.float32)
+            rows = pl.ds(pl.multiple_of(dst * width, width), width)
+            acc_ref[rows, :] += term
+
+    @pl.when(step == pl.num_programs(0) - 1)
+    def _():
+        out_ref[...] = acc_ref[...].astype(out_ref.dtype)
+
+
+def tile_products(tiles, rows, cols, count, panel, out_blocks, transpose):
+    slots, width, _ = tiles.shape
+    feat = panel.shape[1]
+    steps = slots // GROUP
+
+    def tiles_map(i, rows_ref, cols_ref, count_ref):
+        last = jnp.maximum(count_ref[0] - 1, 0) // GROUP
+        return (jnp.minimum(i, last), 0, 0)
+
+    return pl.pallas_call(
+        functools.partial(tile_kernel, transpose),
+        out_shape=jax.ShapeDtypeStruct((out_blocks * width, feat), jnp.bfloat16),
+        grid_spec=pltpu.PrefetchScalarGridSpec(
+            num_scalar_prefetch=3,
+            grid=(steps,),
+            in_specs=[
+                pl.BlockSpec((GROUP, width, width), tiles_map),
+                pl.BlockSpec(panel.shape, lambda i, *_: (0, 0)),
+            ],
+            out_specs=pl.BlockSpec((out_blocks * width, feat), lambda i, *_: (0, 0)),
+            scratch_shapes=[pltpu.VMEM((out_blocks * width, feat), jnp.float32)],
+        ),
+        compiler_params=pltpu.CompilerParams(dimension_semantics=("arbitrary",)),
+        cost_estimate=pl.CostEstimate(
+            flops=2 * slots * width * width * feat,
+            bytes_accessed=tiles.size * 2 + panel.size * 2 + out_blocks * width * feat * 2,
+            transcendentals=0,
+        ),
+    )(rows, cols, count, tiles, panel)
 
 
 def shards(features, tile_rows, tile_cols, tile_count, tile_values, weights, cotangent):
     width = tile_values.shape[-1]
-    slots = tile_values.shape[2]
     local_tiles = tile_values[0, 0]
     block_rows = tile_rows[0, 0]
     block_cols = tile_cols[0, 0]
-    live_mask = (jnp.arange(slots) < tile_count[0, 0]).astype(jnp.float32)
+    count = tile_count[0, 0].reshape(1)
     n_rowdev = lax.axis_size("row")
     n_coldev = lax.axis_size("col")
     local_blocks = features.shape[0] // width
@@ -20,18 +87,9 @@
     col_blocks = local_blocks * n_rowdev
     node_total = features.shape[0] * n_rowdev * n_coldev
     panel = lax.all_gather(features, "row", axis=0, tiled=True)
-    gathered = panel.reshape(col_blocks, width, feat_half)[block_cols]
-    products = jnp.einsum("tij,tjf->tif", local_tiles, gathered, preferred_element_type=jnp.float32)
-    products = products * live_mask[:, None, None]
-    partial_value = (
-        jnp.zeros((row_blocks, width, feat_half), jnp.float32).at[block_rows].add(products)
-    )
-    summed = lax.psum_scatter(
-        partial_value.reshape(row_blocks * width, feat_half).astype(jnp.bfloat16),
-        "col",
-        scatter_dimension=0,
-        tiled=True,
-    )
+    partial_value = tile_products(local_tiles, block_rows, block_cols, count, panel,
+                                  row_blocks, transpose=False)
+    summed = lax.psum_scatter(partial_value, "col", scatter_dimension=0, tiled=True)
     weight_rows = lax.dynamic_slice_in_dim(weights, feat_index * feat_half, feat_half, 0)
     mix_term = jnp.dot(summed, weight_rows, preferred_element_type=jnp.float32)
     hidden = lax.psum_scatter(
@@ -54,20 +112,9 @@
         grad_whole, weight_rows, (((1,), (1,)), ((), ())), preferred_element_type=jnp.float32
     ).astype(jnp.bfloat16)
     spread_panel = lax.all_gather(spread, "col", axis=0, tiled=True)
-    spread_blocks = spread_panel.reshape(row_blocks, width, feat_half)[block_rows]
-    back_products = jnp.einsum(
-        "tji,tjf->tif", local_tiles, spread_blocks, preferred_element_type=jnp.float32
-    )
-    back_products = back_products * live_mask[:, None, None]
-    back_partial = (
-        jnp.zeros((col_blocks, width, feat_half), jnp.float32).at[block_cols].add(back_products)
-    )
-    back_summed = lax.psum_scatter(
-        back_partial.reshape(col_blocks * width, feat_half).astype(jnp.bfloat16),
-        "row",
-        scatter_dimension=0,
-        tiled=True,
-    )
+    back_partial = tile_products(local_tiles, block_rows, block_cols, count, spread_panel,
+                                 col_blocks, transpose=True)
+    back_summed = lax.psum_scatter(back_partial, "row", scatter_dimension=0, tiled=True)
     return (activated, back_summed, weight_grad)
 
 

time: 607 us -> 569 us (0.937)
  other arithmetic: 93.4 us -> 2.37 us
  Pallas kernels: 0 us -> 88.7 us
  local copies, waits for them, and re-layouts: 60.2 us -> 2.62 us
  waiting for transfers between devices: 397 us -> 450 us
  matrix products: 31.5 us -> 2.29 us
    pallas_call x0 -> x2, Pallas kernels: none -> 88.7 us  [tile_products(): pl.pallas_call(functools.partial(tile_kernel, transpose), out_shape=jax.S...]
    scatter-add x2 -> x0, other arithmetic: 85.3 us -> none  [the longest x1 52.1 us: shards(): jnp.zeros((col_blocks, width, feat_half), jnp.float32).at[block_cols]]
    psum x1, waiting for transfers between devices: 153 us -> 205 us  [shards(): slots = lax.psum(slots, ('row', 'col', 'feat'))]
    mul x2 -> x0, local copies, waits for them, and re-layouts: 34.9 us -> none  [the longest x1 17.5 us: shards(): back_products = back_products * live_mask[:, None, None]]
    dot_general x2 -> x0, matrix products: 28.4 us -> none  [the longest x1 15.4 us: shards(): jnp.einsum('tji,tjf->tif', local_tiles, spread_blocks, preferred_element_...]
    gather x2 -> x0, local copies, waits for them, and re-layouts: 20 us -> none  [the longest x1 10.2 us: shards(): gathered = panel.reshape(col_blocks, width, feat_half)[block_cols]]
  transfers between devices with their start and end apart: 6 -> 6, of which waited for: 6 -> 6; matrix products, arithmetic and copies ran while one was open for 17% -> 0% of each run, Pallas kernels for 0% -> 9%
where the time goes in v2:
time: 569 us; the launch traced here: 566 us
  waiting for transfers between devices  450 us (79%)
  Pallas kernels  88.7 us (16%)
  between operations  14.8 us (3%)
    psum x1, waiting for transfers between devices, shards(): slots = lax.psum(slots, ('row', 'col', 'feat'))  205 us
    pallas_call x2, Pallas kernels, tile_products(): pl.pallas_call(functools.partial(tile_kernel, transpose), out_shape=jax.S...  88.7 us
    reduce_scatter x1, waiting for transfers between devices, shards(): lax.psum_scatter(partial_value, 'col', scatter_dimension=0, tiled=True)  72.3 us
    reduce_scatter x1, waiting for transfers between devices, shards(): lax.psum_scatter(back_partial, 'row', scatter_dimension=0, tiled=True)  57.9 us
    all_gather x1, waiting for transfers between devices, shards(): spread_panel = lax.all_gather(spread, 'col', axis=0, tiled=True)  50.9 us
    all_gather x1, waiting for transfers between devices, shards(): panel = lax.all_gather(features, 'row', axis=0, tiled=True)  45.2 us
    unnamed x7, waiting for transfers between devices  19.1 us
  transfers between devices with their start and end apart: 6, of which 6 were waited for; matrix products, arithmetic and copies ran while one was open for 0% of the time, Pallas kernels for 9%

profile of v2, /device:TPU:1, one launch (start us, length us, event | category | flops | bytes accessed | tf_op | source)
XLA Modules:
  0.0 566.3 jit_solution(2564248210198306731)
XLA Ops:
  7.2 0.0 all-gather.3.cloned.1.call-start
  7.2 0.7 all-gather.3.cloned.1.call-update
  7.9 0.0 reduce-scatter.6.cloned.1.call-start
  8.6 45.2 %all-gather.3.cloned.1.call-done.panel_ref = bf16[8192,128]{1,0:T(8,128)(2,1)} async-done(((bf16[512,128]{1,0:T(8,128)(2,1)}), bf16[8192,128]{1,0:T(8,128)(2,1)}) %all-gather.3.cloned.1.call-update) | async-done | bytes 2097168 | tf_op jit(solution)/shard_map/all_gather | solution.py:89
  53.8 38.3 %shard_map.94 = bf16[4096,128]{1,0:T(8,128)(2,1)} custom-call(s32[256]{0:T(256)} %bitcast.22, s32[256]{0:T(256)} %bitcast.24, s32[1]{0:T(128)} %bitcast.16.count_ref, bf16[256,128,128]{2,1,0:T(8,128)(2,1)} %bitcast.18, bf16[8192,128]{1,0:T(8,128)(2,1)} %all-gather.3.cloned.1.call-done.panel_ref), custom_call_target="tpu_custom_call" | custom-call | flops 1073741824 | bytes 11534336 | tf_op jit(solution)/shard_map/pallas_call | solution.py:53
  92.1 0.0 reduce-scatter.10.cloned.1.call-start
  92.2 72.3 %reduce-scatter.6.cloned.1.call-done = bf16[512,128]{1,0:T(8,128)(2,1)} async-done(((bf16[4096,128]{1,0:T(8,128)(2,1)}), bf16[512,128]{1,0:T(8,128)(2,1)}) %reduce-scatter.6.cloned.1.call-update) | async-done | bytes 131088 | tf_op jit(solution)/shard_map/reduce_scatter | solution.py:92
  164.5 1.2 convolution_convert_fusion
  165.7 0.8 copy.10
  166.5 0.0 all-gather.5.cloned.1.call-start
  166.6 18.3 %reduce-scatter.10.cloned.1.call-done = bf16[128,512]{1,0:T(8,128)(2,1)} async-done(((bf16[256,512]{1,0:T(8,128)(2,1)}), bf16[128,512]{1,0:T(8,128)(2,1)}) %reduce-scatter.10.cloned.1.call-update) | async-done | bytes 131088
  184.9 1.0 copy.11
  185.9 0.8 fusion.5
  186.7 5.1 all_gather.10
  191.8 0.9 convolution_convert_fusion.1
  192.7 0.0 all-reduce.2.cloned.1.call-start
  192.8 0.2 fusion
  193.1 0.7 copy-done.1
  193.8 0.0 reduce-scatter.8.cloned.1.call-start
  193.8 50.9 %all-gather.5.cloned.1.call-done.panel_ref = bf16[4096,128]{1,0:T(8,128)(2,1)} async-done(((bf16[512,128]{1,0:T(8,128)(2,1)}), bf16[4096,128]{1,0:T(8,128)(2,1)}) %all-gather.5.cloned.1.call-update) | async-done | bytes 1048592 | tf_op jit(solution)/shard_map/all_gather | solution.py:114
  244.7 50.4 %shard_map.95 = bf16[8192,128]{1,0:T(8,128)(2,1)} custom-call(s32[256]{0:T(256)} %bitcast.23, s32[256]{0:T(256)} %bitcast.25, s32[1]{0:T(128)} %bitcast.17.count_ref, bf16[256,128,128]{2,1,0:T(8,128)(2,1)} %bitcast.19, bf16[4096,128]{1,0:T(8,128)(2,1)} %all-gather.5.cloned.1.call-done.panel_ref), custom_call_target="tpu_custom_call" | custom-call | flops 1073741824 | bytes 11534336 | tf_op jit(solution)/shard_map/pallas_call | solution.py:53
  295.1 204.9 %all-reduce.2.cloned.1.call-done = f32[2,128,256]{2,1,0:T(8,128)} async-done(((f32[2,128,256]{2,1,0:T(8,128)}), f32[2,128,256]{2,1,0:T(8,128)}) %all-reduce.2.cloned.1.call-update) | async-done | bytes 262160 | tf_op jit(solution)/shard_map/psum | solution.py:109
  500.0 1.6 multiply_bitcast_fusion
  501.6 57.9 %reduce-scatter.8.cloned.1.call-done = bf16[512,128]{1,0:T(8,128)(2,1)} async-done(((bf16[8192,128]{1,0:T(8,128)(2,1)}), bf16[512,128]{1,0:T(8,128)(2,1)}) %reduce-scatter.8.cloned.1.call-update) | async-done | bytes 131088 | tf_op jit(solution)/shard_map/reduce_scatter | solution.py:117
  (13 shorter events, 0.1 us)
Async XLA Ops:
  7.2 157.3 %copy-start = (bf16[256,256]{1,0:T(8,128)(2,1)S(1)}, bf16[256,256]{1,0:T(8,128)(2,1)}, u32[]{:S(2)}) copy-start(bf16[256,256]{1,0:T(8,128)(2,1)} %param.12) | copy-start | bytes 393220
  7.2 46.6 %all-gather.3.cloned.1.call-start = ((), (), s32[]{:S(2)}) async-start(), calls=%async_computation.3 | async-start | bytes 2228224 | tf_op jit(solution)/shard_map/all_gather | solution.py:89
  7.9 156.6 %reduce-scatter.6.cloned.1.call-start = ((), (), s32[]{:S(2)}) async-start(), calls=%async_computation.4 | async-start | bytes 1179648 | tf_op jit(solution)/shard_map/reduce_scatter | solution.py:92
  92.1 93.8 %copy-start.3 = (bf16[512,128]{1,0:T(8,128)(2,1)S(1)}, bf16[512,128]{1,0:T(8,128)(2,1)}, u32[]{:S(2)}) copy-start(bf16[512,128]{1,0:T(8,128)(2,1)} %param.13) | copy-start | bytes 393220
  92.1 92.8 %reduce-scatter.10.cloned.1.call-start = ((), (), s32[]{:S(2)}) async-start(), calls=%async_computation.8 | async-start | bytes 393216
  164.5 28.3 %copy-start.2 = (bf16[512,128]{1,0:T(8,128)(2,1)S(1)}, bf16[512,128]{1,0:T(8,128)(2,1)}, u32[]{:S(2)}) copy-start(bf16[512,128]{1,0:T(8,128)(2,1)} %reduce-scatter.6.cloned.1.call-done) | copy-start | bytes 393220
  166.5 78.2 %all-gather.5.cloned.1.call-start = ((), (), s32[]{:S(2)}) async-start(), calls=%async_computation.5 | async-start | bytes 1179648 | tf_op jit(solution)/shard_map/all_gather | solution.py:114
  192.7 307.3 %all-reduce.2.cloned.1.call-start = ((), (), s32[]{:S(2)}) async-start(), calls=%async_computation.7 | async-start | bytes 524288 | tf_op jit(solution)/shard_map/psum | solution.py:109
  193.1 0.7 copy-start.1
  193.8 365.6 %reduce-scatter.8.cloned.1.call-start = ((), (), s32[]{:S(2)}) async-start(), calls=%async_computation.6 | async-start | bytes 2228224 | tf_op jit(solution)/shard_map/reduce_scatter | solution.py:117
Sparse Core Ops, SparseCore 0:
  9.8 43.9 all-gather.2
  92.2 72.1 reduce-scatter.5
  167.1 17.7 reduce-scatter.9
  192.9 51.8 all-gather.4
  250.0 249.9 all-reduce.1
  503.0 56.4 reduce-scatter.7

commit v3 on v2

--- a/solution.py
+++ b/solution.py
@@ -72,6 +72,71 @@
     )(rows, cols, count, tiles, panel)
 
 
+def mesh_coords(axis, peer):
+    return tuple(peer if name == axis else lax.axis_index(name) for name in ("row", "col", "feat"))
+
+
+def exchange_kernel(axis, mode, x_ref, o_ref, *scratch):
+    n = lax.axis_size(axis)
+    me = lax.axis_index(axis)
+    if mode == "gather":
+        recv_ref, (send_sems, recv_sems) = o_ref, scratch
+    else:
+        recv_ref, send_sems, recv_sems = scratch
+    barrier = pltpu.get_barrier_semaphore()
+    for d in range(1, n):
+        peer = lax.rem(me + d, n)
+        pl.semaphore_signal(barrier, inc=1, device_id=mesh_coords(axis, peer),
+                            device_id_type=pl.DeviceIdType.MESH)
+    pl.semaphore_wait(barrier, n - 1)
+    copies = []
+    for d in range(1, n):
+        peer = lax.rem(me + d, n)
+        src = x_ref if mode == "gather" else x_ref.at[peer]
+        copy = pltpu.make_async_remote_copy(
+            src_ref=src, dst_ref=recv_ref.at[me], send_sem=send_sems.at[d],
+            recv_sem=recv_sems.at[me], device_id=mesh_coords(axis, peer),
+            device_id_type=pl.DeviceIdType.MESH)
+        copy.start()
+        copies.append(copy)
+    if mode == "gather":
+        o_ref[me] = x_ref[...]
+    else:
+        total = x_ref[me].astype(jnp.float32)
+    for d in range(1, n):
+        src_dev = lax.rem(me + n - d, n)
+        incoming = pltpu.make_async_remote_copy(
+            src_ref=recv_ref.at[src_dev], dst_ref=recv_ref.at[src_dev], send_sem=send_sems.at[d],
+            recv_sem=recv_sems.at[src_dev], device_id=mesh_coords(axis, src_dev),
+            device_id_type=pl.DeviceIdType.MESH)
+        incoming.wait_recv()
+        if mode != "gather":
+            total = total + recv_ref[src_dev].astype(jnp.float32)
+    for copy in copies:
+        copy.wait_send()
+    if mode != "gather":
+        o_ref[...] = total.astype(o_ref.dtype)
+
+
+def exchange(x, axis, mode, collective_id):
+    n = lax.axis_size(axis)
+    if mode == "gather":
+        out_shape = (n,) + x.shape
+        scratch = []
+    else:
+        out_shape = x.shape[1:]
+        scratch = [pltpu.VMEM(x.shape, x.dtype)]
+    scratch += [pltpu.SemaphoreType.DMA((n,)), pltpu.SemaphoreType.DMA((n,))]
+    return pl.pallas_call(
+        functools.partial(exchange_kernel, axis, mode),
+        out_shape=jax.ShapeDtypeStruct(out_shape, x.dtype),
+        in_specs=[pl.BlockSpec(memory_space=pltpu.VMEM)],
+        out_specs=pl.BlockSpec(memory_space=pltpu.VMEM),
+        scratch_shapes=scratch,
+        compiler_params=pltpu.CompilerParams(collective_id=collective_id, has_side_effects=True),
+    )(x)
+
+
 def shards(features, tile_rows, tile_cols, tile_count, tile_values, weights, cotangent):
     width = tile_values.shape[-1]
     local_tiles = tile_values[0, 0]
@@ -86,10 +151,10 @@
     row_blocks = local_blocks * n_coldev
     col_blocks = local_blocks * n_rowdev
     node_total = features.shape[0] * n_rowdev * n_coldev
-    panel = lax.all_gather(features, "row", axis=0, tiled=True)
+    panel = exchange(features, "row", "gather", 0).reshape(-1, feat_half)
     partial_value = tile_products(local_tiles, block_rows, block_cols, count, panel,
                                   row_blocks, transpose=False)
-    summed = lax.psum_scatter(partial_value, "col", scatter_dimension=0, tiled=True)
+    summed = exchange(partial_value.reshape(n_coldev, -1, feat_half), "col", "scatter", 1)
     weight_rows = lax.dynamic_slice_in_dim(weights, feat_index * feat_half, feat_half, 0)
     mix_term = jnp.dot(summed, weight_rows, preferred_element_type=jnp.float32)
     hidden = lax.psum_scatter(
@@ -111,10 +176,10 @@
     spread = lax.dot_general(
         grad_whole, weight_rows, (((1,), (1,)), ((), ())), preferred_element_type=jnp.float32
     ).astype(jnp.bfloat16)
-    spread_panel = lax.all_gather(spread, "col", axis=0, tiled=True)
+    spread_panel = exchange(spread, "col", "gather", 2).reshape(-1, feat_half)
     back_partial = tile_products(local_tiles, block_rows, block_cols, count, spread_panel,
                                  col_blocks, transpose=True)
-    back_summed = lax.psum_scatter(back_partial, "row", scatter_dimension=0, tiled=True)
+    back_summed = exchange(back_partial.reshape(n_rowdev, -1, feat_half), "row", "scatter", 3)
     return (activated, back_summed, weight_grad)
 
 

time: 569 us -> 428 us (0.75)
  waiting for transfers between devices: 450 us -> 160 us
  Pallas kernels: 88.7 us -> 238 us
    pallas_call x0 -> x4, Pallas kernels: none -> 180 us  [exchange(): pl.pallas_call(functools.partial(exchange_kernel, axis, mode), out_shape=...]
    reduce_scatter x2 -> x0, waiting for transfers between devices: 130 us -> none  [the longest x1 72.3 us: shards(): lax.psum_scatter(partial_value, 'col', scatter_dimension=0, tiled=True)]
    all_gather x2 -> x0, waiting for transfers between devices: 96.1 us -> none  [the longest x1 50.9 us: shards(): spread_panel = lax.all_gather(spread, 'col', axis=0, tiled=True)]
    psum x1, waiting for transfers between devices: 205 us -> 144 us  [shards(): slots = lax.psum(slots, ('row', 'col', 'feat'))]
    pallas_call x2, Pallas kernels: 88.7 us -> 58 us  [tile_products(): pl.pallas_call(functools.partial(tile_kernel, transpose), out_shape=jax.S...]
    unnamed x7 -> x3, waiting for transfers between devices: 19.1 us -> 16.6 us
  transfers between devices with their start and end apart: 6 -> 2, of which waited for: 6 -> 2; matrix products, arithmetic and copies ran while one was open for 0% -> 0% of each run, Pallas kernels for 9% -> 30%
where the time goes in v3:
time: 428 us
  Pallas kernels  238 us (56%)
  waiting for transfers between devices  160 us (37%)
  between operations  14.8 us (3%)
  blocking collectives  5.06 us (1%)
    pallas_call x4, Pallas kernels, exchange(): pl.pallas_call(functools.partial(exchange_kernel, axis, mode), out_shape=...  180 us
    psum x1, waiting for transfers between devices, shards(): slots = lax.psum(slots, ('row', 'col', 'feat'))  144 us
    pallas_call x2, Pallas kernels, tile_products(): pl.pallas_call(functools.partial(tile_kernel, transpose), out_shape=jax.S...  58 us
    unnamed x3, waiting for transfers between devices  16.6 us
  transfers between devices with their start and end apart: 2, of which 2 were waited for; matrix products, arithmetic and copies ran while one was open for 0% of the time, Pallas kernels for 30%

profile of v3, /device:TPU:1, one launch (start us, length us, event | category | flops | bytes accessed | tf_op | source)
XLA Modules:
  0.0 427.5 jit_solution(7920834390647208498)
XLA Ops:
  7.2 0.0 copy-start
  7.2 0.0 reduce-scatter.4.cloned.1.call-start
  7.9 57.7 %shard_map.94 = bf16[16,512,128]{2,1,0:T(8,128)(2,1)} custom-call(bf16[512,128]{1,0:T(8,128)(2,1)} %x_ref.1), custom_call_target="tpu_custom_call" | custom-call | tf_op jit(solution)/shard_map/pallas_call | solution.py:130
  65.6 25.3 %shard_map.95 = bf16[4096,128]{1,0:T(8,128)(2,1)} custom-call(s32[256]{0:T(256)} %bitcast.30, s32[256]{0:T(256)} %bitcast.32, s32[1]{0:T(128)} %bitcast.20.count_ref, bf16[256,128,128]{2,1,0:T(8,128)(2,1)} %bitcast.22, bf16[8192,128]{1,0:T(8,128)(2,1)} %bitcast.25), custom_call_target="tpu_custom_call" | custom-call | flops 1073741824 | bytes 11534336 | tf_op jit(solution)/shard_map/pallas_call | solution.py:53
  90.9 28.7 %shard_map.96 = bf16[512,128]{1,0:T(8,128)(2,1)} custom-call(bf16[8,512,128]{2,1,0:T(8,128)(2,1)} %bitcast.27), custom_call_target="tpu_custom_call" | custom-call | tf_op jit(solution)/shard_map/pallas_call | solution.py:130
  119.6 0.0 copy-start.1
  119.6 1.2 convolution_convert_fusion
  120.8 0.8 copy.10
  121.6 0.0 reduce-scatter.4.cloned.1.call-update
  121.7 0.0 all-reduce.2.cloned.1.call-start
  121.7 16.6 %reduce-scatter.4.cloned.1.call-done = bf16[128,512]{1,0:T(8,128)(2,1)} async-done(((bf16[256,512]{1,0:T(8,128)(2,1)}), bf16[128,512]{1,0:T(8,128)(2,1)}) %reduce-scatter.4.cloned.1.call-update) | async-done | bytes 131088
  138.3 1.0 copy.11
  139.4 0.8 fusion.5
  140.2 5.1 %all_gather.3 = bf16[512,256]{1,0:T(8,128)(2,1)S(1)} all-gather(bf16[512,128]{1,0:T(8,128)(2,1)S(1)} %get-tuple-element.3), channel_id=1, replica_groups=mesh['row'=16,'col'=8,'feat'=2] {'feat'}, dimensions={1}, use_global_device_ids=true | all-gather | bytes 393216 | tf_op jit(solution)/shard_map/all_gather | solution.py:167
  145.3 0.2 fusion
  145.5 0.7 copy-done.2
  146.2 0.0 all-reduce.2.cloned.1.call-update
  146.2 0.9 convolution_convert_fusion.1.x_ref
  147.1 19.9 %shard_map.97 = bf16[8,512,128]{2,1,0:T(8,128)(2,1)} custom-call(bf16[512,128]{1,0:T(8,128)(2,1)} %convolution_convert_fusion.1.x_ref), custom_call_target="tpu_custom_call" | custom-call | tf_op jit(solution)/shard_map/pallas_call | solution.py:130
  167.0 32.7 %shard_map.98 = bf16[8192,128]{1,0:T(8,128)(2,1)} custom-call(s32[256]{0:T(256)} %bitcast.31, s32[256]{0:T(256)} %bitcast.33, s32[1]{0:T(128)} %bitcast.21.count_ref, bf16[256,128,128]{2,1,0:T(8,128)(2,1)} %bitcast.23, bf16[4096,128]{1,0:T(8,128)(2,1)} %bitcast.26), custom_call_target="tpu_custom_call" | custom-call | flops 1073741824 | bytes 11534336 | tf_op jit(solution)/shard_map/pallas_call | solution.py:53
  199.7 74.2 %shard_map.99 = bf16[512,128]{1,0:T(8,128)(2,1)} custom-call(bf16[16,512,128]{2,1,0:T(8,128)(2,1)} %bitcast.24), custom_call_target="tpu_custom_call" | custom-call | tf_op jit(solution)/shard_map/pallas_call | solution.py:130
  273.9 143.6 %all-reduce.2.cloned.1.call-done = f32[2,128,256]{2,1,0:T(8,128)} async-done(((f32[2,128,256]{2,1,0:T(8,128)}), f32[2,128,256]{2,1,0:T(8,128)}) %all-reduce.2.cloned.1.call-update) | async-done | bytes 262160 | tf_op jit(solution)/shard_map/psum | solution.py:174
  417.6 1.6 multiply_bitcast_fusion
  419.1 1.6 copy.16
  (6 shorter events, 0.0 us)
Async XLA Ops:
  7.2 112.5 %copy-start = (bf16[256,256]{1,0:T(8,128)(2,1)S(1)}, bf16[256,256]{1,0:T(8,128)(2,1)}, u32[]{:S(2)}) copy-start(bf16[256,256]{1,0:T(8,128)(2,1)} %param.12) | copy-start | bytes 393220
  7.2 131.1 %reduce-scatter.4.cloned.1.call-start = ((), (), s32[]{:S(2)}) async-start(), calls=%async_computation.2 | async-start | bytes 393216
  90.9 48.4 %copy-start.3 = (bf16[512,128]{1,0:T(8,128)(2,1)S(1)}, bf16[512,128]{1,0:T(8,128)(2,1)}, u32[]{:S(2)}) copy-start(bf16[512,128]{1,0:T(8,128)(2,1)} %param.13) | copy-start | bytes 393220
  119.6 25.6 %copy-start.1 = (bf16[512,128]{1,0:T(8,128)(2,1)S(1)}, bf16[512,128]{1,0:T(8,128)(2,1)}, u32[]{:S(2)}) copy-start(bf16[512,128]{1,0:T(8,128)(2,1)} %shard_map.96) | copy-start | bytes 393220
  121.7 295.9 %all-reduce.2.cloned.1.call-start = ((), (), s32[]{:S(2)}) async-start(), calls=%async_computation.1 | async-start | bytes 524288 | tf_op jit(solution)/shard_map/psum | solution.py:174
  145.5 0.7 copy-start.2
Sparse Core Ops, SparseCore 0:
  121.8 16.4 reduce-scatter.3
  146.3 271.1 all-reduce.1

commit v4 on v3

--- a/solution.py
+++ b/solution.py
@@ -137,6 +137,59 @@
     )(x)
 
 
+def butterfly_partners():
+    rounds = []
+    for axis in ("row", "col"):
+        bit = 1
+        while bit < lax.axis_size(axis):
+            rounds.append((axis, bit))
+            bit *= 2
+    return rounds
+
+
+def allreduce_kernel(x_ref, o_ref, bufs, recv, send_sems, recv_sems):
+    rounds = butterfly_partners()
+
+    def partner(axis, bit):
+        me = lax.axis_index(axis)
+        return me + bit * (1 - 2 * ((me // bit) % 2))
+
+    barrier = pltpu.get_barrier_semaphore()
+    for axis, bit in rounds:
+        pl.semaphore_signal(barrier, inc=1, device_id=mesh_coords(axis, partner(axis, bit)),
+                            device_id_type=pl.DeviceIdType.MESH)
+    pl.semaphore_wait(barrier, len(rounds))
+    for k, (axis, bit) in enumerate(rounds):
+        src = x_ref if k == 0 else bufs.at[k - 1]
+        copy = pltpu.make_async_remote_copy(
+            src_ref=src, dst_ref=recv.at[k], send_sem=send_sems.at[k], recv_sem=recv_sems.at[k],
+            device_id=mesh_coords(axis, partner(axis, bit)), device_id_type=pl.DeviceIdType.MESH)
+        copy.start()
+        copy.wait()
+        total = src[...] + recv[k]
+        if k == len(rounds) - 1:
+            o_ref[...] = total
+        else:
+            bufs[k] = total
+
+
+def allreduce(x, collective_id):
+    steps = len(butterfly_partners())
+    return pl.pallas_call(
+        allreduce_kernel,
+        out_shape=jax.ShapeDtypeStruct(x.shape, x.dtype),
+        in_specs=[pl.BlockSpec(memory_space=pltpu.VMEM)],
+        out_specs=pl.BlockSpec(memory_space=pltpu.VMEM),
+        scratch_shapes=[
+            pltpu.VMEM((max(steps - 1, 1),) + x.shape, x.dtype),
+            pltpu.VMEM((steps,) + x.shape, x.dtype),
+            pltpu.SemaphoreType.DMA((steps,)),
+            pltpu.SemaphoreType.DMA((steps,)),
+        ],
+        compiler_params=pltpu.CompilerParams(collective_id=collective_id, has_side_effects=True),
+    )(x)
+
+
 def shards(features, tile_rows, tile_cols, tile_count, tile_values, weights, cotangent):
     width = tile_values.shape[-1]
     local_tiles = tile_values[0, 0]
@@ -168,11 +221,7 @@
     weight_term = lax.dot_general(
         summed, grad_whole, (((0,), (0,)), ((), ())), preferred_element_type=jnp.float32
     )
-    n_feat = lax.axis_size("feat")
-    slots = jnp.zeros((n_feat,) + weight_term.shape, jnp.float32)
-    slots = lax.dynamic_update_slice_in_dim(slots, weight_term[None], feat_index, 0)
-    slots = lax.psum(slots, ("row", "col", "feat"))
-    weight_grad = lax.dynamic_index_in_dim(slots, feat_index, 0, keepdims=False) * node_total ** (-0.5)
+    weight_grad = allreduce(weight_term, 4) * node_total ** (-0.5)
     spread = lax.dot_general(
         grad_whole, weight_rows, (((1,), (1,)), ((), ())), preferred_element_type=jnp.float32
     ).astype(jnp.bfloat16)

time: 428 us -> 322 us (0.75)
  waiting for transfers between devices: 160 us -> 17.1 us
  Pallas kernels: 238 us -> 274 us
    psum x1 -> x0, waiting for transfers between devices: 144 us -> none  [shards(): slots = lax.psum(slots, ('row', 'col', 'feat'))]
    pallas_call x0 -> x1, Pallas kernels: none -> 42.8 us  [allreduce(): pl.pallas_call(allreduce_kernel, out_shape=jax.ShapeDtypeStruct(x.shape,...]
    pallas_call x2, Pallas kernels: 58 us -> 37.5 us  [tile_products(): pl.pallas_call(functools.partial(tile_kernel, transpose), out_shape=jax.S...]
    pallas_call x4, Pallas kernels: 180 us -> 194 us  [exchange(): pl.pallas_call(functools.partial(exchange_kernel, axis, mode), out_shape=...]
    unnamed x3 -> x2, waiting for transfers between devices: 16.6 us -> 17.1 us
  transfers between devices with their start and end apart: 2 -> 1, of which waited for: 2 -> 1; matrix products, arithmetic and copies ran while one was open for 0% -> 0% of each run, Pallas kernels for 30% -> 0%
where the time goes in v4:
time: 322 us; the launch traced here: 320 us
  Pallas kernels  274 us (85%)
  waiting for transfers between devices  17.1 us (5%)
  between operations  14.8 us (5%)
  blocking collectives  5.09 us (2%)
  local copies, waits for them, and re-layouts  3.44 us (1%)
    pallas_call x4, Pallas kernels, exchange(): pl.pallas_call(functools.partial(exchange_kernel, axis, mode), out_shape=...  194 us
    pallas_call x1, Pallas kernels, allreduce(): pl.pallas_call(allreduce_kernel, out_shape=jax.ShapeDtypeStruct(x.shape,...  42.8 us
    pallas_call x2, Pallas kernels, tile_products(): pl.pallas_call(functools.partial(tile_kernel, transpose), out_shape=jax.S...  37.5 us
    unnamed x2, waiting for transfers between devices  17.1 us
  transfers between devices with their start and end apart: 1, of which 1 were waited for; matrix products, arithmetic and copies ran while one was open for 0% of the time, Pallas kernels for 0%

profile of v4, /device:TPU:1, one launch (start us, length us, event | category | flops | bytes accessed | tf_op | source)
XLA Modules:
  0.0 319.7 jit_solution(15270800325147244947)
XLA Ops:
  7.2 0.0 copy-start
  7.2 0.0 reduce-scatter.4.cloned.1.call-start
  7.9 57.7 %shard_map.94 = bf16[16,512,128]{2,1,0:T(8,128)(2,1)} custom-call(bf16[512,128]{1,0:T(8,128)(2,1)} %x_ref.1), custom_call_target="tpu_custom_call" | custom-call | tf_op jit(solution)/shard_map/pallas_call | solution.py:130
  65.6 16.7 %shard_map.95 = bf16[4096,128]{1,0:T(8,128)(2,1)} custom-call(s32[256]{0:T(256)} %bitcast.24, s32[256]{0:T(256)} %bitcast.26, s32[1]{0:T(128)} %bitcast.14.count_ref, bf16[256,128,128]{2,1,0:T(8,128)(2,1)} %bitcast.16, bf16[8192,128]{1,0:T(8,128)(2,1)} %bitcast.19), custom_call_target="tpu_custom_call" | custom-call | flops 1073741824 | bytes 11534336 | tf_op jit(solution)/shard_map/pallas_call | solution.py:53
  82.3 38.4 %shard_map.96 = bf16[512,128]{1,0:T(8,128)(2,1)} custom-call(bf16[8,512,128]{2,1,0:T(8,128)(2,1)} %bitcast.21), custom_call_target="tpu_custom_call" | custom-call | tf_op jit(solution)/shard_map/pallas_call | solution.py:130
  120.7 0.0 copy-start.1
  120.7 0.0 copy-done
  120.7 1.2 convolution_convert_fusion
  121.9 0.8 copy.10
  122.7 0.0 reduce-scatter.4.cloned.1.call-update
  122.8 17.1 %reduce-scatter.4.cloned.1.call-done = bf16[128,512]{1,0:T(8,128)(2,1)} async-done(((bf16[256,512]{1,0:T(8,128)(2,1)}), bf16[128,512]{1,0:T(8,128)(2,1)}) %reduce-scatter.4.cloned.1.call-update) | async-done | bytes 131088
  139.9 1.0 copy.11
  140.9 0.0 copy-done.2
  140.9 0.8 fusion.4
  141.7 5.1 %all_gather.3 = bf16[512,256]{1,0:T(8,128)(2,1)S(1)} all-gather(bf16[512,128]{1,0:T(8,128)(2,1)S(1)} %get-tuple-element.3), channel_id=1, replica_groups=mesh['row'=16,'col'=8,'feat'=2] {'feat'}, dimensions={1}, use_global_device_ids=true | all-gather | bytes 393216 | tf_op jit(solution)/shard_map/all_gather | solution.py:220
  146.8 0.0 copy-done.1
  146.8 0.9 fusion.10.x_ref
  147.7 0.9 convolution_convert_fusion.1.x_ref
  148.6 42.8 %shard_map.100 = f32[128,256]{1,0:T(8,128)} custom-call(f32[128,256]{1,0:T(8,128)} %fusion.10.x_ref), custom_call_target="tpu_custom_call" | custom-call | tf_op jit(solution)/shard_map/pallas_call | solution.py:178
  191.4 1.6 broadcast_multiply_fusion
  193.0 11.7 %shard_map.97 = bf16[8,512,128]{2,1,0:T(8,128)(2,1)} custom-call(bf16[512,128]{1,0:T(8,128)(2,1)} %convolution_convert_fusion.1.x_ref), custom_call_target="tpu_custom_call" | custom-call | tf_op jit(solution)/shard_map/pallas_call | solution.py:130
  204.7 20.9 %shard_map.98 = bf16[8192,128]{1,0:T(8,128)(2,1)} custom-call(s32[256]{0:T(256)} %bitcast.25, s32[256]{0:T(256)} %bitcast.27, s32[1]{0:T(128)} %bitcast.15.count_ref, bf16[256,128,128]{2,1,0:T(8,128)(2,1)} %bitcast.17, bf16[4096,128]{1,0:T(8,128)(2,1)} %bitcast.20), custom_call_target="tpu_custom_call" | custom-call | flops 1073741824 | bytes 11534336 | tf_op jit(solution)/shard_map/pallas_call | solution.py:53
  225.6 85.7 %shard_map.99 = bf16[512,128]{1,0:T(8,128)(2,1)} custom-call(bf16[16,512,128]{2,1,0:T(8,128)(2,1)} %bitcast.18), custom_call_target="tpu_custom_call" | custom-call | tf_op jit(solution)/shard_map/pallas_call | solution.py:130
  311.3 1.6 copy.14
  (1 shorter events, 0.0 us)
Async XLA Ops:
  7.2 113.6 %copy-start = (bf16[256,256]{1,0:T(8,128)(2,1)S(1)}, bf16[256,256]{1,0:T(8,128)(2,1)}, u32[]{:S(2)}) copy-start(bf16[256,256]{1,0:T(8,128)(2,1)} %param.12) | copy-start | bytes 393220
  7.2 132.7 %reduce-scatter.4.cloned.1.call-start = ((), (), s32[]{:S(2)}) async-start(), calls=%async_computation.1 | async-start | bytes 393216
  82.3 58.7 %copy-start.2 = (bf16[512,128]{1,0:T(8,128)(2,1)S(1)}, bf16[512,128]{1,0:T(8,128)(2,1)}, u32[]{:S(2)}) copy-start(bf16[512,128]{1,0:T(8,128)(2,1)} %param.13) | copy-start | bytes 393220
  120.7 26.1 %copy-start.1 = (bf16[512,128]{1,0:T(8,128)(2,1)S(1)}, bf16[512,128]{1,0:T(8,128)(2,1)}, u32[]{:S(2)}) copy-start(bf16[512,128]{1,0:T(8,128)(2,1)} %shard_map.96) | copy-start | bytes 393220
Sparse Core Ops, SparseCore 0:
  122.9 16.9 reduce-scatter.3

commit v5 on v4

--- a/solution.py
+++ b/solution.py
@@ -7,25 +7,27 @@
 from jax.experimental.pallas import tpu as pltpu
 from jax.sharding import PartitionSpec as P
 
-GROUP = 8
+GROUP = 64
 
 
 def tile_kernel(transpose, rows_ref, cols_ref, count_ref, tiles_ref, panel_ref, out_ref, acc_ref):
     step = pl.program_id(0)
     width = tiles_ref.shape[-1]
     count = count_ref[0]
+    src_blocks = panel_ref.shape[0] // width
+    dst_blocks = acc_ref.shape[0] // width
 
     @pl.when(step == 0)
     def _():
         acc_ref[...] = jnp.zeros_like(acc_ref)
 
-    for j in range(GROUP):
-        slot = step * GROUP + j
-
-        @pl.when(slot < count)
-        def _():
+    @pl.when(step * GROUP < count)
+    def _():
+        terms = []
+        for j in range(GROUP):
+            slot = step * GROUP + j
             src = rows_ref[slot] if transpose else cols_ref[slot]
-            dst = cols_ref[slot] if transpose else rows_ref[slot]
+            src = jnp.minimum(jnp.maximum(src, 0), src_blocks - 1)
             block = panel_ref[pl.ds(pl.multiple_of(src * width, width), width), :]
             tile = tiles_ref[j]
             if transpose:
@@ -33,8 +35,13 @@
                                        preferred_element_type=jnp.float32)
             else:
                 term = jnp.dot(tile, block, preferred_element_type=jnp.float32)
+            terms.append(jnp.where(slot < count, term, 0.0))
+        for j in range(GROUP):
+            slot = step * GROUP + j
+            dst = cols_ref[slot] if transpose else rows_ref[slot]
+            dst = jnp.minimum(jnp.maximum(dst, 0), dst_blocks - 1)
             rows = pl.ds(pl.multiple_of(dst * width, width), width)
-            acc_ref[rows, :] += term
+            acc_ref[rows, :] += terms[j]
 
     @pl.when(step == pl.num_programs(0) - 1)
     def _():

time: 322 us -> 255 us (0.79)
  Pallas kernels: 274 us -> 208 us
    pallas_call x4, Pallas kernels: 194 us -> 154 us  [exchange(): pl.pallas_call(functools.partial(exchange_kernel, axis, mode), out_shape=...]
    pallas_call x2, Pallas kernels: 37.5 us -> 12.1 us  [tile_products(): pl.pallas_call(functools.partial(tile_kernel, transpose), out_shape=jax.S...]
where the time goes in v5:
time: 255 us
  Pallas kernels  208 us (82%)
  waiting for transfers between devices  17.4 us (7%)
  between operations  14.8 us (6%)
  blocking collectives  5.09 us (2%)
  local copies, waits for them, and re-layouts  3.44 us (1%)
  matrix products  2.93 us (1%)
    pallas_call x4, Pallas kernels, exchange(): pl.pallas_call(functools.partial(exchange_kernel, axis, mode), out_shape=...  154 us
    pallas_call x1, Pallas kernels, allreduce(): pl.pallas_call(allreduce_kernel, out_shape=jax.ShapeDtypeStruct(x.shape,...  42.8 us
    unnamed x2, waiting for transfers between devices  17.4 us
    pallas_call x2, Pallas kernels, tile_products(): pl.pallas_call(functools.partial(tile_kernel, transpose), out_shape=jax.S...  12.1 us
  transfers between devices with their start and end apart: 1, of which 1 were waited for; matrix products, arithmetic and copies ran while one was open for 0% of the time, Pallas kernels for 0%

profile of v5, /device:TPU:1, one launch (start us, length us, event | category | flops | bytes accessed | tf_op | source)
XLA Modules:
  0.0 254.5 jit_solution(5296342187734905226)
XLA Ops:
  7.2 0.0 copy-start
  7.2 0.0 reduce-scatter.4.cloned.1.call-start
  7.9 57.7 %shard_map.94 = bf16[16,512,128]{2,1,0:T(8,128)(2,1)} custom-call(bf16[512,128]{1,0:T(8,128)(2,1)} %x_ref.1), custom_call_target="tpu_custom_call" | custom-call | tf_op jit(solution)/shard_map/pallas_call | solution.py:137
  65.6 5.9 %shard_map.95 = bf16[4096,128]{1,0:T(8,128)(2,1)} custom-call(s32[256]{0:T(256)} %bitcast.24, s32[256]{0:T(256)} %bitcast.26, s32[1]{0:T(128)} %bitcast.14.count_ref, bf16[256,128,128]{2,1,0:T(8,128)(2,1)} %bitcast.16, bf16[8192,128]{1,0:T(8,128)(2,1)} %bitcast.19), custom_call_target="tpu_custom_call" | custom-call | flops 1073741824 | bytes 11534336 | tf_op jit(solution)/shard_map/pallas_call | solution.py:60
  71.5 21.7 %shard_map.96 = bf16[512,128]{1,0:T(8,128)(2,1)} custom-call(bf16[8,512,128]{2,1,0:T(8,128)(2,1)} %bitcast.21), custom_call_target="tpu_custom_call" | custom-call | tf_op jit(solution)/shard_map/pallas_call | solution.py:137
  93.1 0.0 copy-start.1
  93.2 0.0 copy-done
  93.2 1.2 convolution_convert_fusion
  94.3 0.8 copy.10
  95.2 0.0 reduce-scatter.4.cloned.1.call-update
  95.2 17.4 %reduce-scatter.4.cloned.1.call-done = bf16[128,512]{1,0:T(8,128)(2,1)} async-done(((bf16[256,512]{1,0:T(8,128)(2,1)}), bf16[128,512]{1,0:T(8,128)(2,1)}) %reduce-scatter.4.cloned.1.call-update) | async-done | bytes 131088
  112.6 1.0 copy.11
  113.6 0.0 copy-done.2
  113.6 0.8 fusion.4
  114.4 5.1 %all_gather.3 = bf16[512,256]{1,0:T(8,128)(2,1)S(1)} all-gather(bf16[512,128]{1,0:T(8,128)(2,1)S(1)} %get-tuple-element.3), channel_id=1, replica_groups=mesh['row'=16,'col'=8,'feat'=2] {'feat'}, dimensions={1}, use_global_device_ids=true | all-gather | bytes 393216 | tf_op jit(solution)/shard_map/all_gather | solution.py:227
  119.5 0.0 copy-done.1
  119.5 0.9 fusion.10.x_ref
  120.4 0.9 convolution_convert_fusion.1.x_ref
  121.3 42.8 %shard_map.100 = f32[128,256]{1,0:T(8,128)} custom-call(f32[128,256]{1,0:T(8,128)} %fusion.10.x_ref), custom_call_target="tpu_custom_call" | custom-call | tf_op jit(solution)/shard_map/pallas_call | solution.py:185
  164.0 1.6 broadcast_multiply_fusion
  165.6 11.7 %shard_map.97 = bf16[8,512,128]{2,1,0:T(8,128)(2,1)} custom-call(bf16[512,128]{1,0:T(8,128)(2,1)} %convolution_convert_fusion.1.x_ref), custom_call_target="tpu_custom_call" | custom-call | tf_op jit(solution)/shard_map/pallas_call | solution.py:137
  177.3 6.2 %shard_map.98 = bf16[8192,128]{1,0:T(8,128)(2,1)} custom-call(s32[256]{0:T(256)} %bitcast.25, s32[256]{0:T(256)} %bitcast.27, s32[1]{0:T(128)} %bitcast.15.count_ref, bf16[256,128,128]{2,1,0:T(8,128)(2,1)} %bitcast.17, bf16[4096,128]{1,0:T(8,128)(2,1)} %bitcast.20), custom_call_target="tpu_custom_call" | custom-call | flops 1073741824 | bytes 11534336 | tf_op jit(solution)/shard_map/pallas_call | solution.py:60
  183.5 62.6 %shard_map.99 = bf16[512,128]{1,0:T(8,128)(2,1)} custom-call(bf16[16,512,128]{2,1,0:T(8,128)(2,1)} %bitcast.18), custom_call_target="tpu_custom_call" | custom-call | tf_op jit(solution)/shard_map/pallas_call | solution.py:137
  246.1 1.6 copy.14
  (1 shorter events, 0.0 us)
Async XLA Ops:
  7.2 86.0 %copy-start = (bf16[256,256]{1,0:T(8,128)(2,1)S(1)}, bf16[256,256]{1,0:T(8,128)(2,1)}, u32[]{:S(2)}) copy-start(bf16[256,256]{1,0:T(8,128)(2,1)} %param.12) | copy-start | bytes 393220
  7.2 105.4 %reduce-scatter.4.cloned.1.call-start = ((), (), s32[]{:S(2)}) async-start(), calls=%async_computation.1 | async-start | bytes 393216
  71.5 42.1 %copy-start.2 = (bf16[512,128]{1,0:T(8,128)(2,1)S(1)}, bf16[512,128]{1,0:T(8,128)(2,1)}, u32[]{:S(2)}) copy-start(bf16[512,128]{1,0:T(8,128)(2,1)} %param.13) | copy-start | bytes 393220
  93.1 26.4 %copy-start.1 = (bf16[512,128]{1,0:T(8,128)(2,1)S(1)}, bf16[512,128]{1,0:T(8,128)(2,1)}, u32[]{:S(2)}) copy-start(bf16[512,128]{1,0:T(8,128)(2,1)} %shard_map.96) | copy-start | bytes 393220
Sparse Core Ops, SparseCore 0:
  95.3 17.2 reduce-scatter.3

commit v6 on v5

--- a/solution.py
+++ b/solution.py
@@ -83,26 +83,30 @@
     return tuple(peer if name == axis else lax.axis_index(name) for name in ("row", "col", "feat"))
 
 
-def exchange_kernel(axis, mode, x_ref, o_ref, *scratch):
-    n = lax.axis_size(axis)
-    me = lax.axis_index(axis)
+def exchange_kernel(axis, stride, size, mode, x_ref, o_ref, *scratch):
+    index = lax.axis_index(axis)
+    me = (index // stride) % size
+    base = index - me * stride
+
+    def member(k):
+        return mesh_coords(axis, base + k * stride)
+
     if mode == "gather":
         recv_ref, (send_sems, recv_sems) = o_ref, scratch
     else:
         recv_ref, send_sems, recv_sems = scratch
     barrier = pltpu.get_barrier_semaphore()
-    for d in range(1, n):
-        peer = lax.rem(me + d, n)
-        pl.semaphore_signal(barrier, inc=1, device_id=mesh_coords(axis, peer),
+    for d in range(1, size):
+        pl.semaphore_signal(barrier, inc=1, device_id=member(lax.rem(me + d, size)),
                             device_id_type=pl.DeviceIdType.MESH)
-    pl.semaphore_wait(barrier, n - 1)
+    pl.semaphore_wait(barrier, size - 1)
     copies = []
-    for d in range(1, n):
-        peer = lax.rem(me + d, n)
+    for d in range(1, size):
+        peer = lax.rem(me + d, size)
         src = x_ref if mode == "gather" else x_ref.at[peer]
         copy = pltpu.make_async_remote_copy(
             src_ref=src, dst_ref=recv_ref.at[me], send_sem=send_sems.at[d],
-            recv_sem=recv_sems.at[me], device_id=mesh_coords(axis, peer),
+            recv_sem=recv_sems.at[me], device_id=member(peer),
             device_id_type=pl.DeviceIdType.MESH)
         copy.start()
         copies.append(copy)
@@ -110,11 +114,11 @@
         o_ref[me] = x_ref[...]
     else:
         total = x_ref[me].astype(jnp.float32)
-    for d in range(1, n):
-        src_dev = lax.rem(me + n - d, n)
+    for d in range(1, size):
+        src_dev = lax.rem(me + size - d, size)
         incoming = pltpu.make_async_remote_copy(
             src_ref=recv_ref.at[src_dev], dst_ref=recv_ref.at[src_dev], send_sem=send_sems.at[d],
-            recv_sem=recv_sems.at[src_dev], device_id=mesh_coords(axis, src_dev),
+            recv_sem=recv_sems.at[src_dev], device_id=member(src_dev),
             device_id_type=pl.DeviceIdType.MESH)
         incoming.wait_recv()
         if mode != "gather":
@@ -125,17 +129,17 @@
         o_ref[...] = total.astype(o_ref.dtype)
 
 
-def exchange(x, axis, mode, collective_id):
-    n = lax.axis_size(axis)
+def exchange(x, axis, mode, collective_id, stride=1, size=None):
+    size = lax.axis_size(axis) if size is None else size
     if mode == "gather":
-        out_shape = (n,) + x.shape
+        out_shape = (size,) + x.shape
         scratch = []
     else:
         out_shape = x.shape[1:]
         scratch = [pltpu.VMEM(x.shape, x.dtype)]
-    scratch += [pltpu.SemaphoreType.DMA((n,)), pltpu.SemaphoreType.DMA((n,))]
+    scratch += [pltpu.SemaphoreType.DMA((size,)), pltpu.SemaphoreType.DMA((size,))]
     return pl.pallas_call(
-        functools.partial(exchange_kernel, axis, mode),
+        functools.partial(exchange_kernel, axis, stride, size, mode),
         out_shape=jax.ShapeDtypeStruct(out_shape, x.dtype),
         in_specs=[pl.BlockSpec(memory_space=pltpu.VMEM)],
         out_specs=pl.BlockSpec(memory_space=pltpu.VMEM),
@@ -211,7 +215,12 @@
     row_blocks = local_blocks * n_coldev
     col_blocks = local_blocks * n_rowdev
     node_total = features.shape[0] * n_rowdev * n_coldev
-    panel = exchange(features, "row", "gather", 0).reshape(-1, feat_half)
+    pair = 2 if n_rowdev % 2 == 0 else 1
+    chips = n_rowdev // pair
+    panel = exchange(features, "row", "gather", 0, stride=pair, size=chips)
+    panel = exchange(panel, "row", "gather", 5, stride=1, size=pair).reshape(-1, feat_half)
+    owner = block_cols // local_blocks
+    block_cols = ((owner % pair) * chips + owner // pair) * local_blocks + block_cols % local_blocks
     partial_value = tile_products(local_tiles, block_rows, block_cols, count, panel,
                                   row_blocks, transpose=False)
     summed = exchange(partial_value.reshape(n_coldev, -1, feat_half), "col", "scatter", 1)
@@ -235,7 +244,10 @@
     spread_panel = exchange(spread, "col", "gather", 2).reshape(-1, feat_half)
     back_partial = tile_products(local_tiles, block_rows, block_cols, count, spread_panel,
                                  col_blocks, transpose=True)
-    back_summed = exchange(back_partial.reshape(n_rowdev, -1, feat_half), "row", "scatter", 3)
+    back_pairs = exchange(back_partial.reshape(pair, -1, feat_half), "row", "scatter", 3,
+                          stride=1, size=pair)
+    back_summed = exchange(back_pairs.reshape(chips, -1, feat_half), "row", "scatter", 6,
+                           stride=pair, size=chips)
     return (activated, back_summed, weight_grad)
 
 

time: 255 us -> 223 us (0.87)
  Pallas kernels: 208 us -> 174 us
    pallas_call x4 -> x6, Pallas kernels: 154 us -> 114 us  [exchange(): pl.pallas_call(functools.partial(exchange_kernel, axis, stride, size, mod...]
    pallas_call x2, Pallas kernels: 12.1 us -> 17.1 us  [tile_products(): pl.pallas_call(functools.partial(tile_kernel, transpose), out_shape=jax.S...]
where the time goes in v6:
time: 223 us; the launch traced here: 221 us
  Pallas kernels  174 us (78%)
  waiting for transfers between devices  17.5 us (8%)
  between operations  14.8 us (7%)
  blocking collectives  5.07 us (2%)
  other arithmetic  3.65 us (2%)
  local copies, waits for them, and re-layouts  3.44 us (2%)
  matrix products  2.94 us (1%)
    pallas_call x6, Pallas kernels, exchange(): pl.pallas_call(functools.partial(exchange_kernel, axis, stride, size, mod...  114 us
    pallas_call x1, Pallas kernels, allreduce(): pl.pallas_call(allreduce_kernel, out_shape=jax.ShapeDtypeStruct(x.shape,...  42.8 us
    unnamed x2, waiting for transfers between devices  17.5 us
    pallas_call x2, Pallas kernels, tile_products(): pl.pallas_call(functools.partial(tile_kernel, transpose), out_shape=jax.S...  17.1 us
    all_gather x1, blocking collectives, shards(): grad_whole = lax.all_gather(grad_out, 'feat', axis=1, tiled=True)  5.07 us
  transfers between devices with their start and end apart: 1, of which 1 were waited for; matrix products, arithmetic and copies ran while one was open for 0% of the time, Pallas kernels for 0%

profile of v6, /device:TPU:1, one launch (start us, length us, event | category | flops | bytes accessed | tf_op | source)
XLA Modules:
  0.0 221.1 jit_solution(7558791853125694622)
XLA Ops:
  7.2 0.0 copy-start
  7.2 0.0 reduce-scatter.4.cloned.1.call-start
  7.9 1.3 fusion.10.cols_ref
  9.2 33.7 %shard_map.94.x_ref = bf16[8,512,128]{2,1,0:T(8,128)(2,1)} custom-call(bf16[512,128]{1,0:T(8,128)(2,1)} %x_ref.1), custom_call_target="tpu_custom_call" | custom-call | tf_op jit(solution)/shard_map/pallas_call | solution.py:141
  42.9 6.0 %shard_map.95 = bf16[2,8,512,128]{3,2,1,0:T(8,128)(2,1)} custom-call(bf16[8,512,128]{2,1,0:T(8,128)(2,1)} %shard_map.94.x_ref), custom_call_target="tpu_custom_call" | custom-call | tf_op jit(solution)/shard_map/pallas_call | solution.py:141
  48.9 8.3 %shard_map.96 = bf16[4096,128]{1,0:T(8,128)(2,1)} custom-call(s32[256]{0:T(256)} %bitcast.26, s32[256]{0:T(256)} %fusion.10.cols_ref, s32[1]{0:T(128)} %bitcast.15.count_ref, bf16[256,128,128]{2,1,0:T(8,128)(2,1)} %bitcast.17, bf16[8192,128]{1,0:T(8,128)(2,1)} %bitcast.20), custom_call_target="tpu_custom_call" | custom-call | flops 1073741824 | bytes 11534336 | tf_op jit(solution)/shard_map/pallas_call | solution.py:60
  57.2 20.7 %shard_map.97 = bf16[512,128]{1,0:T(8,128)(2,1)} custom-call(bf16[8,512,128]{2,1,0:T(8,128)(2,1)} %bitcast.22), custom_call_target="tpu_custom_call" | custom-call | tf_op jit(solution)/shard_map/pallas_call | solution.py:141
  78.0 1.2 convolution_convert_fusion
  79.2 0.8 copy.10
  80.0 0.0 reduce-scatter.4.cloned.1.call-update
  80.0 17.4 %reduce-scatter.4.cloned.1.call-done = bf16[128,512]{1,0:T(8,128)(2,1)} async-done(((bf16[256,512]{1,0:T(8,128)(2,1)}), bf16[128,512]{1,0:T(8,128)(2,1)}) %reduce-scatter.4.cloned.1.call-update) | async-done | bytes 131088
  97.5 1.0 copy.11
  98.5 0.0 copy-done.2
  98.5 0.8 fusion.4
  99.3 5.1 %all_gather.3 = bf16[512,256]{1,0:T(8,128)(2,1)S(1)} all-gather(bf16[512,128]{1,0:T(8,128)(2,1)S(1)} %get-tuple-element.3), channel_id=1, replica_groups=mesh['row'=16,'col'=8,'feat'=2] {'feat'}, dimensions={1}, use_global_device_ids=true | all-gather | bytes 393216 | tf_op jit(solution)/shard_map/all_gather | solution.py:236
  104.4 0.9 fusion.13.x_ref
  105.3 0.9 convolution_convert_fusion.1.x_ref
  106.1 42.8 %shard_map.102 = f32[128,256]{1,0:T(8,128)} custom-call(f32[128,256]{1,0:T(8,128)} %fusion.13.x_ref), custom_call_target="tpu_custom_call" | custom-call | tf_op jit(solution)/shard_map/pallas_call | solution.py:189
  149.0 1.6 broadcast_multiply_fusion
  150.6 11.7 %shard_map.98 = bf16[8,512,128]{2,1,0:T(8,128)(2,1)} custom-call(bf16[512,128]{1,0:T(8,128)(2,1)} %convolution_convert_fusion.1.x_ref), custom_call_target="tpu_custom_call" | custom-call | tf_op jit(solution)/shard_map/pallas_call | solution.py:141
  162.3 8.8 %shard_map.99 = bf16[8192,128]{1,0:T(8,128)(2,1)} custom-call(s32[256]{0:T(256)} %bitcast.27, s32[256]{0:T(256)} %fusion.10.cols_ref, s32[1]{0:T(128)} %bitcast.16.count_ref, bf16[256,128,128]{2,1,0:T(8,128)(2,1)} %bitcast.18, bf16[4096,128]{1,0:T(8,128)(2,1)} %bitcast.21), custom_call_target="tpu_custom_call" | custom-call | flops 1073741824 | bytes 11534336 | tf_op jit(solution)/shard_map/pallas_call | solution.py:60
  171.0 11.4 %shard_map.100 = bf16[4096,128]{1,0:T(8,128)(2,1)} custom-call(bf16[2,4096,128]{2,1,0:T(8,128)(2,1)} %bitcast.19), custom_call_target="tpu_custom_call" | custom-call | tf_op jit(solution)/shard_map/pallas_call | solution.py:141
  182.4 30.3 %shard_map.101 = bf16[512,128]{1,0:T(8,128)(2,1)} custom-call(bf16[8,512,128]{2,1,0:T(8,128)(2,1)} %bitcast.23), custom_call_target="tpu_custom_call" | custom-call | tf_op jit(solution)/shard_map/pallas_call | solution.py:141
  212.7 1.6 copy.14
  (4 shorter events, 0.0 us)
Async XLA Ops:
  7.2 70.8 %copy-start = (bf16[256,256]{1,0:T(8,128)(2,1)S(1)}, bf16[256,256]{1,0:T(8,128)(2,1)}, u32[]{:S(2)}) copy-start(bf16[256,256]{1,0:T(8,128)(2,1)} %param.12) | copy-start | bytes 393220
  7.2 90.3 %reduce-scatter.4.cloned.1.call-start = ((), (), s32[]{:S(2)}) async-start(), calls=%async_computation.1 | async-start | bytes 393216
  57.2 41.3 %copy-start.2 = (bf16[512,128]{1,0:T(8,128)(2,1)S(1)}, bf16[512,128]{1,0:T(8,128)(2,1)}, u32[]{:S(2)}) copy-start(bf16[512,128]{1,0:T(8,128)(2,1)} %param.13) | copy-start | bytes 393220
  78.0 26.4 %copy-start.1 = (bf16[512,128]{1,0:T(8,128)(2,1)S(1)}, bf16[512,128]{1,0:T(8,128)(2,1)}, u32[]{:S(2)}) copy-start(bf16[512,128]{1,0:T(8,128)(2,1)} %shard_map.97) | copy-start | bytes 393220
Sparse Core Ops, SparseCore 0:
  80.1 17.2 reduce-scatter.3

commit v7 on v6

--- a/solution.py
+++ b/solution.py
@@ -148,52 +148,82 @@
     )(x)
 
 
-def butterfly_partners():
-    rounds = []
-    for axis in ("row", "col"):
-        bit = 1
-        while bit < lax.axis_size(axis):
-            rounds.append((axis, bit))
-            bit *= 2
-    return rounds
-
-
-def allreduce_kernel(x_ref, o_ref, bufs, recv, send_sems, recv_sems):
-    rounds = butterfly_partners()
+def reduction_plan(rows):
+    pairs = []
+    for bit in (1, 2, 4, 8, 16, 32, 64):
+        for axis in ("row", "col"):
+            if bit < lax.axis_size(axis):
+                pairs.append((axis, bit))
+    halving = []
+    while pairs and rows // 2 >= 8 and rows % 16 == 0:
+        halving.append(pairs.pop(0))
+        rows //= 2
+    return halving, pairs
+
+
+def allreduce_kernel(x_ref, o_ref, recv, send_sems, recv_sems):
+    halving, whole = reduction_plan(x_ref.shape[0])
+
+    def bitval(axis, bit):
+        return (lax.axis_index(axis) // bit) % 2
 
     def partner(axis, bit):
-        me = lax.axis_index(axis)
-        return me + bit * (1 - 2 * ((me // bit) % 2))
+        return mesh_coords(axis, lax.axis_index(axis) + bit * (1 - 2 * bitval(axis, bit)))
 
     barrier = pltpu.get_barrier_semaphore()
-    for axis, bit in rounds:
-        pl.semaphore_signal(barrier, inc=1, device_id=mesh_coords(axis, partner(axis, bit)),
+    for axis, bit in halving + whole:
+        pl.semaphore_signal(barrier, inc=1, device_id=partner(axis, bit),
                             device_id_type=pl.DeviceIdType.MESH)
-    pl.semaphore_wait(barrier, len(rounds))
-    for k, (axis, bit) in enumerate(rounds):
-        src = x_ref if k == 0 else bufs.at[k - 1]
+    pl.semaphore_wait(barrier, len(halving) + len(whole))
+
+    o_ref[...] = x_ref[...]
+    k = 0
+
+    def swap(k, axis, bit, send_rows, length):
         copy = pltpu.make_async_remote_copy(
-            src_ref=src, dst_ref=recv.at[k], send_sem=send_sems.at[k], recv_sem=recv_sems.at[k],
-            device_id=mesh_coords(axis, partner(axis, bit)), device_id_type=pl.DeviceIdType.MESH)
+            src_ref=o_ref.at[pl.ds(send_rows, length)], dst_ref=recv.at[k, pl.ds(0, length)],
+            send_sem=send_sems.at[k], recv_sem=recv_sems.at[k],
+            device_id=partner(axis, bit), device_id_type=pl.DeviceIdType.MESH)
         copy.start()
         copy.wait()
-        total = src[...] + recv[k]
-        if k == len(rounds) - 1:
-            o_ref[...] = total
-        else:
-            bufs[k] = total
+
+    lo = jnp.int32(0)
+    length = x_ref.shape[0]
+    starts = []
+    for axis, bit in halving:
+        length //= 2
+        mine = bitval(axis, bit)
+        starts.append(lo)
+        keep = pl.multiple_of(lo + mine * length, 8)
+        give = pl.multiple_of(lo + (1 - mine) * length, 8)
+        swap(k, axis, bit, give, length)
+        o_ref[pl.ds(keep, length)] = o_ref[pl.ds(keep, length)] + recv[k, pl.ds(0, length)]
+        lo = keep
+        k += 1
+    for axis, bit in whole:
+        swap(k, axis, bit, lo, length)
+        o_ref[pl.ds(lo, length)] = o_ref[pl.ds(lo, length)] + recv[k, pl.ds(0, length)]
+        k += 1
+    for (axis, bit), base in zip(reversed(halving), reversed(starts)):
+        mine = bitval(axis, bit)
+        other = pl.multiple_of(base + (1 - mine) * length, 8)
+        swap(k, axis, bit, lo, length)
+        o_ref[pl.ds(other, length)] = recv[k, pl.ds(0, length)]
+        lo = base
+        length *= 2
+        k += 1
 
 
 def allreduce(x, collective_id):
-    steps = len(butterfly_partners())
+    halving, whole = reduction_plan(x.shape[0])
+    steps = 2 * len(halving) + len(whole)
     return pl.pallas_call(
         allreduce_kernel,
         out_shape=jax.ShapeDtypeStruct(x.shape, x.dtype),
         in_specs=[pl.BlockSpec(memory_space=pltpu.VMEM)],
         out_specs=pl.BlockSpec(memory_space=pltpu.VMEM),
         scratch_shapes=[
-            pltpu.VMEM((max(steps - 1, 1),) + x.shape, x.dtype),
-            pltpu.VMEM((steps,) + x.shape, x.dtype),
+            pltpu.VMEM((steps, x.shape[0] // 2) + x.shape[1:], x.dtype),
             pltpu.SemaphoreType.DMA((steps,)),
             pltpu.SemaphoreType.DMA((steps,)),
         ],

time: 223 us -> 220 us (0.987)
  Pallas kernels: 174 us -> 169 us
    pallas_call x1, Pallas kernels: 42.8 us -> 40.1 us  [allreduce(): pl.pallas_call(allreduce_kernel, out_shape=jax.ShapeDtypeStruct(x.shape,...]
where the time goes in v7:
time: 220 us; the launch traced here: 217 us
  Pallas kernels  169 us (77%)
  waiting for transfers between devices  17.4 us (8%)
  between operations  14.8 us (7%)
  blocking collectives  5.09 us (2%)
  other arithmetic  3.65 us (2%)
  local copies, waits for them, and re-layouts  3.44 us (2%)
  matrix products  2.94 us (1%)
    pallas_call x6, Pallas kernels, exchange(): pl.pallas_call(functools.partial(exchange_kernel, axis, stride, size, mod...  114 us
    pallas_call x1, Pallas kernels, allreduce(): pl.pallas_call(allreduce_kernel, out_shape=jax.ShapeDtypeStruct(x.shape,...  40.1 us
    unnamed x2, waiting for transfers between devices  17.4 us
    pallas_call x2, Pallas kernels, tile_products(): pl.pallas_call(functools.partial(tile_kernel, transpose), out_shape=jax.S...  15.2 us
    all_gather x1, blocking collectives, shards(): grad_whole = lax.all_gather(grad_out, 'feat', axis=1, tiled=True)  5.09 us
  transfers between devices with their start and end apart: 1, of which 1 were waited for; matrix products, arithmetic and copies ran while one was open for 0% of the time, Pallas kernels for 0%

profile of v7, /device:TPU:1, one launch (start us, length us, event | category | flops | bytes accessed | tf_op | source)
XLA Modules:
  0.0 216.5 jit_solution(724050215123984874)
XLA Ops:
  7.2 0.0 copy-start
  7.2 0.0 reduce-scatter.4.cloned.1.call-start
  7.9 1.3 fusion.10.cols_ref
  9.2 33.7 %shard_map.94.x_ref = bf16[8,512,128]{2,1,0:T(8,128)(2,1)} custom-call(bf16[512,128]{1,0:T(8,128)(2,1)} %x_ref.1), custom_call_target="tpu_custom_call" | custom-call | tf_op jit(solution)/shard_map/pallas_call | solution.py:141
  42.9 6.0 %shard_map.95 = bf16[2,8,512,128]{3,2,1,0:T(8,128)(2,1)} custom-call(bf16[8,512,128]{2,1,0:T(8,128)(2,1)} %shard_map.94.x_ref), custom_call_target="tpu_custom_call" | custom-call | tf_op jit(solution)/shard_map/pallas_call | solution.py:141
  48.9 7.4 %shard_map.96 = bf16[4096,128]{1,0:T(8,128)(2,1)} custom-call(s32[256]{0:T(256)} %bitcast.26, s32[256]{0:T(256)} %fusion.10.cols_ref, s32[1]{0:T(128)} %bitcast.15.count_ref, bf16[256,128,128]{2,1,0:T(8,128)(2,1)} %bitcast.17, bf16[8192,128]{1,0:T(8,128)(2,1)} %bitcast.20), custom_call_target="tpu_custom_call" | custom-call | flops 1073741824 | bytes 11534336 | tf_op jit(solution)/shard_map/pallas_call | solution.py:60
  56.3 21.6 %shard_map.97 = bf16[512,128]{1,0:T(8,128)(2,1)} custom-call(bf16[8,512,128]{2,1,0:T(8,128)(2,1)} %bitcast.22), custom_call_target="tpu_custom_call" | custom-call | tf_op jit(solution)/shard_map/pallas_call | solution.py:141
  77.9 1.2 convolution_convert_fusion
  79.1 0.8 copy.10
  79.9 0.0 reduce-scatter.4.cloned.1.call-update
  80.0 17.4 %reduce-scatter.4.cloned.1.call-done = bf16[128,512]{1,0:T(8,128)(2,1)} async-done(((bf16[256,512]{1,0:T(8,128)(2,1)}), bf16[128,512]{1,0:T(8,128)(2,1)}) %reduce-scatter.4.cloned.1.call-update) | async-done | bytes 131088
  97.3 1.0 copy.11
  98.3 0.0 copy-done.2
  98.4 0.8 fusion.4
  99.2 5.1 %all_gather.3 = bf16[512,256]{1,0:T(8,128)(2,1)S(1)} all-gather(bf16[512,128]{1,0:T(8,128)(2,1)S(1)} %get-tuple-element.3), channel_id=1, replica_groups=mesh['row'=16,'col'=8,'feat'=2] {'feat'}, dimensions={1}, use_global_device_ids=true | all-gather | bytes 393216 | tf_op jit(solution)/shard_map/all_gather | solution.py:266
  104.3 0.9 fusion.13.x_ref
  105.2 0.9 convolution_convert_fusion.1.x_ref
  106.0 40.1 %shard_map.102 = f32[128,256]{1,0:T(8,128)} custom-call(f32[128,256]{1,0:T(8,128)} %fusion.13.x_ref), custom_call_target="tpu_custom_call" | custom-call | tf_op jit(solution)/shard_map/pallas_call | solution.py:220
  146.1 1.6 broadcast_multiply_fusion
  147.7 17.5 %shard_map.98 = bf16[8,512,128]{2,1,0:T(8,128)(2,1)} custom-call(bf16[512,128]{1,0:T(8,128)(2,1)} %convolution_convert_fusion.1.x_ref), custom_call_target="tpu_custom_call" | custom-call | tf_op jit(solution)/shard_map/pallas_call | solution.py:141
  165.2 7.8 %shard_map.99 = bf16[8192,128]{1,0:T(8,128)(2,1)} custom-call(s32[256]{0:T(256)} %bitcast.27, s32[256]{0:T(256)} %fusion.10.cols_ref, s32[1]{0:T(128)} %bitcast.16.count_ref, bf16[256,128,128]{2,1,0:T(8,128)(2,1)} %bitcast.18, bf16[4096,128]{1,0:T(8,128)(2,1)} %bitcast.21), custom_call_target="tpu_custom_call" | custom-call | flops 1073741824 | bytes 11534336 | tf_op jit(solution)/shard_map/pallas_call | solution.py:60
  172.9 6.3 %shard_map.100 = bf16[4096,128]{1,0:T(8,128)(2,1)} custom-call(bf16[2,4096,128]{2,1,0:T(8,128)(2,1)} %bitcast.19), custom_call_target="tpu_custom_call" | custom-call | tf_op jit(solution)/shard_map/pallas_call | solution.py:141
  179.2 28.9 %shard_map.101 = bf16[512,128]{1,0:T(8,128)(2,1)} custom-call(bf16[8,512,128]{2,1,0:T(8,128)(2,1)} %bitcast.23), custom_call_target="tpu_custom_call" | custom-call | tf_op jit(solution)/shard_map/pallas_call | solution.py:141
  208.1 1.6 copy.14
  (4 shorter events, 0.0 us)
Async XLA Ops:
  7.2 70.8 %copy-start = (bf16[256,256]{1,0:T(8,128)(2,1)S(1)}, bf16[256,256]{1,0:T(8,128)(2,1)}, u32[]{:S(2)}) copy-start(bf16[256,256]{1,0:T(8,128)(2,1)} %param.12) | copy-start | bytes 393220
  7.2 90.1 %reduce-scatter.4.cloned.1.call-start = ((), (), s32[]{:S(2)}) async-start(), calls=%async_computation.1 | async-start | bytes 393216
  56.3 42.1 %copy-start.2 = (bf16[512,128]{1,0:T(8,128)(2,1)S(1)}, bf16[512,128]{1,0:T(8,128)(2,1)}, u32[]{:S(2)}) copy-start(bf16[512,128]{1,0:T(8,128)(2,1)} %param.13) | copy-start | bytes 393220
  77.9 26.3 %copy-start.1 = (bf16[512,128]{1,0:T(8,128)(2,1)S(1)}, bf16[512,128]{1,0:T(8,128)(2,1)}, u32[]{:S(2)}) copy-start(bf16[512,128]{1,0:T(8,128)(2,1)} %shard_map.97) | copy-start | bytes 393220
Sparse Core Ops, SparseCore 0:
  80.1 17.1 reduce-scatter.3

commit v8 on v7

--- a/solution.py
+++ b/solution.py
@@ -254,22 +254,30 @@
     partial_value = tile_products(local_tiles, block_rows, block_cols, count, panel,
                                   row_blocks, transpose=False)
     summed = exchange(partial_value.reshape(n_coldev, -1, feat_half), "col", "scatter", 1)
-    weight_rows = lax.dynamic_slice_in_dim(weights, feat_index * feat_half, feat_half, 0)
-    mix_term = jnp.dot(summed, weight_rows, preferred_element_type=jnp.float32)
-    hidden = lax.psum_scatter(
-        mix_term.astype(jnp.bfloat16), "feat", scatter_dimension=1, tiled=True
-    ).astype(jnp.float32)
+    n_feat = lax.axis_size("feat")
+    agg_halves = exchange(summed, "feat", "gather", 7)
+    weight_cols = lax.dynamic_slice_in_dim(weights, feat_index * feat_half, feat_half, 1)
+    hidden = sum(
+        jnp.dot(agg_halves[h], weight_cols[h * feat_half:(h + 1) * feat_half],
+                preferred_element_type=jnp.float32)
+        for h in range(n_feat)
+    )
     negative = jnp.minimum(hidden, 0.0)
     activated = jnp.where(hidden > 0, hidden, jnp.expm1(negative)).astype(jnp.bfloat16)
     slope_factor = jnp.where(hidden > 0, 1.0, jnp.exp(negative))
     grad_out = (cotangent.astype(jnp.float32) * slope_factor).astype(jnp.bfloat16)
-    grad_whole = lax.all_gather(grad_out, "feat", axis=1, tiled=True)
-    weight_term = lax.dot_general(
-        summed, grad_whole, (((0,), (0,)), ((), ())), preferred_element_type=jnp.float32
-    )
+    grad_halves = exchange(grad_out, "feat", "gather", 8)
+    weight_term = jnp.concatenate([
+        lax.dot_general(summed, grad_halves[h], (((0,), (0,)), ((), ())),
+                        preferred_element_type=jnp.float32)
+        for h in range(n_feat)
+    ], axis=1)
     weight_grad = allreduce(weight_term, 4) * node_total ** (-0.5)
-    spread = lax.dot_general(
-        grad_whole, weight_rows, (((1,), (1,)), ((), ())), preferred_element_type=jnp.float32
+    weight_rows = lax.dynamic_slice_in_dim(weights, feat_index * feat_half, feat_half, 0)
+    spread = sum(
+        lax.dot_general(grad_halves[h], weight_rows[:, h * feat_half:(h + 1) * feat_half],
+                        (((1,), (1,)), ((), ())), preferred_element_type=jnp.float32)
+        for h in range(n_feat)
     ).astype(jnp.bfloat16)
     spread_panel = exchange(spread, "col", "gather", 2).reshape(-1, feat_half)
     back_partial = tile_products(local_tiles, block_rows, block_cols, count, spread_panel,

time: 220 us -> 203 us (0.923)
  waiting for transfers between devices: 17.4 us -> 0 us
  Pallas kernels: 169 us -> 185 us
  between operations: 14.8 us -> 1.47 us
  matrix products: 2.94 us -> 8.07 us
  blocking collectives: 5.09 us -> 0 us
    unnamed x2 -> x0, waiting for transfers between devices: 17.4 us -> none
    pallas_call x6 -> x8, Pallas kernels: 114 us -> 126 us  [exchange(): pl.pallas_call(functools.partial(exchange_kernel, axis, stride, size, mod...]
    dot_general x3 -> x6, matrix products: 2.94 us -> 8.07 us  [the longest x2 2.98 us: shards(): jnp.dot(agg_halves[h], weight_cols[h * feat_half:(h + 1) * feat_half], pr...]
    all_gather x1 -> x0, blocking collectives: 5.09 us -> none  [shards(): grad_whole = lax.all_gather(grad_out, 'feat', axis=1, tiled=True)]
    pallas_call x1, Pallas kernels: 40.1 us -> 43.4 us  [allreduce(): pl.pallas_call(allreduce_kernel, out_shape=jax.ShapeDtypeStruct(x.shape,...]
  transfers between devices with their start and end apart: 1 -> 0, of which waited for: 1 -> 0; matrix products, arithmetic and copies ran while one was open for 0% -> 0% of each run, Pallas kernels for 0% -> 0%
where the time goes in v8:
time: 203 us; the launch traced here: 199 us
  Pallas kernels  185 us (91%)
  matrix products  8.07 us (4%)
  other arithmetic  3.53 us (2%)
    pallas_call x8, Pallas kernels, exchange(): pl.pallas_call(functools.partial(exchange_kernel, axis, stride, size, mod...  126 us
    pallas_call x1, Pallas kernels, allreduce(): pl.pallas_call(allreduce_kernel, out_shape=jax.ShapeDtypeStruct(x.shape,...  43.4 us
    pallas_call x2, Pallas kernels, tile_products(): pl.pallas_call(functools.partial(tile_kernel, transpose), out_shape=jax.S...  15.3 us

profile of v8, /device:TPU:1, one launch (start us, length us, event | category | flops | bytes accessed | tf_op | source)
XLA Modules:
  0.0 199.2 jit_solution(555976483583524411)
XLA Ops:
  0.6 0.0 copy-start
  1.3 1.3 fusion.26.cols_ref
  2.6 33.7 %shard_map.94.x_ref = bf16[8,512,128]{2,1,0:T(8,128)(2,1)} custom-call(bf16[512,128]{1,0:T(8,128)(2,1)} %x_ref.1), custom_call_target="tpu_custom_call" | custom-call | tf_op jit(solution)/shard_map/pallas_call | solution.py:141
  36.4 6.0 %shard_map.95 = bf16[2,8,512,128]{3,2,1,0:T(8,128)(2,1)} custom-call(bf16[8,512,128]{2,1,0:T(8,128)(2,1)} %shard_map.94.x_ref), custom_call_target="tpu_custom_call" | custom-call | tf_op jit(solution)/shard_map/pallas_call | solution.py:141
  42.3 0.0 copy-start.2
  42.4 7.5 %shard_map.96 = bf16[4096,128]{1,0:T(8,128)(2,1)} custom-call(s32[256]{0:T(256)} %bitcast.38, s32[256]{0:T(256)} %fusion.26.cols_ref, s32[1]{0:T(128)} %bitcast.29.count_ref, bf16[256,128,128]{2,1,0:T(8,128)(2,1)} %bitcast.31, bf16[8192,128]{1,0:T(8,128)(2,1)} %bitcast.34), custom_call_target="tpu_custom_call" | custom-call | flops 1073741824 | bytes 11534336 | tf_op jit(solution)/shard_map/pallas_call | solution.py:60
  49.9 20.1 %shard_map.97.x_ref = bf16[512,128]{1,0:T(8,128)(2,1)} custom-call(bf16[8,512,128]{2,1,0:T(8,128)(2,1)} %bitcast.36), custom_call_target="tpu_custom_call" | custom-call | tf_op jit(solution)/shard_map/pallas_call | solution.py:141
  70.0 0.0 copy-start.1
  70.0 5.6 %shard_map.98 = bf16[2,512,128]{2,1,0:T(8,128)(2,1)} custom-call(bf16[512,128]{1,0:T(8,128)(2,1)} %shard_map.97.x_ref), custom_call_target="tpu_custom_call" | custom-call | tf_op jit(solution)/shard_map/pallas_call | solution.py:141
  75.6 1.1 fusion.12
  76.7 1.9 fusion.3
  78.6 5.4 %shard_map.99 = bf16[2,512,128]{2,1,0:T(8,128)(2,1)} custom-call(bf16[512,128]{1,0:T(8,128)(2,1)} %get-tuple-element.3.x_ref), custom_call_target="tpu_custom_call" | custom-call | tf_op jit(solution)/shard_map/pallas_call | solution.py:141
  84.1 1.1 fusion.7
  85.2 1.1 fusion.4
  86.4 0.7 pad_maximum_fusion.x_ref
  87.0 43.4 %shard_map.104 = f32[128,256]{1,0:T(8,128)} custom-call(f32[128,256]{1,0:T(8,128)} %pad_maximum_fusion.x_ref), custom_call_target="tpu_custom_call" | custom-call | tf_op jit(solution)/shard_map/pallas_call | solution.py:220
  130.5 1.6 broadcast_multiply_fusion
  132.0 1.1 fusion.9
  133.1 1.8 fusion.x_ref
  134.9 18.7 %shard_map.100 = bf16[8,512,128]{2,1,0:T(8,128)(2,1)} custom-call(bf16[512,128]{1,0:T(8,128)(2,1)} %fusion.x_ref), custom_call_target="tpu_custom_call" | custom-call | tf_op jit(solution)/shard_map/pallas_call | solution.py:141
  153.6 7.8 %shard_map.101 = bf16[8192,128]{1,0:T(8,128)(2,1)} custom-call(s32[256]{0:T(256)} %bitcast.39, s32[256]{0:T(256)} %fusion.26.cols_ref, s32[1]{0:T(128)} %bitcast.30.count_ref, bf16[256,128,128]{2,1,0:T(8,128)(2,1)} %bitcast.32, bf16[4096,128]{1,0:T(8,128)(2,1)} %bitcast.35), custom_call_target="tpu_custom_call" | custom-call | flops 1073741824 | bytes 11534336 | tf_op jit(solution)/shard_map/pallas_call | solution.py:60
  161.4 5.7 %shard_map.102 = bf16[4096,128]{1,0:T(8,128)(2,1)} custom-call(bf16[2,4096,128]{2,1,0:T(8,128)(2,1)} %bitcast.33), custom_call_target="tpu_custom_call" | custom-call | tf_op jit(solution)/shard_map/pallas_call | solution.py:141
  167.1 30.5 %shard_map.103 = bf16[512,128]{1,0:T(8,128)(2,1)} custom-call(bf16[8,512,128]{2,1,0:T(8,128)(2,1)} %bitcast.37), custom_call_target="tpu_custom_call" | custom-call | tf_op jit(solution)/shard_map/pallas_call | solution.py:141
  197.7 1.6 copy.16
  (3 shorter events, 0.0 us)
Async XLA Ops:
  0.6 75.0 %copy-start = (bf16[256,256]{1,0:T(8,128)(2,1)S(1)}, bf16[256,256]{1,0:T(8,128)(2,1)}, u32[]{:S(2)}) copy-start(bf16[256,256]{1,0:T(8,128)(2,1)} %param.12) | copy-start | bytes 393220
  42.3 34.4 %copy-start.2 = (bf16[512,128]{1,0:T(8,128)(2,1)S(1)}, bf16[512,128]{1,0:T(8,128)(2,1)}, u32[]{:S(2)}) copy-start(bf16[512,128]{1,0:T(8,128)(2,1)} %param.13) | copy-start | bytes 393220
  70.0 14.1 %copy-start.1 = (bf16[512,128]{1,0:T(8,128)(2,1)S(1)}, bf16[512,128]{1,0:T(8,128)(2,1)}, u32[]{:S(2)}) copy-start(bf16[512,128]{1,0:T(8,128)(2,1)} %shard_map.97.x_ref) | copy-start | bytes 393220

commit v9 on v8

--- a/solution.py
+++ b/solution.py
@@ -83,23 +83,27 @@
     return tuple(peer if name == axis else lax.axis_index(name) for name in ("row", "col", "feat"))
 
 
-def exchange_kernel(axis, stride, size, mode, x_ref, o_ref, *scratch):
+def group_of(axis, stride, size):
     index = lax.axis_index(axis)
     me = (index // stride) % size
     base = index - me * stride
-
-    def member(k):
-        return mesh_coords(axis, base + k * stride)
-
-    if mode == "gather":
-        recv_ref, (send_sems, recv_sems) = o_ref, scratch
-    else:
-        recv_ref, send_sems, recv_sems = scratch
+    return me, lambda k: mesh_coords(axis, base + k * stride)
+
+
+def exchange_targets(axis, stride, size):
+    me, member = group_of(axis, stride, size)
+    return [member(lax.rem(me + d, size)) for d in range(1, size)]
+
+
+def enter(targets):
     barrier = pltpu.get_barrier_semaphore()
-    for d in range(1, size):
-        pl.semaphore_signal(barrier, inc=1, device_id=member(lax.rem(me + d, size)),
-                            device_id_type=pl.DeviceIdType.MESH)
-    pl.semaphore_wait(barrier, size - 1)
+    for target in targets:
+        pl.semaphore_signal(barrier, inc=1, device_id=target, device_id_type=pl.DeviceIdType.MESH)
+    pl.semaphore_wait(barrier, len(targets))
+
+
+def exchange_start(axis, stride, size, mode, x_ref, recv_ref, send_sems, recv_sems):
+    me, member = group_of(axis, stride, size)
     copies = []
     for d in range(1, size):
         peer = lax.rem(me + d, size)
@@ -110,6 +114,11 @@
             device_id_type=pl.DeviceIdType.MESH)
         copy.start()
         copies.append(copy)
+    return copies
+
+
+def exchange_finish(axis, stride, size, mode, x_ref, o_ref, recv_ref, send_sems, recv_sems, copies):
+    me, member = group_of(axis, stride, size)
     if mode == "gather":
         o_ref[me] = x_ref[...]
     else:
@@ -129,21 +138,34 @@
         o_ref[...] = total.astype(o_ref.dtype)
 
 
+def exchange_kernel(axis, stride, size, mode, x_ref, o_ref, *scratch):
+    if mode == "gather":
+        recv_ref, (send_sems, recv_sems) = o_ref, scratch
+    else:
+        recv_ref, send_sems, recv_sems = scratch
+    enter(exchange_targets(axis, stride, size))
+    copies = exchange_start(axis, stride, size, mode, x_ref, recv_ref, send_sems, recv_sems)
+    exchange_finish(axis, stride, size, mode, x_ref, o_ref, recv_ref, send_sems, recv_sems, copies)
+
+
+def exchange_scratch(x, mode, size):
+    scratch = [] if mode == "gather" else [pltpu.VMEM(x.shape, x.dtype)]
+    return scratch + [pltpu.SemaphoreType.DMA((size,)), pltpu.SemaphoreType.DMA((size,))]
+
+
+def exchange_shape(x, mode, size):
+    shape = (size,) + x.shape if mode == "gather" else x.shape[1:]
+    return jax.ShapeDtypeStruct(shape, x.dtype)
+
+
 def exchange(x, axis, mode, collective_id, stride=1, size=None):
     size = lax.axis_size(axis) if size is None else size
-    if mode == "gather":
-        out_shape = (size,) + x.shape
-        scratch = []
-    else:
-        out_shape = x.shape[1:]
-        scratch = [pltpu.VMEM(x.shape, x.dtype)]
-    scratch += [pltpu.SemaphoreType.DMA((size,)), pltpu.SemaphoreType.DMA((size,))]
     return pl.pallas_call(
         functools.partial(exchange_kernel, axis, stride, size, mode),
-        out_shape=jax.ShapeDtypeStruct(out_shape, x.dtype),
+        out_shape=exchange_shape(x, mode, size),
         in_specs=[pl.BlockSpec(memory_space=pltpu.VMEM)],
         out_specs=pl.BlockSpec(memory_space=pltpu.VMEM),
-        scratch_shapes=scratch,
+        scratch_shapes=exchange_scratch(x, mode, size),
         compiler_params=pltpu.CompilerParams(collective_id=collective_id, has_side_effects=True),
     )(x)
 
@@ -161,21 +183,21 @@
     return halving, pairs
 
 
-def allreduce_kernel(x_ref, o_ref, recv, send_sems, recv_sems):
+def bitval(axis, bit):
+    return (lax.axis_index(axis) // bit) % 2
+
+
+def partner(axis, bit):
+    return mesh_coords(axis, lax.axis_index(axis) + bit * (1 - 2 * bitval(axis, bit)))
+
+
+def reduce_targets(rows):
+    halving, whole = reduction_plan(rows)
+    return [partner(axis, bit) for axis, bit in halving + whole]
+
+
+def reduce_rounds(x_ref, o_ref, recv, send_sems, recv_sems):
     halving, whole = reduction_plan(x_ref.shape[0])
-
-    def bitval(axis, bit):
-        return (lax.axis_index(axis) // bit) % 2
-
-    def partner(axis, bit):
-        return mesh_coords(axis, lax.axis_index(axis) + bit * (1 - 2 * bitval(axis, bit)))
-
-    barrier = pltpu.get_barrier_semaphore()
-    for axis, bit in halving + whole:
-        pl.semaphore_signal(barrier, inc=1, device_id=partner(axis, bit),
-                            device_id_type=pl.DeviceIdType.MESH)
-    pl.semaphore_wait(barrier, len(halving) + len(whole))
-
     o_ref[...] = x_ref[...]
     k = 0
 
@@ -214,21 +236,34 @@
         k += 1
 
 
-def allreduce(x, collective_id):
-    halving, whole = reduction_plan(x.shape[0])
+def reduce_scratch(w):
+    halving, whole = reduction_plan(w.shape[0])
     steps = 2 * len(halving) + len(whole)
+    return [
+        pltpu.VMEM((steps, w.shape[0] // 2) + w.shape[1:], w.dtype),
+        pltpu.SemaphoreType.DMA((steps,)),
+        pltpu.SemaphoreType.DMA((steps,)),
+    ]
+
+
+def gather_reduce_kernel(axis, x_ref, w_ref, o_ref, ow_ref, g_send, g_recv, recv, send_sems, recv_sems):
+    size = lax.axis_size(axis)
+    enter(exchange_targets(axis, 1, size) + reduce_targets(w_ref.shape[0]))
+    copies = exchange_start(axis, 1, size, "gather", x_ref, o_ref, g_send, g_recv)
+    reduce_rounds(w_ref, ow_ref, recv, send_sems, recv_sems)
+    exchange_finish(axis, 1, size, "gather", x_ref, o_ref, o_ref, g_send, g_recv, copies)
+
+
+def gather_and_reduce(x, w, axis, collective_id):
+    size = lax.axis_size(axis)
     return pl.pallas_call(
-        allreduce_kernel,
-        out_shape=jax.ShapeDtypeStruct(x.shape, x.dtype),
-        in_specs=[pl.BlockSpec(memory_space=pltpu.VMEM)],
-        out_specs=pl.BlockSpec(memory_space=pltpu.VMEM),
-        scratch_shapes=[
-            pltpu.VMEM((steps, x.shape[0] // 2) + x.shape[1:], x.dtype),
-            pltpu.SemaphoreType.DMA((steps,)),
-            pltpu.SemaphoreType.DMA((steps,)),
-        ],
+        functools.partial(gather_reduce_kernel, axis),
+        out_shape=(exchange_shape(x, "gather", size), jax.ShapeDtypeStruct(w.shape, w.dtype)),
+        in_specs=[pl.BlockSpec(memory_space=pltpu.VMEM)] * 2,
+        out_specs=(pl.BlockSpec(memory_space=pltpu.VMEM),) * 2,
+        scratch_shapes=exchange_scratch(x, "gather", size) + reduce_scratch(w),
         compiler_params=pltpu.CompilerParams(collective_id=collective_id, has_side_effects=True),
-    )(x)
+    )(x, w)
 
 
 def shards(features, tile_rows, tile_cols, tile_count, tile_values, weights, cotangent):
@@ -272,14 +307,15 @@
                         preferred_element_type=jnp.float32)
         for h in range(n_feat)
     ], axis=1)
-    weight_grad = allreduce(weight_term, 4) * node_total ** (-0.5)
     weight_rows = lax.dynamic_slice_in_dim(weights, feat_index * feat_half, feat_half, 0)
     spread = sum(
         lax.dot_general(grad_halves[h], weight_rows[:, h * feat_half:(h + 1) * feat_half],
                         (((1,), (1,)), ((), ())), preferred_element_type=jnp.float32)
         for h in range(n_feat)
     ).astype(jnp.bfloat16)
-    spread_panel = exchange(spread, "col", "gather", 2).reshape(-1, feat_half)
+    spread_panel, weight_sum = gather_and_reduce(spread, weight_term, "col", 2)
+    spread_panel = spread_panel.reshape(-1, feat_half)
+    weight_grad = weight_sum * node_total ** (-0.5)
     back_partial = tile_products(local_tiles, block_rows, block_cols, count, spread_panel,
                                  col_blocks, transpose=True)
     back_pairs = exchange(back_partial.reshape(pair, -1, feat_half), "row", "scatter", 3,

time: 203 us -> 191 us (0.941); the launches traced: 199 us -> 190 us
  Pallas kernels: 185 us -> 176 us
    pallas_call x8 -> x7, Pallas kernels: 126 us -> 107 us  [exchange(): pl.pallas_call(functools.partial(exchange_kernel, axis, stride, size, mod...]
    pallas_call x1, Pallas kernels: 43.4 us -> 51.5 us  [gather_and_reduce(): pl.pallas_call(functools.partial(gather_reduce_kernel, axis), out_shape=(...]
where the time goes in v9:
time: 191 us; the launch traced here: 190 us
  Pallas kernels  176 us (92%)
  matrix products  8.07 us (4%)
  other arithmetic  3.51 us (2%)
    pallas_call x7, Pallas kernels, exchange(): pl.pallas_call(functools.partial(exchange_kernel, axis, stride, size, mod...  107 us
    pallas_call x1, Pallas kernels, gather_and_reduce(): pl.pallas_call(functools.partial(gather_reduce_kernel, axis), out_shape=(...  51.5 us
    pallas_call x2, Pallas kernels, tile_products(): pl.pallas_call(functools.partial(tile_kernel, transpose), out_shape=jax.S...  17.2 us

profile of v9, /device:TPU:1, one launch (start us, length us, event | category | flops | bytes accessed | tf_op | source)
XLA Modules:
  0.0 190.2 jit_solution(18209075739340811241)
XLA Ops:
  0.6 0.0 copy-start
  1.3 1.3 fusion.26.cols_ref
  2.6 33.7 %shard_map.94.x_ref = bf16[8,512,128]{2,1,0:T(8,128)(2,1)} custom-call(bf16[512,128]{1,0:T(8,128)(2,1)} %x_ref.1), custom_call_target="tpu_custom_call" | custom-call | tf_op jit(solution)/shard_map/pallas_call | solution.py:163
  36.3 6.0 %shard_map.95 = bf16[2,8,512,128]{3,2,1,0:T(8,128)(2,1)} custom-call(bf16[8,512,128]{2,1,0:T(8,128)(2,1)} %shard_map.94.x_ref), custom_call_target="tpu_custom_call" | custom-call | tf_op jit(solution)/shard_map/pallas_call | solution.py:163
  42.3 0.0 copy-start.2
  42.3 8.5 %shard_map.96 = bf16[4096,128]{1,0:T(8,128)(2,1)} custom-call(s32[256]{0:T(256)} %bitcast.38, s32[256]{0:T(256)} %fusion.26.cols_ref, s32[1]{0:T(128)} %bitcast.29.count_ref, bf16[256,128,128]{2,1,0:T(8,128)(2,1)} %bitcast.31, bf16[8192,128]{1,0:T(8,128)(2,1)} %bitcast.34), custom_call_target="tpu_custom_call" | custom-call | flops 1073741824 | bytes 11534336 | tf_op jit(solution)/shard_map/pallas_call | solution.py:60
  50.8 20.2 %shard_map.97.x_ref = bf16[512,128]{1,0:T(8,128)(2,1)} custom-call(bf16[8,512,128]{2,1,0:T(8,128)(2,1)} %bitcast.35), custom_call_target="tpu_custom_call" | custom-call | tf_op jit(solution)/shard_map/pallas_call | solution.py:163
  71.0 0.0 copy-start.1
  71.0 6.4 %shard_map.98 = bf16[2,512,128]{2,1,0:T(8,128)(2,1)} custom-call(bf16[512,128]{1,0:T(8,128)(2,1)} %shard_map.97.x_ref), custom_call_target="tpu_custom_call" | custom-call | tf_op jit(solution)/shard_map/pallas_call | solution.py:163
  77.4 1.1 fusion.12
  78.5 0.0 copy-done.2
  78.5 1.9 %fusion.3 = (bf16[512,128]{1,0:T(8,128)(2,1)}, bf16[512,128]{1,0:T(8,128)(2,1)}) fusion(bf16[512,128]{1,0:T(8,128)(2,1)S(1)} %copy-done.2, f32[512,128]{1,0:T(8,128)S(1)} %fusion.12, bf16[256,256]{1,0:T(8,128)(2,1)S(1)} %copy-done, s32[]{:T(128)S(6)} %add.35, s32[]{:T(128)S(6)} %select_n.35, bf16[2,512,128]{2,1,0:T(8,128)(2,1)} %shard_map.98), kind=kOutput, calls=%fused_computation.7 | convolution fusion | flops 17367040 | bytes 819208 | tf_op jit(solution)/shard_map/dot_general | solution.py:296
  80.4 5.4 %shard_map.99 = bf16[2,512,128]{2,1,0:T(8,128)(2,1)} custom-call(bf16[512,128]{1,0:T(8,128)(2,1)} %get-tuple-element.7.x_ref), custom_call_target="tpu_custom_call" | custom-call | tf_op jit(solution)/shard_map/pallas_call | solution.py:163
  85.9 1.1 fusion.7
  87.0 1.1 fusion.4
  88.1 0.7 pad_maximum_fusion.w_ref
  88.8 1.1 fusion.9
  89.9 1.8 fusion.x_ref
  91.6 51.5 %shard_map.100 = (bf16[8,512,128]{2,1,0:T(8,128)(2,1)}, f32[128,256]{1,0:T(8,128)}) custom-call(bf16[512,128]{1,0:T(8,128)(2,1)} %fusion.x_ref, f32[128,256]{1,0:T(8,128)} %pad_maximum_fusion.w_ref), custom_call_target="tpu_custom_call" | custom-call | tf_op jit(solution)/shard_map/pallas_call | solution.py:259
  143.1 1.6 broadcast_multiply_fusion
  144.7 8.8 %shard_map.101 = bf16[8192,128]{1,0:T(8,128)(2,1)} custom-call(s32[256]{0:T(256)} %bitcast.39, s32[256]{0:T(256)} %fusion.26.cols_ref, s32[1]{0:T(128)} %bitcast.30.count_ref, bf16[256,128,128]{2,1,0:T(8,128)(2,1)} %bitcast.32, bf16[4096,128]{1,0:T(8,128)(2,1)} %bitcast.37), custom_call_target="tpu_custom_call" | custom-call | flops 1073741824 | bytes 11534336 | tf_op jit(solution)/shard_map/pallas_call | solution.py:60
  153.5 5.7 %shard_map.102 = bf16[4096,128]{1,0:T(8,128)(2,1)} custom-call(bf16[2,4096,128]{2,1,0:T(8,128)(2,1)} %bitcast.33), custom_call_target="tpu_custom_call" | custom-call | tf_op jit(solution)/shard_map/pallas_call | solution.py:163
  159.2 29.4 %shard_map.103 = bf16[512,128]{1,0:T(8,128)(2,1)} custom-call(bf16[8,512,128]{2,1,0:T(8,128)(2,1)} %bitcast.36), custom_call_target="tpu_custom_call" | custom-call | tf_op jit(solution)/shard_map/pallas_call | solution.py:163
  188.6 1.6 copy.16
  (2 shorter events, 0.0 us)
Async XLA Ops:
  0.6 76.8 %copy-start = (bf16[256,256]{1,0:T(8,128)(2,1)S(1)}, bf16[256,256]{1,0:T(8,128)(2,1)}, u32[]{:S(2)}) copy-start(bf16[256,256]{1,0:T(8,128)(2,1)} %param.12) | copy-start | bytes 393220
  42.3 36.2 %copy-start.2 = (bf16[512,128]{1,0:T(8,128)(2,1)S(1)}, bf16[512,128]{1,0:T(8,128)(2,1)}, u32[]{:S(2)}) copy-start(bf16[512,128]{1,0:T(8,128)(2,1)} %param.13) | copy-start | bytes 393220
  71.0 14.9 %copy-start.1 = (bf16[512,128]{1,0:T(8,128)(2,1)S(1)}, bf16[512,128]{1,0:T(8,128)(2,1)}, u32[]{:S(2)}) copy-start(bf16[512,128]{1,0:T(8,128)(2,1)} %shard_map.97.x_ref) | copy-start | bytes 393220

commit v10 on v9

--- a/solution.py
+++ b/solution.py
@@ -166,6 +166,123 @@
         in_specs=[pl.BlockSpec(memory_space=pltpu.VMEM)],
         out_specs=pl.BlockSpec(memory_space=pltpu.VMEM),
         scratch_shapes=exchange_scratch(x, mode, size),
+        compiler_params=pltpu.CompilerParams(collective_id=collective_id, has_side_effects=True),
+    )(x)
+
+
+def pair_targets(chips):
+    me, member = group_of("row", 2, chips)
+    _, sibling = group_of("row", 1, 2)
+    return [member(lax.rem(me + d, chips)) for d in range(1, chips)], sibling
+
+
+def row_gather_kernel(chips, x_ref, o_ref, send_sems, recv_sems, fwd_send, fwd_recv):
+    z_me, z_member = group_of("row", 2, chips)
+    c_me, core_member = group_of("row", 1, 2)
+    sibling = core_member(1 - c_me)
+    peers, _ = pair_targets(chips)
+    enter(peers + [sibling])
+    copies = []
+    for d in range(1, chips):
+        peer = lax.rem(z_me + d, chips)
+        copy = pltpu.make_async_remote_copy(
+            src_ref=x_ref, dst_ref=o_ref.at[c_me, z_me], send_sem=send_sems.at[d],
+            recv_sem=recv_sems.at[z_me], device_id=z_member(peer),
+            device_id_type=pl.DeviceIdType.MESH)
+        copy.start()
+        copies.append(copy)
+    own = pltpu.make_async_remote_copy(
+        src_ref=x_ref, dst_ref=o_ref.at[c_me, z_me], send_sem=fwd_send.at[z_me],
+        recv_sem=fwd_recv.at[z_me], device_id=sibling, device_id_type=pl.DeviceIdType.MESH)
+    own.start()
+    copies.append(own)
+    o_ref[c_me, z_me] = x_ref[...]
+    for d in range(1, chips):
+        src_dev = lax.rem(z_me + chips - d, chips)
+        incoming = pltpu.make_async_remote_copy(
+            src_ref=o_ref.at[c_me, src_dev], dst_ref=o_ref.at[c_me, src_dev],
+            send_sem=send_sems.at[d], recv_sem=recv_sems.at[src_dev],
+            device_id=z_member(src_dev), device_id_type=pl.DeviceIdType.MESH)
+        incoming.wait_recv()
+        forward = pltpu.make_async_remote_copy(
+            src_ref=o_ref.at[c_me, src_dev], dst_ref=o_ref.at[c_me, src_dev],
+            send_sem=fwd_send.at[src_dev], recv_sem=fwd_recv.at[src_dev], device_id=sibling,
+            device_id_type=pl.DeviceIdType.MESH)
+        forward.start()
+        copies.append(forward)
+    for k in range(chips):
+        incoming = pltpu.make_async_remote_copy(
+            src_ref=o_ref.at[1 - c_me, k], dst_ref=o_ref.at[1 - c_me, k],
+            send_sem=fwd_send.at[k], recv_sem=fwd_recv.at[k], device_id=sibling,
+            device_id_type=pl.DeviceIdType.MESH)
+        incoming.wait_recv()
+    for copy in copies:
+        copy.wait_send()
+
+
+def row_gather(x, chips, collective_id):
+    return pl.pallas_call(
+        functools.partial(row_gather_kernel, chips),
+        out_shape=jax.ShapeDtypeStruct((2, chips) + x.shape, x.dtype),
+        in_specs=[pl.BlockSpec(memory_space=pltpu.VMEM)],
+        out_specs=pl.BlockSpec(memory_space=pltpu.VMEM),
+        scratch_shapes=[pltpu.SemaphoreType.DMA((chips,))] * 4,
+        compiler_params=pltpu.CompilerParams(collective_id=collective_id, has_side_effects=True),
+    )(x)
+
+
+def row_scatter_kernel(chips, x_ref, o_ref, pair_recv, pair_sum, z_recv,
+                       pair_send_sems, pair_recv_sems, z_send_sems, z_recv_sems):
+    z_me, z_member = group_of("row", 2, chips)
+    c_me, core_member = group_of("row", 1, 2)
+    sibling = core_member(1 - c_me)
+    peers, _ = pair_targets(chips)
+    enter(peers + [sibling])
+    copies = []
+    for k in range(chips):
+        copy = pltpu.make_async_remote_copy(
+            src_ref=x_ref.at[1 - c_me, k], dst_ref=pair_recv.at[k], send_sem=pair_send_sems.at[k],
+            recv_sem=pair_recv_sems.at[k], device_id=sibling, device_id_type=pl.DeviceIdType.MESH)
+        copy.start()
+        copies.append(copy)
+    order = [lax.rem(z_me + d, chips) for d in range(1, chips)] + [z_me]
+    for d, k in enumerate(order, start=1):
+        incoming = pltpu.make_async_remote_copy(
+            src_ref=pair_recv.at[k], dst_ref=pair_recv.at[k], send_sem=pair_send_sems.at[k],
+            recv_sem=pair_recv_sems.at[k], device_id=sibling, device_id_type=pl.DeviceIdType.MESH)
+        incoming.wait_recv()
+        pair_sum[k] = (x_ref[c_me, k].astype(jnp.float32)
+                       + pair_recv[k].astype(jnp.float32)).astype(pair_sum.dtype)
+        if d < chips:
+            copy = pltpu.make_async_remote_copy(
+                src_ref=pair_sum.at[k], dst_ref=z_recv.at[z_me], send_sem=z_send_sems.at[d],
+                recv_sem=z_recv_sems.at[z_me], device_id=z_member(k),
+                device_id_type=pl.DeviceIdType.MESH)
+            copy.start()
+            copies.append(copy)
+    total = pair_sum[z_me].astype(jnp.float32)
+    for d in range(1, chips):
+        src_dev = lax.rem(z_me + chips - d, chips)
+        incoming = pltpu.make_async_remote_copy(
+            src_ref=z_recv.at[src_dev], dst_ref=z_recv.at[src_dev], send_sem=z_send_sems.at[d],
+            recv_sem=z_recv_sems.at[src_dev], device_id=z_member(src_dev),
+            device_id_type=pl.DeviceIdType.MESH)
+        incoming.wait_recv()
+        total = total + z_recv[src_dev].astype(jnp.float32)
+    for copy in copies:
+        copy.wait_send()
+    o_ref[...] = total.astype(o_ref.dtype)
+
+
+def row_scatter(x, chips, collective_id):
+    block = x.shape[2:]
+    return pl.pallas_call(
+        functools.partial(row_scatter_kernel, chips),
+        out_shape=jax.ShapeDtypeStruct(block, x.dtype),
+        in_specs=[pl.BlockSpec(memory_space=pltpu.VMEM)],
+        out_specs=pl.BlockSpec(memory_space=pltpu.VMEM),
+        scratch_shapes=[pltpu.VMEM((chips,) + block, x.dtype)] * 3
+        + [pltpu.SemaphoreType.DMA((chips,))] * 4,
         compiler_params=pltpu.CompilerParams(collective_id=collective_id, has_side_effects=True),
     )(x)
 
@@ -282,8 +399,10 @@
     node_total = features.shape[0] * n_rowdev * n_coldev
     pair = 2 if n_rowdev % 2 == 0 else 1
     chips = n_rowdev // pair
-    panel = exchange(features, "row", "gather", 0, stride=pair, size=chips)
-    panel = exchange(panel, "row", "gather", 5, stride=1, size=pair).reshape(-1, feat_half)
+    if pair == 2:
+        panel = row_gather(features, chips, 0).reshape(-1, feat_half)
+    else:
+        panel = exchange(features, "row", "gather", 0).reshape(-1, feat_half)
     owner = block_cols // local_blocks
     block_cols = ((owner % pair) * chips + owner // pair) * local_blocks + block_cols % local_blocks
     partial_value = tile_products(local_tiles, block_rows, block_cols, count, panel,
@@ -318,10 +437,10 @@
     weight_grad = weight_sum * node_total ** (-0.5)
     back_partial = tile_products(local_tiles, block_rows, block_cols, count, spread_panel,
                                  col_blocks, transpose=True)
-    back_pairs = exchange(back_partial.reshape(pair, -1, feat_half), "row", "scatter", 3,
-                          stride=1, size=pair)
-    back_summed = exchange(back_pairs.reshape(chips, -1, feat_half), "row", "scatter", 6,
-                           stride=pair, size=chips)
+    if pair == 2:
+        back_summed = row_scatter(back_partial.reshape(pair, chips, -1, feat_half), chips, 3)
+    else:
+        back_summed = exchange(back_partial.reshape(n_rowdev, -1, feat_half), "row", "scatter", 3)
     return (activated, back_summed, weight_grad)
 
 

time: 191 us -> 183 us (0.958)
  Pallas kernels: 176 us -> 168 us
    pallas_call x7 -> x3, Pallas kernels: 107 us -> 33.7 us  [exchange(): pl.pallas_call(functools.partial(exchange_kernel, axis, stride, size, mod...]
    pallas_call x0 -> x2, Pallas kernels: none -> 68.8 us  [the longest x1 36 us: row_gather(): pl.pallas_call(functools.partial(row_gather_kernel, chips), out_shape=jax...]
    pallas_call x2, Pallas kernels: 17.2 us -> 12.2 us  [tile_products(): pl.pallas_call(functools.partial(tile_kernel, transpose), out_shape=jax.S...]
where the time goes in v10:
time: 183 us
  Pallas kernels  168 us (92%)
  matrix products  8.07 us (4%)
  other arithmetic  3.51 us (2%)
    pallas_call x1, Pallas kernels, gather_and_reduce(): pl.pallas_call(functools.partial(gather_reduce_kernel, axis), out_shape=(...  53.3 us
    pallas_call x1, Pallas kernels, row_gather(): pl.pallas_call(functools.partial(row_gather_kernel, chips), out_shape=jax...  36 us
    pallas_call x3, Pallas kernels, exchange(): pl.pallas_call(functools.partial(exchange_kernel, axis, stride, size, mod...  33.7 us
    pallas_call x1, Pallas kernels, row_scatter(): pl.pallas_call(functools.partial(row_scatter_kernel, chips), out_shape=ja...  32.7 us
    pallas_call x2, Pallas kernels, tile_products(): pl.pallas_call(functools.partial(tile_kernel, transpose), out_shape=jax.S...  12.2 us

profile of v10, /device:TPU:1, one launch (start us, length us, event | category | flops | bytes accessed | tf_op | source)
XLA Modules:
  0.0 182.6 jit_solution(1118219026345135182)
XLA Ops:
  0.6 0.0 copy-start
  1.3 1.3 fusion.26.cols_ref
  2.6 36.0 %shard_map.94 = bf16[2,8,512,128]{3,2,1,0:T(8,128)(2,1)} custom-call(bf16[512,128]{1,0:T(8,128)(2,1)} %x_ref.1), custom_call_target="tpu_custom_call" | custom-call | tf_op jit(solution)/shard_map/pallas_call | solution.py:224
  38.6 0.0 copy-start.2
  38.6 6.0 %shard_map.95 = bf16[4096,128]{1,0:T(8,128)(2,1)} custom-call(s32[256]{0:T(256)} %bitcast.36, s32[256]{0:T(256)} %fusion.26.cols_ref, s32[1]{0:T(128)} %bitcast.28.count_ref, bf16[256,128,128]{2,1,0:T(8,128)(2,1)} %bitcast.30, bf16[8192,128]{1,0:T(8,128)(2,1)} %bitcast.33), custom_call_target="tpu_custom_call" | custom-call | flops 1073741824 | bytes 11534336 | tf_op jit(solution)/shard_map/pallas_call | solution.py:60
  44.6 22.6 %shard_map.96.x_ref = bf16[512,128]{1,0:T(8,128)(2,1)} custom-call(bf16[8,512,128]{2,1,0:T(8,128)(2,1)} %bitcast.34), custom_call_target="tpu_custom_call" | custom-call | tf_op jit(solution)/shard_map/pallas_call | solution.py:163
  67.3 0.0 copy-start.1
  67.3 5.6 %shard_map.97 = bf16[2,512,128]{2,1,0:T(8,128)(2,1)} custom-call(bf16[512,128]{1,0:T(8,128)(2,1)} %shard_map.96.x_ref), custom_call_target="tpu_custom_call" | custom-call | tf_op jit(solution)/shard_map/pallas_call | solution.py:163
  72.9 0.0 copy-done
  72.9 1.1 fusion.12
  74.0 0.0 copy-done.2
  74.0 1.9 %fusion.3 = (bf16[512,128]{1,0:T(8,128)(2,1)}, bf16[512,128]{1,0:T(8,128)(2,1)}) fusion(bf16[512,128]{1,0:T(8,128)(2,1)S(1)} %copy-done.2, f32[512,128]{1,0:T(8,128)S(1)} %fusion.12, bf16[256,256]{1,0:T(8,128)(2,1)S(1)} %copy-done, s32[]{:T(128)S(6)} %add.35, s32[]{:T(128)S(6)} %select_n.35, bf16[2,512,128]{2,1,0:T(8,128)(2,1)} %shard_map.97), kind=kOutput, calls=%fused_computation.7 | convolution fusion | flops 17367040 | bytes 819208 | tf_op jit(solution)/shard_map/dot_general | solution.py:415
  75.9 5.4 %shard_map.98 = bf16[2,512,128]{2,1,0:T(8,128)(2,1)} custom-call(bf16[512,128]{1,0:T(8,128)(2,1)} %get-tuple-element.7.x_ref), custom_call_target="tpu_custom_call" | custom-call | tf_op jit(solution)/shard_map/pallas_call | solution.py:163
  81.3 0.0 copy-done.1
  81.4 1.1 fusion.7
  82.5 1.1 fusion.4
  83.6 0.7 pad_maximum_fusion.w_ref
  84.3 1.1 fusion.9
  85.4 1.8 fusion.x_ref
  87.1 53.3 %shard_map.99 = (bf16[8,512,128]{2,1,0:T(8,128)(2,1)}, f32[128,256]{1,0:T(8,128)}) custom-call(bf16[512,128]{1,0:T(8,128)(2,1)} %fusion.x_ref, f32[128,256]{1,0:T(8,128)} %pad_maximum_fusion.w_ref), custom_call_target="tpu_custom_call" | custom-call | tf_op jit(solution)/shard_map/pallas_call | solution.py:376
  140.4 1.6 broadcast_multiply_fusion
  142.0 6.2 %shard_map.100 = bf16[8192,128]{1,0:T(8,128)(2,1)} custom-call(s32[256]{0:T(256)} %bitcast.37, s32[256]{0:T(256)} %fusion.26.cols_ref, s32[1]{0:T(128)} %bitcast.29.count_ref, bf16[256,128,128]{2,1,0:T(8,128)(2,1)} %bitcast.31, bf16[4096,128]{1,0:T(8,128)(2,1)} %bitcast.35), custom_call_target="tpu_custom_call" | custom-call | flops 1073741824 | bytes 11534336 | tf_op jit(solution)/shard_map/pallas_call | solution.py:60
  148.3 32.7 %shard_map.101 = bf16[512,128]{1,0:T(8,128)(2,1)} custom-call(bf16[2,8,512,128]{3,2,1,0:T(8,128)(2,1)} %bitcast.32), custom_call_target="tpu_custom_call" | custom-call | tf_op jit(solution)/shard_map/pallas_call | solution.py:279
  181.0 1.6 copy.16
Async XLA Ops:
  0.6 72.3 %copy-start = (bf16[256,256]{1,0:T(8,128)(2,1)S(1)}, bf16[256,256]{1,0:T(8,128)(2,1)}, u32[]{:S(2)}) copy-start(bf16[256,256]{1,0:T(8,128)(2,1)} %param.12) | copy-start | bytes 393220
  38.6 35.3 %copy-start.2 = (bf16[512,128]{1,0:T(8,128)(2,1)S(1)}, bf16[512,128]{1,0:T(8,128)(2,1)}, u32[]{:S(2)}) copy-start(bf16[512,128]{1,0:T(8,128)(2,1)} %param.13) | copy-start | bytes 393220
  67.3 14.1 %copy-start.1 = (bf16[512,128]{1,0:T(8,128)(2,1)S(1)}, bf16[512,128]{1,0:T(8,128)(2,1)}, u32[]{:S(2)}) copy-start(bf16[512,128]{1,0:T(8,128)(2,1)} %shard_map.96.x_ref) | copy-start | bytes 393220

commit v11 on v10

--- a/solution.py
+++ b/solution.py
@@ -363,6 +363,136 @@
     ]
 
 
+def radix_groups():
+    n_row, n_col = lax.axis_size("row"), lax.axis_size("col")
+    if n_row % 2 or n_col % 4:
+        return None
+    return ((("row", 1, 2), ("col", 1, 4)), ("row", 2, n_row // 2), ("col", 4, n_col // 4))
+
+
+def first_group():
+    (core, ring), _, _ = radix_groups()
+    me_a, _ = group_of(*core)
+    me_b, _ = group_of(*ring)
+    size = core[2] * ring[2]
+    me = me_a + core[2] * me_b
+    row = lax.axis_index("row") - me_a * core[1]
+    col = lax.axis_index("col") - me_b * ring[1]
+
+    def member(m):
+        return (row + (m % core[2]) * core[1], col + (m // core[2]) * ring[1], lax.axis_index("feat"))
+
+    return me, size, member
+
+
+def reduce_radix_targets():
+    me, size, member = first_group()
+    targets = [member(lax.rem(me + d, size)) for d in range(1, size)]
+    _, z_group, x_group = radix_groups()
+    return targets + exchange_targets(*z_group) + exchange_targets(*x_group)
+
+
+def ordered_allreduce(group, value, recv, send_sems, recv_sems):
+    axis, stride, size = group
+    me, member = group_of(axis, stride, size)
+    recv[me] = value
+    copies = []
+    for d in range(1, size):
+        peer = lax.rem(me + d, size)
+        copy = pltpu.make_async_remote_copy(
+            src_ref=recv.at[me], dst_ref=recv.at[me], send_sem=send_sems.at[d],
+            recv_sem=recv_sems.at[me], device_id=member(peer), device_id_type=pl.DeviceIdType.MESH)
+        copy.start()
+        copies.append(copy)
+    for d in range(1, size):
+        src_dev = lax.rem(me + size - d, size)
+        pltpu.make_async_remote_copy(
+            src_ref=recv.at[src_dev], dst_ref=recv.at[src_dev], send_sem=send_sems.at[d],
+            recv_sem=recv_sems.at[src_dev], device_id=member(src_dev),
+            device_id_type=pl.DeviceIdType.MESH).wait_recv()
+    for copy in copies:
+        copy.wait_send()
+    total = recv[0]
+    for k in range(1, size):
+        total = total + recv[k]
+    return total
+
+
+def reduce_radix(w_ref, o_ref, seg_recv, z_recv, x_recv, sems):
+    _, z_group, x_group = radix_groups()
+    me, size, member = first_group()
+    seg = w_ref.shape[0] // size
+    mine = pl.ds(pl.multiple_of(me * seg, 8), seg)
+    copies = []
+    for d in range(1, size):
+        peer = lax.rem(me + d, size)
+        copy = pltpu.make_async_remote_copy(
+            src_ref=w_ref.at[pl.ds(pl.multiple_of(peer * seg, 8), seg)], dst_ref=seg_recv.at[me],
+            send_sem=sems.at[0, d], recv_sem=sems.at[1, me], device_id=member(peer),
+            device_id_type=pl.DeviceIdType.MESH)
+        copy.start()
+        copies.append(copy)
+    total = w_ref[mine]
+    for d in range(1, size):
+        src_dev = lax.rem(me + size - d, size)
+        pltpu.make_async_remote_copy(
+            src_ref=seg_recv.at[src_dev], dst_ref=seg_recv.at[src_dev], send_sem=sems.at[0, d],
+            recv_sem=sems.at[1, src_dev], device_id=member(src_dev),
+            device_id_type=pl.DeviceIdType.MESH).wait_recv()
+        total = total + seg_recv[src_dev]
+    for copy in copies:
+        copy.wait_send()
+    total = ordered_allreduce(z_group, total, z_recv, sems.at[2], sems.at[3])
+    total = ordered_allreduce(x_group, total, x_recv, sems.at[4], sems.at[5])
+    o_ref[mine] = total
+    copies = []
+    for d in range(1, size):
+        peer = lax.rem(me + d, size)
+        copy = pltpu.make_async_remote_copy(
+            src_ref=o_ref.at[mine], dst_ref=o_ref.at[mine], send_sem=sems.at[6, d],
+            recv_sem=sems.at[7, me], device_id=member(peer), device_id_type=pl.DeviceIdType.MESH)
+        copy.start()
+        copies.append(copy)
+    for d in range(1, size):
+        src_dev = lax.rem(me + size - d, size)
+        rows = pl.ds(pl.multiple_of(src_dev * seg, 8), seg)
+        pltpu.make_async_remote_copy(
+            src_ref=o_ref.at[rows], dst_ref=o_ref.at[rows], send_sem=sems.at[6, d],
+            recv_sem=sems.at[7, src_dev], device_id=member(src_dev),
+            device_id_type=pl.DeviceIdType.MESH).wait_recv()
+    for copy in copies:
+        copy.wait_send()
+
+
+def radix_scratch(w):
+    (core, ring), z_group, x_group = radix_groups()
+    size = core[2] * ring[2]
+    seg = (w.shape[0] // size,) + w.shape[1:]
+    width = max(size, z_group[2], x_group[2])
+    return [
+        pltpu.VMEM((size,) + seg, w.dtype),
+        pltpu.VMEM((z_group[2],) + seg, w.dtype),
+        pltpu.VMEM((x_group[2],) + seg, w.dtype),
+        pltpu.SemaphoreType.DMA((8, width)),
+    ]
+
+
+def radix_fits(w):
+    groups = radix_groups()
+    if groups is None:
+        return False
+    size = groups[0][0][2] * groups[0][1][2]
+    return w.shape[0] % (8 * size) == 0
+
+
+def gather_radix_kernel(axis, x_ref, w_ref, o_ref, ow_ref, g_send, g_recv, *scratch):
+    size = lax.axis_size(axis)
+    enter(exchange_targets(axis, 1, size) + reduce_radix_targets())
+    copies = exchange_start(axis, 1, size, "gather", x_ref, o_ref, g_send, g_recv)
+    reduce_radix(w_ref, ow_ref, *scratch)
+    exchange_finish(axis, 1, size, "gather", x_ref, o_ref, o_ref, g_send, g_recv, copies)
+
+
 def gather_reduce_kernel(axis, x_ref, w_ref, o_ref, ow_ref, g_send, g_recv, recv, send_sems, recv_sems):
     size = lax.axis_size(axis)
     enter(exchange_targets(axis, 1, size) + reduce_targets(w_ref.shape[0]))
@@ -373,12 +503,16 @@
 
 def gather_and_reduce(x, w, axis, collective_id):
     size = lax.axis_size(axis)
+    if radix_fits(w):
+        kernel, scratch = gather_radix_kernel, radix_scratch(w)
+    else:
+        kernel, scratch = gather_reduce_kernel, reduce_scratch(w)
     return pl.pallas_call(
-        functools.partial(gather_reduce_kernel, axis),
+        functools.partial(kernel, axis),
         out_shape=(exchange_shape(x, "gather", size), jax.ShapeDtypeStruct(w.shape, w.dtype)),
         in_specs=[pl.BlockSpec(memory_space=pltpu.VMEM)] * 2,
         out_specs=(pl.BlockSpec(memory_space=pltpu.VMEM),) * 2,
-        scratch_shapes=exchange_scratch(x, "gather", size) + reduce_scratch(w),
+        scratch_shapes=exchange_scratch(x, "gather", size) + scratch,
         compiler_params=pltpu.CompilerParams(collective_id=collective_id, has_side_effects=True),
     )(x, w)
 

time: 183 us -> 173 us (0.945)
  Pallas kernels: 168 us -> 158 us
    pallas_call x1, Pallas kernels: 53.3 us -> 37.8 us  [gather_and_reduce(): pl.pallas_call(functools.partial(kernel, axis), out_shape=(exchange_shape...]
    pallas_call x3, Pallas kernels: 33.7 us -> 36.8 us  [exchange(): pl.pallas_call(functools.partial(exchange_kernel, axis, stride, size, mod...]
    pallas_call x1, Pallas kernels: 32.7 us -> 35.3 us  [row_scatter(): pl.pallas_call(functools.partial(row_scatter_kernel, chips), out_shape=ja...]
where the time goes in v11:
time: 173 us
  Pallas kernels  158 us (91%)
  matrix products  8.08 us (5%)
  other arithmetic  3.51 us (2%)
    pallas_call x1, Pallas kernels, gather_and_reduce(): pl.pallas_call(functools.partial(kernel, axis), out_shape=(exchange_shape...  37.8 us
    pallas_call x3, Pallas kernels, exchange(): pl.pallas_call(functools.partial(exchange_kernel, axis, stride, size, mod...  36.8 us
    pallas_call x1, Pallas kernels, row_gather(): pl.pallas_call(functools.partial(row_gather_kernel, chips), out_shape=jax...  36 us
    pallas_call x1, Pallas kernels, row_scatter(): pl.pallas_call(functools.partial(row_scatter_kernel, chips), out_shape=ja...  35.3 us
    pallas_call x2, Pallas kernels, tile_products(): pl.pallas_call(functools.partial(tile_kernel, transpose), out_shape=jax.S...  12.2 us

profile of v11, /device:TPU:1, one launch (start us, length us, event | category | flops | bytes accessed | tf_op | source)
XLA Modules:
  0.0 172.7 jit_solution(9348452811539367614)
XLA Ops:
  0.6 0.0 copy-start
  1.3 1.3 fusion.26.cols_ref
  2.6 36.0 %shard_map.94 = bf16[2,8,512,128]{3,2,1,0:T(8,128)(2,1)} custom-call(bf16[512,128]{1,0:T(8,128)(2,1)} %x_ref.1), custom_call_target="tpu_custom_call" | custom-call | tf_op jit(solution)/shard_map/pallas_call | solution.py:224
  38.6 0.0 copy-start.2
  38.6 6.0 %shard_map.95 = bf16[4096,128]{1,0:T(8,128)(2,1)} custom-call(s32[256]{0:T(256)} %bitcast.36, s32[256]{0:T(256)} %fusion.26.cols_ref, s32[1]{0:T(128)} %bitcast.28.count_ref, bf16[256,128,128]{2,1,0:T(8,128)(2,1)} %bitcast.30, bf16[8192,128]{1,0:T(8,128)(2,1)} %bitcast.33), custom_call_target="tpu_custom_call" | custom-call | flops 1073741824 | bytes 11534336 | tf_op jit(solution)/shard_map/pallas_call | solution.py:60
  44.6 23.4 %shard_map.96.x_ref = bf16[512,128]{1,0:T(8,128)(2,1)} custom-call(bf16[8,512,128]{2,1,0:T(8,128)(2,1)} %bitcast.34), custom_call_target="tpu_custom_call" | custom-call | tf_op jit(solution)/shard_map/pallas_call | solution.py:163
  68.1 0.0 copy-start.1
  68.1 7.2 %shard_map.97 = bf16[2,512,128]{2,1,0:T(8,128)(2,1)} custom-call(bf16[512,128]{1,0:T(8,128)(2,1)} %shard_map.96.x_ref), custom_call_target="tpu_custom_call" | custom-call | tf_op jit(solution)/shard_map/pallas_call | solution.py:163
  75.3 0.0 copy-done
  75.3 1.1 fusion.12
  76.4 0.0 copy-done.2
  76.4 1.9 %fusion.3 = (bf16[512,128]{1,0:T(8,128)(2,1)}, bf16[512,128]{1,0:T(8,128)(2,1)}) fusion(bf16[512,128]{1,0:T(8,128)(2,1)S(1)} %copy-done.2, f32[512,128]{1,0:T(8,128)S(1)} %fusion.12, bf16[256,256]{1,0:T(8,128)(2,1)S(1)} %copy-done, s32[]{:T(128)S(6)} %add.35, s32[]{:T(128)S(6)} %select_n.35, bf16[2,512,128]{2,1,0:T(8,128)(2,1)} %shard_map.97), kind=kOutput, calls=%fused_computation.7 | convolution fusion | flops 17367040 | bytes 819208 | tf_op jit(solution)/shard_map/dot_general | solution.py:549
  78.3 6.2 %shard_map.98 = bf16[2,512,128]{2,1,0:T(8,128)(2,1)} custom-call(bf16[512,128]{1,0:T(8,128)(2,1)} %get-tuple-element.7.x_ref), custom_call_target="tpu_custom_call" | custom-call | tf_op jit(solution)/shard_map/pallas_call | solution.py:163
  84.5 0.0 copy-done.1
  84.5 1.1 fusion.7
  85.6 1.1 fusion.4
  86.7 0.7 pad_maximum_fusion.w_ref
  87.4 1.1 fusion.9
  88.5 1.8 %fusion.x_ref = bf16[512,128]{1,0:T(8,128)(2,1)} fusion(f32[512,128]{1,0:T(8,128)S(1)} %fusion.9, bf16[2,512,128]{2,1,0:T(8,128)(2,1)} %shard_map.98, bf16[256,256]{1,0:T(8,128)(2,1)S(1)} %copy-done, s32[]{:T(128)S(6)} %select_n.35, s32[]{:T(128)S(6)} %add.35), kind=kOutput, calls=%fused_computation.2 | convolution fusion | flops 16908288 | bytes 557064 | tf_op jit(solution)/shard_map/dot_general | solution.py:565
  90.3 37.8 %shard_map.99 = (bf16[8,512,128]{2,1,0:T(8,128)(2,1)}, f32[128,256]{1,0:T(8,128)}) custom-call(bf16[512,128]{1,0:T(8,128)(2,1)} %fusion.x_ref, f32[128,256]{1,0:T(8,128)} %pad_maximum_fusion.w_ref), custom_call_target="tpu_custom_call" | custom-call | tf_op jit(solution)/shard_map/pallas_call | solution.py:510
  128.1 1.6 broadcast_multiply_fusion
  129.6 6.2 %shard_map.100 = bf16[8192,128]{1,0:T(8,128)(2,1)} custom-call(s32[256]{0:T(256)} %bitcast.37, s32[256]{0:T(256)} %fusion.26.cols_ref, s32[1]{0:T(128)} %bitcast.29.count_ref, bf16[256,128,128]{2,1,0:T(8,128)(2,1)} %bitcast.31, bf16[4096,128]{1,0:T(8,128)(2,1)} %bitcast.35), custom_call_target="tpu_custom_call" | custom-call | flops 1073741824 | bytes 11534336 | tf_op jit(solution)/shard_map/pallas_call | solution.py:60
  135.9 35.3 %shard_map.101 = bf16[512,128]{1,0:T(8,128)(2,1)} custom-call(bf16[2,8,512,128]{3,2,1,0:T(8,128)(2,1)} %bitcast.32), custom_call_target="tpu_custom_call" | custom-call | tf_op jit(solution)/shard_map/pallas_call | solution.py:279
  171.2 1.6 copy.16
Async XLA Ops:
  0.6 74.6 %copy-start = (bf16[256,256]{1,0:T(8,128)(2,1)S(1)}, bf16[256,256]{1,0:T(8,128)(2,1)}, u32[]{:S(2)}) copy-start(bf16[256,256]{1,0:T(8,128)(2,1)} %param.12) | copy-start | bytes 393220
  38.6 37.7 %copy-start.2 = (bf16[512,128]{1,0:T(8,128)(2,1)S(1)}, bf16[512,128]{1,0:T(8,128)(2,1)}, u32[]{:S(2)}) copy-start(bf16[512,128]{1,0:T(8,128)(2,1)} %param.13) | copy-start | bytes 393220
  68.1 16.4 %copy-start.1 = (bf16[512,128]{1,0:T(8,128)(2,1)S(1)}, bf16[512,128]{1,0:T(8,128)(2,1)}, u32[]{:S(2)}) copy-start(bf16[512,128]{1,0:T(8,128)(2,1)} %shard_map.96.x_ref) | copy-start | bytes 393220

commit v12 on v11

--- a/solution.py
+++ b/solution.py
@@ -285,6 +285,75 @@
         + [pltpu.SemaphoreType.DMA((chips,))] * 4,
         compiler_params=pltpu.CompilerParams(collective_id=collective_id, has_side_effects=True),
     )(x)
+
+
+def feat_push(value_ref, halves_ref, send_sems, recv_sems, slot):
+    n = lax.axis_size("feat")
+    me = lax.axis_index("feat")
+    halves_ref[me] = value_ref[...]
+    copies = []
+    for d in range(1, n):
+        peer = lax.rem(me + d, n)
+        copy = pltpu.make_async_remote_copy(
+            src_ref=halves_ref.at[me], dst_ref=halves_ref.at[me], send_sem=send_sems.at[slot, d],
+            recv_sem=recv_sems.at[slot, me], device_id=mesh_coords("feat", peer),
+            device_id_type=pl.DeviceIdType.MESH)
+        copy.start()
+        copies.append(copy)
+    for d in range(1, n):
+        src_dev = lax.rem(me + n - d, n)
+        pltpu.make_async_remote_copy(
+            src_ref=halves_ref.at[src_dev], dst_ref=halves_ref.at[src_dev],
+            send_sem=send_sems.at[slot, d], recv_sem=recv_sems.at[slot, src_dev],
+            device_id=mesh_coords("feat", src_dev), device_id_type=pl.DeviceIdType.MESH).wait_recv()
+    for copy in copies:
+        copy.wait_send()
+
+
+def layer_kernel(x_ref, w_ref, cot_ref, summed_ref, hidden_ref, grad_ref,
+                 recv_ref, send_sems, recv_sems, agg_ref, grad_out_ref, f_send, f_recv):
+    n_col = lax.axis_size("col")
+    n_feat = lax.axis_size("feat")
+    me = lax.axis_index("feat")
+    peers = [mesh_coords("feat", lax.rem(me + d, n_feat)) for d in range(1, n_feat)]
+    enter(exchange_targets("col", 1, n_col) + peers)
+    copies = exchange_start("col", 1, n_col, "scatter", x_ref, recv_ref, send_sems, recv_sems)
+    exchange_finish("col", 1, n_col, "scatter", x_ref, summed_ref, recv_ref, send_sems, recv_sems,
+                    copies)
+    feat_push(summed_ref, agg_ref, f_send, f_recv, 0)
+    half = agg_ref.shape[-1]
+    hidden = jnp.dot(agg_ref[0], w_ref[pl.ds(0, half), :], preferred_element_type=jnp.float32)
+    for h in range(1, n_feat):
+        hidden = hidden + jnp.dot(agg_ref[h], w_ref[pl.ds(h * half, half), :],
+                                  preferred_element_type=jnp.float32)
+    hidden_ref[...] = hidden
+    slope = jnp.where(hidden > 0, 1.0, jnp.exp(jnp.minimum(hidden, 0.0)))
+    grad_out_ref[...] = (cot_ref[...].astype(jnp.float32) * slope).astype(grad_out_ref.dtype)
+    feat_push(grad_out_ref, grad_ref, f_send, f_recv, 1)
+
+
+def layer_step(partials, weight_cols, cotangent, collective_id):
+    n_col = lax.axis_size("col")
+    n_feat = lax.axis_size("feat")
+    block = partials.shape[1:]
+    vmem = pl.BlockSpec(memory_space=pltpu.VMEM)
+    return pl.pallas_call(
+        layer_kernel,
+        out_shape=(
+            jax.ShapeDtypeStruct(block, partials.dtype),
+            jax.ShapeDtypeStruct(block, jnp.float32),
+            jax.ShapeDtypeStruct((n_feat,) + block, jnp.bfloat16),
+        ),
+        in_specs=[vmem] * 3,
+        out_specs=(vmem,) * 3,
+        scratch_shapes=exchange_scratch(partials, "scatter", n_col) + [
+            pltpu.VMEM((n_feat,) + block, partials.dtype),
+            pltpu.VMEM(block, jnp.bfloat16),
+            pltpu.SemaphoreType.DMA((2, n_feat)),
+            pltpu.SemaphoreType.DMA((2, n_feat)),
+        ],
+        compiler_params=pltpu.CompilerParams(collective_id=collective_id, has_side_effects=True),
+    )(partials, weight_cols, cotangent)
 
 
 def reduction_plan(rows):
@@ -541,20 +610,12 @@
     block_cols = ((owner % pair) * chips + owner // pair) * local_blocks + block_cols % local_blocks
     partial_value = tile_products(local_tiles, block_rows, block_cols, count, panel,
                                   row_blocks, transpose=False)
-    summed = exchange(partial_value.reshape(n_coldev, -1, feat_half), "col", "scatter", 1)
     n_feat = lax.axis_size("feat")
-    agg_halves = exchange(summed, "feat", "gather", 7)
     weight_cols = lax.dynamic_slice_in_dim(weights, feat_index * feat_half, feat_half, 1)
-    hidden = sum(
-        jnp.dot(agg_halves[h], weight_cols[h * feat_half:(h + 1) * feat_half],
-                preferred_element_type=jnp.float32)
-        for h in range(n_feat)
-    )
+    summed, hidden, grad_halves = layer_step(partial_value.reshape(n_coldev, -1, feat_half),
+                                             weight_cols, cotangent, 1)
     negative = jnp.minimum(hidden, 0.0)
     activated = jnp.where(hidden > 0, hidden, jnp.expm1(negative)).astype(jnp.bfloat16)
-    slope_factor = jnp.where(hidden > 0, 1.0, jnp.exp(negative))
-    grad_out = (cotangent.astype(jnp.float32) * slope_factor).astype(jnp.bfloat16)
-    grad_halves = exchange(grad_out, "feat", "gather", 8)
     weight_term = jnp.concatenate([
         lax.dot_general(summed, grad_halves[h], (((0,), (0,)), ((), ())),
                         preferred_element_type=jnp.float32)

time: 173 us -> 170 us (0.983); the launches traced: 173 us -> 167 us
  Pallas kernels: 158 us -> 153 us
  matrix products: 8.08 us -> 5.22 us
    pallas_call x3 -> x1, Pallas kernels: 36.8 us -> 29.6 us  [layer_step(): pl.pallas_call(layer_kernel, out_shape=(jax.ShapeDtypeStruct(block, parti...]
    dot_general x2 -> x0, matrix products: 2.98 us -> none  [shards(): jnp.dot(agg_halves[h], weight_cols[h * feat_half:(h + 1) * feat_half], pr...]
    pallas_call x2, Pallas kernels: 12.2 us -> 15.2 us  [tile_products(): pl.pallas_call(functools.partial(tile_kernel, transpose), out_shape=jax.S...]
    pallas_call x1, Pallas kernels: 35.3 us -> 33 us  [row_scatter(): pl.pallas_call(functools.partial(row_scatter_kernel, chips), out_shape=ja...]
where the time goes in v12:
time: 170 us; the launch traced here: 167 us
  Pallas kernels  153 us (90%)
  matrix products  5.22 us (3%)
  other arithmetic  5.16 us (3%)
  local copies, waits for them, and re-layouts  2.21 us (1%)
    pallas_call x1, Pallas kernels, gather_and_reduce(): pl.pallas_call(functools.partial(kernel, axis), out_shape=(exchange_shape...  39.5 us
    pallas_call x1, Pallas kernels, row_gather(): pl.pallas_call(functools.partial(row_gather_kernel, chips), out_shape=jax...  36 us
    pallas_call x1, Pallas kernels, row_scatter(): pl.pallas_call(functools.partial(row_scatter_kernel, chips), out_shape=ja...  33 us
    pallas_call x1, Pallas kernels, layer_step(): pl.pallas_call(layer_kernel, out_shape=(jax.ShapeDtypeStruct(block, parti...  29.6 us
    pallas_call x2, Pallas kernels, tile_products(): pl.pallas_call(functools.partial(tile_kernel, transpose), out_shape=jax.S...  15.2 us

profile of v12, /device:TPU:1, one launch (start us, length us, event | category | flops | bytes accessed | tf_op | source)
XLA Modules:
  0.0 167.3 jit_solution(5590161737041923986)
XLA Ops:
  0.6 0.0 copy-start
  1.3 1.2 fusion.17.cols_ref
  2.5 0.0 copy-done
  2.5 0.6 constant_dynamic-slice_fusion.w_ref
  3.2 36.0 %shard_map.94 = bf16[2,8,512,128]{3,2,1,0:T(8,128)(2,1)} custom-call(bf16[512,128]{1,0:T(8,128)(2,1)} %x_ref.1), custom_call_target="tpu_custom_call" | custom-call | tf_op jit(solution)/shard_map/pallas_call | solution.py:224
  39.2 7.4 %shard_map.95 = bf16[4096,128]{1,0:T(8,128)(2,1)} custom-call(s32[256]{0:T(256)} %bitcast.28, s32[256]{0:T(256)} %fusion.17.cols_ref, s32[1]{0:T(128)} %bitcast.20.count_ref, bf16[256,128,128]{2,1,0:T(8,128)(2,1)} %bitcast.22, bf16[8192,128]{1,0:T(8,128)(2,1)} %bitcast.25), custom_call_target="tpu_custom_call" | custom-call | flops 1073741824 | bytes 11534336 | tf_op jit(solution)/shard_map/pallas_call | solution.py:60
  46.6 29.6 %shard_map.96 = (bf16[512,128]{1,0:T(8,128)(2,1)}, f32[512,128]{1,0:T(8,128)}, bf16[2,512,128]{2,1,0:T(8,128)(2,1)}) custom-call(bf16[8,512,128]{2,1,0:T(8,128)(2,1)} %bitcast.26, bf16[256,128]{1,0:T(8,128)(2,1)} %constant_dynamic-slice_fusion.w_ref, bf16[512,128]{1,0:T(8,128)(2,1)} %cot_ref.1), custom_call_target="tpu_custom_call" | custom-call | tf_op jit(solution)/shard_map/pallas_call | solution.py:340
  76.2 1.7 %fusion.1 = bf16[512,128]{1,0:T(8,128)(2,1)} fusion(f32[512,128]{1,0:T(8,128)} %get-tuple-element.8), kind=kLoop, calls=%fused_computation.3 | loop fusion | flops 262144 | bytes 393216 | tf_op jit(solution)/shard_map/convert_element_type | solution.py:618
  77.9 1.2 fusion.2
  79.1 1.2 fusion.5
  80.3 0.7 pad_maximum_fusion.w_ref
  81.0 1.1 fusion.7
  82.1 1.8 %fusion.x_ref = bf16[512,128]{1,0:T(8,128)(2,1)} fusion(f32[512,128]{1,0:T(8,128)S(1)} %fusion.7, bf16[2,512,128]{2,1,0:T(8,128)(2,1)} %get-tuple-element.9, bf16[256,256]{1,0:T(8,128)(2,1)S(1)} %copy-done, s32[]{:T(128)S(6)} %select_n.31, s32[]{:T(128)S(6)} %add.31), kind=kOutput, calls=%fused_computation.1 | convolution fusion | flops 16908288 | bytes 557064 | tf_op jit(solution)/shard_map/dot_general | solution.py:626
  83.8 39.5 %shard_map.97 = (bf16[8,512,128]{2,1,0:T(8,128)(2,1)}, f32[128,256]{1,0:T(8,128)}) custom-call(bf16[512,128]{1,0:T(8,128)(2,1)} %fusion.x_ref, f32[128,256]{1,0:T(8,128)} %pad_maximum_fusion.w_ref), custom_call_target="tpu_custom_call" | custom-call | tf_op jit(solution)/shard_map/pallas_call | solution.py:579
  123.4 1.6 broadcast_multiply_fusion
  124.9 7.8 %shard_map.98 = bf16[8192,128]{1,0:T(8,128)(2,1)} custom-call(s32[256]{0:T(256)} %bitcast.29, s32[256]{0:T(256)} %fusion.17.cols_ref, s32[1]{0:T(128)} %bitcast.21.count_ref, bf16[256,128,128]{2,1,0:T(8,128)(2,1)} %bitcast.23, bf16[4096,128]{1,0:T(8,128)(2,1)} %bitcast.27), custom_call_target="tpu_custom_call" | custom-call | flops 1073741824 | bytes 11534336 | tf_op jit(solution)/shard_map/pallas_call | solution.py:60
  132.7 33.0 %shard_map.99 = bf16[512,128]{1,0:T(8,128)(2,1)} custom-call(bf16[2,8,512,128]{3,2,1,0:T(8,128)(2,1)} %bitcast.24), custom_call_target="tpu_custom_call" | custom-call | tf_op jit(solution)/shard_map/pallas_call | solution.py:279
  165.7 1.6 copy.16
Async XLA Ops:
  0.6 1.9 %copy-start = (bf16[256,256]{1,0:T(8,128)(2,1)S(1)}, bf16[256,256]{1,0:T(8,128)(2,1)}, u32[]{:S(2)}) copy-start(bf16[256,256]{1,0:T(8,128)(2,1)} %param.12) | copy-start | bytes 393220

commit v13 on v12

--- a/solution.py
+++ b/solution.py
@@ -310,8 +310,9 @@
         copy.wait_send()
 
 
-def layer_kernel(x_ref, w_ref, cot_ref, summed_ref, hidden_ref, grad_ref,
-                 recv_ref, send_sems, recv_sems, agg_ref, grad_out_ref, f_send, f_recv):
+def layer_kernel(x_ref, w_ref, wr_ref, cot_ref, hidden_ref, term_ref, spread_ref,
+                 recv_ref, send_sems, recv_sems, summed_ref, agg_ref, grad_out_ref, grad_ref,
+                 f_send, f_recv):
     n_col = lax.axis_size("col")
     n_feat = lax.axis_size("feat")
     me = lax.axis_index("feat")
@@ -330,30 +331,43 @@
     slope = jnp.where(hidden > 0, 1.0, jnp.exp(jnp.minimum(hidden, 0.0)))
     grad_out_ref[...] = (cot_ref[...].astype(jnp.float32) * slope).astype(grad_out_ref.dtype)
     feat_push(grad_out_ref, grad_ref, f_send, f_recv, 1)
-
-
-def layer_step(partials, weight_cols, cotangent, collective_id):
+    spread = None
+    for h in range(n_feat):
+        columns = pl.ds(h * half, half)
+        term_ref[:, columns] = lax.dot_general(
+            summed_ref[...], grad_ref[h], (((0,), (0,)), ((), ())),
+            preferred_element_type=jnp.float32)
+        part = lax.dot_general(grad_ref[h], wr_ref[:, columns], (((1,), (1,)), ((), ())),
+                               preferred_element_type=jnp.float32)
+        spread = part if spread is None else spread + part
+    spread_ref[...] = spread.astype(spread_ref.dtype)
+
+
+def layer_step(partials, weight_cols, weight_rows, cotangent, collective_id):
     n_col = lax.axis_size("col")
     n_feat = lax.axis_size("feat")
     block = partials.shape[1:]
+    half = block[-1]
     vmem = pl.BlockSpec(memory_space=pltpu.VMEM)
     return pl.pallas_call(
         layer_kernel,
         out_shape=(
-            jax.ShapeDtypeStruct(block, partials.dtype),
             jax.ShapeDtypeStruct(block, jnp.float32),
-            jax.ShapeDtypeStruct((n_feat,) + block, jnp.bfloat16),
+            jax.ShapeDtypeStruct((half, n_feat * half), jnp.float32),
+            jax.ShapeDtypeStruct(block, jnp.bfloat16),
         ),
-        in_specs=[vmem] * 3,
+        in_specs=[vmem] * 4,
         out_specs=(vmem,) * 3,
         scratch_shapes=exchange_scratch(partials, "scatter", n_col) + [
+            pltpu.VMEM(block, partials.dtype),
             pltpu.VMEM((n_feat,) + block, partials.dtype),
             pltpu.VMEM(block, jnp.bfloat16),
+            pltpu.VMEM((n_feat,) + block, jnp.bfloat16),
             pltpu.SemaphoreType.DMA((2, n_feat)),
             pltpu.SemaphoreType.DMA((2, n_feat)),
         ],
         compiler_params=pltpu.CompilerParams(collective_id=collective_id, has_side_effects=True),
-    )(partials, weight_cols, cotangent)
+    )(partials, weight_cols, weight_rows, cotangent)
 
 
 def reduction_plan(rows):
@@ -610,23 +624,12 @@
     block_cols = ((owner % pair) * chips + owner // pair) * local_blocks + block_cols % local_blocks
     partial_value = tile_products(local_tiles, block_rows, block_cols, count, panel,
                                   row_blocks, transpose=False)
-    n_feat = lax.axis_size("feat")
     weight_cols = lax.dynamic_slice_in_dim(weights, feat_index * feat_half, feat_half, 1)
-    summed, hidden, grad_halves = layer_step(partial_value.reshape(n_coldev, -1, feat_half),
-                                             weight_cols, cotangent, 1)
+    weight_rows = lax.dynamic_slice_in_dim(weights, feat_index * feat_half, feat_half, 0)
+    hidden, weight_term, spread = layer_step(partial_value.reshape(n_coldev, -1, feat_half),
+                                             weight_cols, weight_rows, cotangent, 1)
     negative = jnp.minimum(hidden, 0.0)
     activated = jnp.where(hidden > 0, hidden, jnp.expm1(negative)).astype(jnp.bfloat16)
-    weight_term = jnp.concatenate([
-        lax.dot_general(summed, grad_halves[h], (((0,), (0,)), ((), ())),
-                        preferred_element_type=jnp.float32)
-        for h in range(n_feat)
-    ], axis=1)
-    weight_rows = lax.dynamic_slice_in_dim(weights, feat_index * feat_half, feat_half, 0)
-    spread = sum(
-        lax.dot_general(grad_halves[h], weight_rows[:, h * feat_half:(h + 1) * feat_half],
-                        (((1,), (1,)), ((), ())), preferred_element_type=jnp.float32)
-        for h in range(n_feat)
-    ).astype(jnp.bfloat16)
     spread_panel, weight_sum = gather_and_reduce(spread, weight_term, "col", 2)
     spread_panel = spread_panel.reshape(-1, feat_half)
     weight_grad = weight_sum * node_total ** (-0.5)

time: 170 us -> 165 us (0.971); the launches traced: 167 us -> 165 us
  matrix products: 5.22 us -> 0 us
  Pallas kernels: 153 us -> 156 us
    dot_general x4 -> x0, matrix products: 5.22 us -> none  [the longest x2 2.85 us: shards(): lax.dot_general(grad_halves[h], weight_rows[:, h * feat_half:(h + 1) * fe...]
    pallas_call x2, Pallas kernels: 15.2 us -> 12.1 us  [tile_products(): pl.pallas_call(functools.partial(tile_kernel, transpose), out_shape=jax.S...]
    pallas_call x1, Pallas kernels: 33 us -> 35.8 us  [row_scatter(): pl.pallas_call(functools.partial(row_scatter_kernel, chips), out_shape=ja...]
    pallas_call x1, Pallas kernels: 39.5 us -> 41.4 us  [gather_and_reduce(): pl.pallas_call(functools.partial(kernel, axis), out_shape=(exchange_shape...]
where the time goes in v13:
time: 165 us
  Pallas kernels  156 us (95%)
  other arithmetic  4.5 us (3%)
  local copies, waits for them, and re-layouts  2.85 us (2%)
    pallas_call x1, Pallas kernels, gather_and_reduce(): pl.pallas_call(functools.partial(kernel, axis), out_shape=(exchange_shape...  41.4 us
    pallas_call x1, Pallas kernels, row_gather(): pl.pallas_call(functools.partial(row_gather_kernel, chips), out_shape=jax...  36 us
    pallas_call x1, Pallas kernels, row_scatter(): pl.pallas_call(functools.partial(row_scatter_kernel, chips), out_shape=ja...  35.8 us
    pallas_call x1, Pallas kernels, layer_step(): pl.pallas_call(layer_kernel, out_shape=(jax.ShapeDtypeStruct(block, jnp.f...  30.6 us
    pallas_call x2, Pallas kernels, tile_products(): pl.pallas_call(functools.partial(tile_kernel, transpose), out_shape=jax.S...  12.1 us

profile of v13, /device:TPU:1, one launch (start us, length us, event | category | flops | bytes accessed | tf_op | source)
XLA Modules:
  0.0 164.7 jit_solution(15762110432574386027)
XLA Ops:
  0.6 0.0 copy-start
  1.3 1.2 fusion.3.cols_ref
  2.5 0.0 copy-done
  2.5 0.6 constant_dynamic-slice_fusion.wr_ref
  3.2 0.6 constant_dynamic-slice_fusion.1.w_ref
  3.8 36.0 %shard_map.94 = bf16[2,8,512,128]{3,2,1,0:T(8,128)(2,1)} custom-call(bf16[512,128]{1,0:T(8,128)(2,1)} %x_ref.1), custom_call_target="tpu_custom_call" | custom-call | tf_op jit(solution)/shard_map/pallas_call | solution.py:224
  39.9 5.9 %shard_map.95 = bf16[4096,128]{1,0:T(8,128)(2,1)} custom-call(s32[256]{0:T(256)} %bitcast.16, s32[256]{0:T(256)} %fusion.3.cols_ref, s32[1]{0:T(128)} %bitcast.8.count_ref, bf16[256,128,128]{2,1,0:T(8,128)(2,1)} %bitcast.10, bf16[8192,128]{1,0:T(8,128)(2,1)} %bitcast.13), custom_call_target="tpu_custom_call" | custom-call | flops 1073741824 | bytes 11534336 | tf_op jit(solution)/shard_map/pallas_call | solution.py:60
  45.7 30.6 %shard_map.96 = (f32[512,128]{1,0:T(8,128)}, f32[128,256]{1,0:T(8,128)}, bf16[512,128]{1,0:T(8,128)(2,1)}) custom-call(bf16[8,512,128]{2,1,0:T(8,128)(2,1)} %bitcast.14, bf16[256,128]{1,0:T(8,128)(2,1)} %constant_dynamic-slice_fusion.1.w_ref, bf16[128,256]{1,0:T(8,128)(2,1)} %constant_dynamic-slice_fusion.wr_ref, bf16[512,128]{1,0:T(8,128)(2,1)} %cot_ref.1), custom_call_target="tpu_custom_call" | custom-call | tf_op jit(solution)/shard_map/pallas_call | solution.py:352
  76.4 1.7 %fusion = bf16[512,128]{1,0:T(8,128)(2,1)} fusion(f32[512,128]{1,0:T(8,128)} %get-tuple-element.8), kind=kLoop, calls=%fused_computation.1 | loop fusion | flops 262144 | bytes 393216 | tf_op jit(solution)/shard_map/convert_element_type | solution.py:632
  78.1 41.4 %shard_map.97 = (bf16[8,512,128]{2,1,0:T(8,128)(2,1)}, f32[128,256]{1,0:T(8,128)}) custom-call(bf16[512,128]{1,0:T(8,128)(2,1)} %get-tuple-element.9.x_ref, f32[128,256]{1,0:T(8,128)} %get-tuple-element.10.w_ref), custom_call_target="tpu_custom_call" | custom-call | tf_op jit(solution)/shard_map/pallas_call | solution.py:593
  119.5 1.6 broadcast_multiply_fusion
  121.1 6.2 %shard_map.98 = bf16[8192,128]{1,0:T(8,128)(2,1)} custom-call(s32[256]{0:T(256)} %bitcast.17, s32[256]{0:T(256)} %fusion.3.cols_ref, s32[1]{0:T(128)} %bitcast.9.count_ref, bf16[256,128,128]{2,1,0:T(8,128)(2,1)} %bitcast.11, bf16[4096,128]{1,0:T(8,128)(2,1)} %bitcast.15), custom_call_target="tpu_custom_call" | custom-call | flops 1073741824 | bytes 11534336 | tf_op jit(solution)/shard_map/pallas_call | solution.py:60
  127.3 35.8 %shard_map.99 = bf16[512,128]{1,0:T(8,128)(2,1)} custom-call(bf16[2,8,512,128]{3,2,1,0:T(8,128)(2,1)} %bitcast.12), custom_call_target="tpu_custom_call" | custom-call | tf_op jit(solution)/shard_map/pallas_call | solution.py:279
  163.1 1.6 copy.12
Async XLA Ops:
  0.6 1.9 %copy-start = (bf16[256,256]{1,0:T(8,128)(2,1)S(1)}, bf16[256,256]{1,0:T(8,128)(2,1)}, u32[]{:S(2)}) copy-start(bf16[256,256]{1,0:T(8,128)(2,1)} %param.12) | copy-start | bytes 393220

commit v14 on v13

--- a/solution.py
+++ b/solution.py
@@ -310,14 +310,16 @@
         copy.wait_send()
 
 
-def layer_kernel(x_ref, w_ref, wr_ref, cot_ref, hidden_ref, term_ref, spread_ref,
+def layer_kernel(x_ref, w_ref, wr_ref, cot_ref, hidden_ref, panel_ref, sum_ref,
                  recv_ref, send_sems, recv_sems, summed_ref, agg_ref, grad_out_ref, grad_ref,
-                 f_send, f_recv):
+                 f_send, f_recv, term_ref, spread_ref, g_send, g_recv, *reduce_scratch):
     n_col = lax.axis_size("col")
     n_feat = lax.axis_size("feat")
     me = lax.axis_index("feat")
     peers = [mesh_coords("feat", lax.rem(me + d, n_feat)) for d in range(1, n_feat)]
-    enter(exchange_targets("col", 1, n_col) + peers)
+    radix = len(reduce_scratch) == 4
+    others = reduce_radix_targets() if radix else reduce_targets(term_ref.shape[0])
+    enter(exchange_targets("col", 1, n_col) + peers + exchange_targets("col", 1, n_col) + others)
     copies = exchange_start("col", 1, n_col, "scatter", x_ref, recv_ref, send_sems, recv_sems)
     exchange_finish("col", 1, n_col, "scatter", x_ref, summed_ref, recv_ref, send_sems, recv_sems,
                     copies)
@@ -341,6 +343,13 @@
                                preferred_element_type=jnp.float32)
         spread = part if spread is None else spread + part
     spread_ref[...] = spread.astype(spread_ref.dtype)
+    copies = exchange_start("col", 1, n_col, "gather", spread_ref, panel_ref, g_send, g_recv)
+    if radix:
+        reduce_radix(term_ref, sum_ref, *reduce_scratch)
+    else:
+        reduce_rounds(term_ref, sum_ref, *reduce_scratch)
+    exchange_finish("col", 1, n_col, "gather", spread_ref, panel_ref, panel_ref, g_send, g_recv,
+                    copies)
 
 
 def layer_step(partials, weight_cols, weight_rows, cotangent, collective_id):
@@ -348,13 +357,15 @@
     n_feat = lax.axis_size("feat")
     block = partials.shape[1:]
     half = block[-1]
+    term = jax.ShapeDtypeStruct((half, n_feat * half), jnp.float32)
+    reduce_space = radix_scratch(term) if radix_fits(term) else reduce_scratch(term)
     vmem = pl.BlockSpec(memory_space=pltpu.VMEM)
     return pl.pallas_call(
         layer_kernel,
         out_shape=(
             jax.ShapeDtypeStruct(block, jnp.float32),
-            jax.ShapeDtypeStruct((half, n_feat * half), jnp.float32),
-            jax.ShapeDtypeStruct(block, jnp.bfloat16),
+            jax.ShapeDtypeStruct((n_col,) + block, jnp.bfloat16),
+            term,
         ),
         in_specs=[vmem] * 4,
         out_specs=(vmem,) * 3,
@@ -365,7 +376,11 @@
             pltpu.VMEM((n_feat,) + block, jnp.bfloat16),
             pltpu.SemaphoreType.DMA((2, n_feat)),
             pltpu.SemaphoreType.DMA((2, n_feat)),
-        ],
+            pltpu.VMEM(term.shape, term.dtype),
+            pltpu.VMEM(block, jnp.bfloat16),
+            pltpu.SemaphoreType.DMA((n_col,)),
+            pltpu.SemaphoreType.DMA((n_col,)),
+        ] + reduce_space,
         compiler_params=pltpu.CompilerParams(collective_id=collective_id, has_side_effects=True),
     )(partials, weight_cols, weight_rows, cotangent)
 
@@ -626,11 +641,10 @@
                                   row_blocks, transpose=False)
     weight_cols = lax.dynamic_slice_in_dim(weights, feat_index * feat_half, feat_half, 1)
     weight_rows = lax.dynamic_slice_in_dim(weights, feat_index * feat_half, feat_half, 0)
-    hidden, weight_term, spread = layer_step(partial_value.reshape(n_coldev, -1, feat_half),
-                                             weight_cols, weight_rows, cotangent, 1)
+    hidden, spread_panel, weight_sum = layer_step(partial_value.reshape(n_coldev, -1, feat_half),
+                                                  weight_cols, weight_rows, cotangent, 1)
     negative = jnp.minimum(hidden, 0.0)
     activated = jnp.where(hidden > 0, hidden, jnp.expm1(negative)).astype(jnp.bfloat16)
-    spread_panel, weight_sum = gather_and_reduce(spread, weight_term, "col", 2)
     spread_panel = spread_panel.reshape(-1, feat_half)
     weight_grad = weight_sum * node_total ** (-0.5)
     back_partial = tile_products(local_tiles, block_rows, block_cols, count, spread_panel,

time: 165 us -> 158 us (0.958)
  Pallas kernels: 156 us -> 149 us
    pallas_call x1 -> x0, Pallas kernels: 41.4 us -> none  [gather_and_reduce(): pl.pallas_call(functools.partial(kernel, axis), out_shape=(exchange_shape...]
    pallas_call x1, Pallas kernels: 30.6 us -> 62.2 us  [layer_step(): pl.pallas_call(layer_kernel, out_shape=(jax.ShapeDtypeStruct(block, jnp.f...]
    pallas_call x2, Pallas kernels: 12.1 us -> 17.1 us  [tile_products(): pl.pallas_call(functools.partial(tile_kernel, transpose), out_shape=jax.S...]
    pallas_call x1, Pallas kernels: 35.8 us -> 33.6 us  [row_scatter(): pl.pallas_call(functools.partial(row_scatter_kernel, chips), out_shape=ja...]
where the time goes in v14:
time: 158 us
  Pallas kernels  149 us (94%)
  other arithmetic  4.57 us (3%)
  local copies, waits for them, and re-layouts  2.85 us (2%)
    pallas_call x1, Pallas kernels, layer_step(): pl.pallas_call(layer_kernel, out_shape=(jax.ShapeDtypeStruct(block, jnp.f...  62.2 us
    pallas_call x1, Pallas kernels, row_gather(): pl.pallas_call(functools.partial(row_gather_kernel, chips), out_shape=jax...  36 us
    pallas_call x1, Pallas kernels, row_scatter(): pl.pallas_call(functools.partial(row_scatter_kernel, chips), out_shape=ja...  33.6 us
    pallas_call x2, Pallas kernels, tile_products(): pl.pallas_call(functools.partial(tile_kernel, transpose), out_shape=jax.S...  17.1 us

profile of v14, /device:TPU:1, one launch (start us, length us, event | category | flops | bytes accessed | tf_op | source)
XLA Modules:
  0.0 157.8 jit_solution(7172354348646350047)
XLA Ops:
  0.6 0.0 copy-start
  1.3 1.3 fusion.3.cols_ref
  2.6 0.0 copy-done
  2.6 0.6 constant_dynamic-slice_fusion.wr_ref
  3.3 0.6 constant_dynamic-slice_fusion.1.w_ref
  3.9 36.0 %shard_map.94 = bf16[2,8,512,128]{3,2,1,0:T(8,128)(2,1)} custom-call(bf16[512,128]{1,0:T(8,128)(2,1)} %x_ref.1), custom_call_target="tpu_custom_call" | custom-call | tf_op jit(solution)/shard_map/pallas_call | solution.py:224
  39.9 8.3 %shard_map.95 = bf16[4096,128]{1,0:T(8,128)(2,1)} custom-call(s32[256]{0:T(256)} %bitcast.16, s32[256]{0:T(256)} %fusion.3.cols_ref, s32[1]{0:T(128)} %bitcast.8.count_ref, bf16[256,128,128]{2,1,0:T(8,128)(2,1)} %bitcast.10, bf16[8192,128]{1,0:T(8,128)(2,1)} %bitcast.13), custom_call_target="tpu_custom_call" | custom-call | flops 1073741824 | bytes 11534336 | tf_op jit(solution)/shard_map/pallas_call | solution.py:60
  48.2 62.2 %shard_map.96 = (f32[512,128]{1,0:T(8,128)}, bf16[8,512,128]{2,1,0:T(8,128)(2,1)}, f32[128,256]{1,0:T(8,128)}) custom-call(bf16[8,512,128]{2,1,0:T(8,128)(2,1)} %bitcast.14, bf16[256,128]{1,0:T(8,128)(2,1)} %constant_dynamic-slice_fusion.1.w_ref, bf16[128,256]{1,0:T(8,128)(2,1)} %constant_dynamic-slice_fusion.wr_ref, bf16[512,128]{1,0:T(8,128)(2,1)} %cot_ref.1), custom_call_target="tpu_custom_call" | custom-call | tf_op jit(solution)/shard_map/pallas_call | solution.py:363
  110.5 1.7 %fusion = bf16[512,128]{1,0:T(8,128)(2,1)} fusion(f32[512,128]{1,0:T(8,128)} %get-tuple-element.6), kind=kLoop, calls=%fused_computation.1 | loop fusion | flops 262144 | bytes 393216 | tf_op jit(solution)/shard_map/convert_element_type | solution.py:647
  112.2 1.6 broadcast_multiply_fusion
  113.8 8.8 %shard_map.97 = bf16[8192,128]{1,0:T(8,128)(2,1)} custom-call(s32[256]{0:T(256)} %bitcast.17, s32[256]{0:T(256)} %fusion.3.cols_ref, s32[1]{0:T(128)} %bitcast.9.count_ref, bf16[256,128,128]{2,1,0:T(8,128)(2,1)} %bitcast.11, bf16[4096,128]{1,0:T(8,128)(2,1)} %bitcast.15), custom_call_target="tpu_custom_call" | custom-call | flops 1073741824 | bytes 11534336 | tf_op jit(solution)/shard_map/pallas_call | solution.py:60
  122.6 33.6 %shard_map.98 = bf16[512,128]{1,0:T(8,128)(2,1)} custom-call(bf16[2,8,512,128]{3,2,1,0:T(8,128)(2,1)} %bitcast.12), custom_call_target="tpu_custom_call" | custom-call | tf_op jit(solution)/shard_map/pallas_call | solution.py:279
  156.2 1.6 copy.12
Async XLA Ops:
  0.6 2.0 %copy-start = (bf16[256,256]{1,0:T(8,128)(2,1)S(1)}, bf16[256,256]{1,0:T(8,128)(2,1)}, u32[]{:S(2)}) copy-start(bf16[256,256]{1,0:T(8,128)(2,1)} %param.12) | copy-start | bytes 393220

commit v15 on v14

--- a/solution.py
+++ b/solution.py
@@ -7,7 +7,7 @@
 from jax.experimental.pallas import tpu as pltpu
 from jax.sharding import PartitionSpec as P
 
-GROUP = 64
+GROUP = 128
 
 
 def tile_kernel(transpose, rows_ref, cols_ref, count_ref, tiles_ref, panel_ref, out_ref, acc_ref):

time: 158 us -> 156 us (0.987)
  Pallas kernels: 149 us -> 147 us
    pallas_call x2, Pallas kernels: 17.1 us -> 12.9 us  [tile_products(): pl.pallas_call(functools.partial(tile_kernel, transpose), out_shape=jax.S...]
    pallas_call x1, Pallas kernels: 62.2 us -> 64.1 us  [layer_step(): pl.pallas_call(layer_kernel, out_shape=(jax.ShapeDtypeStruct(block, jnp.f...]
where the time goes in v15:
time: 156 us
  Pallas kernels  147 us (94%)
  other arithmetic  4.57 us (3%)
  local copies, waits for them, and re-layouts  2.85 us (2%)
    pallas_call x1, Pallas kernels, layer_step(): pl.pallas_call(layer_kernel, out_shape=(jax.ShapeDtypeStruct(block, jnp.f...  64.1 us
    pallas_call x1, Pallas kernels, row_gather(): pl.pallas_call(functools.partial(row_gather_kernel, chips), out_shape=jax...  36 us
    pallas_call x1, Pallas kernels, row_scatter(): pl.pallas_call(functools.partial(row_scatter_kernel, chips), out_shape=ja...  34.3 us
    pallas_call x2, Pallas kernels, tile_products(): pl.pallas_call(functools.partial(tile_kernel, transpose), out_shape=jax.S...  12.9 us

profile of v15, /device:TPU:1, one launch (start us, length us, event | category | flops | bytes accessed | tf_op | source)
XLA Modules:
  0.0 156.2 jit_solution(4799254692406727563)
XLA Ops:
  0.6 0.0 copy-start
  1.3 1.3 fusion.3.cols_ref
  2.6 0.0 copy-done
  2.6 0.6 constant_dynamic-slice_fusion.wr_ref
  3.3 0.6 constant_dynamic-slice_fusion.1.w_ref
  3.9 36.0 %shard_map.94 = bf16[2,8,512,128]{3,2,1,0:T(8,128)(2,1)} custom-call(bf16[512,128]{1,0:T(8,128)(2,1)} %x_ref.1), custom_call_target="tpu_custom_call" | custom-call | tf_op jit(solution)/shard_map/pallas_call | solution.py:224
  39.9 6.3 %shard_map.95 = bf16[4096,128]{1,0:T(8,128)(2,1)} custom-call(s32[256]{0:T(256)} %bitcast.16, s32[256]{0:T(256)} %fusion.3.cols_ref, s32[1]{0:T(128)} %bitcast.8.count_ref, bf16[256,128,128]{2,1,0:T(8,128)(2,1)} %bitcast.10, bf16[8192,128]{1,0:T(8,128)(2,1)} %bitcast.13), custom_call_target="tpu_custom_call" | custom-call | flops 1073741824 | bytes 11534336 | tf_op jit(solution)/shard_map/pallas_call | solution.py:60
  46.2 64.1 %shard_map.96 = (f32[512,128]{1,0:T(8,128)}, bf16[8,512,128]{2,1,0:T(8,128)(2,1)}, f32[128,256]{1,0:T(8,128)}) custom-call(bf16[8,512,128]{2,1,0:T(8,128)(2,1)} %bitcast.14, bf16[256,128]{1,0:T(8,128)(2,1)} %constant_dynamic-slice_fusion.1.w_ref, bf16[128,256]{1,0:T(8,128)(2,1)} %constant_dynamic-slice_fusion.wr_ref, bf16[512,128]{1,0:T(8,128)(2,1)} %cot_ref.1), custom_call_target="tpu_custom_call" | custom-call | tf_op jit(solution)/shard_map/pallas_call | solution.py:363
  110.4 1.7 %fusion = bf16[512,128]{1,0:T(8,128)(2,1)} fusion(f32[512,128]{1,0:T(8,128)} %get-tuple-element.6), kind=kLoop, calls=%fused_computation.1 | loop fusion | flops 262144 | bytes 393216 | tf_op jit(solution)/shard_map/convert_element_type | solution.py:647
  112.1 1.6 %broadcast_multiply_fusion = f32[128,256]{1,0:T(8,128)} fusion(f32[128,256]{1,0:T(8,128)} %get-tuple-element.8), kind=kLoop, calls=%fused_computation.2 | loop fusion | flops 32768 | bytes 262144 | tf_op jit(solution)/shard_map/mul | solution.py:649
  113.6 6.6 %shard_map.97 = bf16[8192,128]{1,0:T(8,128)(2,1)} custom-call(s32[256]{0:T(256)} %bitcast.17, s32[256]{0:T(256)} %fusion.3.cols_ref, s32[1]{0:T(128)} %bitcast.9.count_ref, bf16[256,128,128]{2,1,0:T(8,128)(2,1)} %bitcast.11, bf16[4096,128]{1,0:T(8,128)(2,1)} %bitcast.15), custom_call_target="tpu_custom_call" | custom-call | flops 1073741824 | bytes 11534336 | tf_op jit(solution)/shard_map/pallas_call | solution.py:60
  120.3 34.3 %shard_map.98 = bf16[512,128]{1,0:T(8,128)(2,1)} custom-call(bf16[2,8,512,128]{3,2,1,0:T(8,128)(2,1)} %bitcast.12), custom_call_target="tpu_custom_call" | custom-call | tf_op jit(solution)/shard_map/pallas_call | solution.py:279
  154.6 1.6 %copy.12 = bf16[512,128]{1,0:T(8,128)(2,1)} copy(bf16[512,128]{1,0:T(8,128)(2,1)} %shard_map.98) | data formatting | bytes 262144
Async XLA Ops:
  0.6 2.0 %copy-start = (bf16[256,256]{1,0:T(8,128)(2,1)S(1)}, bf16[256,256]{1,0:T(8,128)(2,1)}, u32[]{:S(2)}) copy-start(bf16[256,256]{1,0:T(8,128)(2,1)} %param.12) | copy-start | bytes 393220

commit v16 on v14

--- a/solution.py
+++ b/solution.py
@@ -10,7 +10,7 @@
 GROUP = 64
 
 
-def tile_kernel(transpose, rows_ref, cols_ref, count_ref, tiles_ref, panel_ref, out_ref, acc_ref):
+def tile_kernel(transpose, remap, rows_ref, cols_ref, count_ref, tiles_ref, panel_ref, out_ref, acc_ref):
     step = pl.program_id(0)
     width = tiles_ref.shape[-1]
     count = count_ref[0]
@@ -26,7 +26,7 @@
         terms = []
         for j in range(GROUP):
             slot = step * GROUP + j
-            src = rows_ref[slot] if transpose else cols_ref[slot]
+            src = rows_ref[slot] if transpose else remap(cols_ref[slot])
             src = jnp.minimum(jnp.maximum(src, 0), src_blocks - 1)
             block = panel_ref[pl.ds(pl.multiple_of(src * width, width), width), :]
             tile = tiles_ref[j]
@@ -38,7 +38,7 @@
             terms.append(jnp.where(slot < count, term, 0.0))
         for j in range(GROUP):
             slot = step * GROUP + j
-            dst = cols_ref[slot] if transpose else rows_ref[slot]
+            dst = remap(cols_ref[slot]) if transpose else rows_ref[slot]
             dst = jnp.minimum(jnp.maximum(dst, 0), dst_blocks - 1)
             rows = pl.ds(pl.multiple_of(dst * width, width), width)
             acc_ref[rows, :] += terms[j]
@@ -48,7 +48,7 @@
         out_ref[...] = acc_ref[...].astype(out_ref.dtype)
 
 
-def tile_products(tiles, rows, cols, count, panel, out_blocks, transpose):
+def tile_products(tiles, rows, cols, count, panel, out_blocks, transpose, remap):
     slots, width, _ = tiles.shape
     feat = panel.shape[1]
     steps = slots // GROUP
@@ -58,7 +58,7 @@
         return (jnp.minimum(i, last), 0, 0)
 
     return pl.pallas_call(
-        functools.partial(tile_kernel, transpose),
+        functools.partial(tile_kernel, transpose, remap),
         out_shape=jax.ShapeDtypeStruct((out_blocks * width, feat), jnp.bfloat16),
         grid_spec=pltpu.PrefetchScalarGridSpec(
             num_scalar_prefetch=3,
@@ -329,7 +329,9 @@
     for h in range(1, n_feat):
         hidden = hidden + jnp.dot(agg_ref[h], w_ref[pl.ds(h * half, half), :],
                                   preferred_element_type=jnp.float32)
-    hidden_ref[...] = hidden
+    negative = jnp.minimum(hidden, 0.0)
+    below = jnp.tanh(negative * 0.5) * (jnp.exp(negative) + 1.0)
+    hidden_ref[...] = jnp.where(hidden > 0, hidden, below).astype(hidden_ref.dtype)
     slope = jnp.where(hidden > 0, 1.0, jnp.exp(jnp.minimum(hidden, 0.0)))
     grad_out_ref[...] = (cot_ref[...].astype(jnp.float32) * slope).astype(grad_out_ref.dtype)
     feat_push(grad_out_ref, grad_ref, f_send, f_recv, 1)
@@ -363,7 +365,7 @@
     return pl.pallas_call(
         layer_kernel,
         out_shape=(
-            jax.ShapeDtypeStruct(block, jnp.float32),
+            jax.ShapeDtypeStruct(block, jnp.bfloat16),
             jax.ShapeDtypeStruct((n_col,) + block, jnp.bfloat16),
             term,
         ),
@@ -635,20 +637,21 @@
         panel = row_gather(features, chips, 0).reshape(-1, feat_half)
     else:
         panel = exchange(features, "row", "gather", 0).reshape(-1, feat_half)
-    owner = block_cols // local_blocks
-    block_cols = ((owner % pair) * chips + owner // pair) * local_blocks + block_cols % local_blocks
+
+    def remap(col):
+        owner = col // local_blocks
+        return ((owner % pair) * chips + owner // pair) * local_blocks + col % local_blocks
+
     partial_value = tile_products(local_tiles, block_rows, block_cols, count, panel,
-                                  row_blocks, transpose=False)
+                                  row_blocks, transpose=False, remap=remap)
     weight_cols = lax.dynamic_slice_in_dim(weights, feat_index * feat_half, feat_half, 1)
     weight_rows = lax.dynamic_slice_in_dim(weights, feat_index * feat_half, feat_half, 0)
-    hidden, spread_panel, weight_sum = layer_step(partial_value.reshape(n_coldev, -1, feat_half),
+    activated, spread_panel, weight_sum = layer_step(partial_value.reshape(n_coldev, -1, feat_half),
                                                   weight_cols, weight_rows, cotangent, 1)
-    negative = jnp.minimum(hidden, 0.0)
-    activated = jnp.where(hidden > 0, hidden, jnp.expm1(negative)).astype(jnp.bfloat16)
     spread_panel = spread_panel.reshape(-1, feat_half)
     weight_grad = weight_sum * node_total ** (-0.5)
     back_partial = tile_products(local_tiles, block_rows, block_cols, count, spread_panel,
-                                 col_blocks, transpose=True)
+                                 col_blocks, transpose=True, remap=remap)
     if pair == 2:
         back_summed = row_scatter(back_partial.reshape(pair, chips, -1, feat_half), chips, 3)
     else:

time: 158 us -> 161 us (1.019)
  Pallas kernels: 149 us -> 154 us
  other arithmetic: 4.57 us -> 1.57 us
    pallas_call x3, Pallas kernels: 79.4 us -> 83.8 us  [the longest x1 64.1 us: layer_step(): pl.pallas_call(layer_kernel, out_shape=(jax.ShapeDtypeStruct(block, jnp.b...]
    convert_element_type x1 -> x0, other arithmetic: 1.71 us -> none  [shards(): jnp.where(hidden > 0, hidden, jnp.expm1(negative)).astype(jnp.bfloat16)]
where the time goes in v16:
time: 161 us
  Pallas kernels  154 us (96%)
  local copies, waits for them, and re-layouts  3.73 us (2%)
    pallas_call x1, Pallas kernels, layer_step(): pl.pallas_call(layer_kernel, out_shape=(jax.ShapeDtypeStruct(block, jnp.b...  64.1 us
    pallas_call x1, Pallas kernels, row_gather(): pl.pallas_call(functools.partial(row_gather_kernel, chips), out_shape=jax...  36 us
    pallas_call x1, Pallas kernels, row_scatter(): pl.pallas_call(functools.partial(row_scatter_kernel, chips), out_shape=ja...  34.6 us
    pallas_call x2, Pallas kernels, tile_products(): pl.pallas_call(functools.partial(tile_kernel, transpose, remap), out_shap...  19.7 us

profile of v16, /device:TPU:1, one launch (start us, length us, event | category | flops | bytes accessed | tf_op | source)
XLA Modules:
  0.0 161.0 jit_solution(11918588821899806024)
XLA Ops:
  0.6 0.0 copy-start
  1.3 0.2 copy-done
  1.6 0.6 constant_dynamic-slice_fusion.wr_ref
  2.2 0.6 constant_dynamic-slice_fusion.1.w_ref
  2.8 36.0 %shard_map.94 = bf16[2,8,512,128]{3,2,1,0:T(8,128)(2,1)} custom-call(bf16[512,128]{1,0:T(8,128)(2,1)} %x_ref.1), custom_call_target="tpu_custom_call" | custom-call | tf_op jit(solution)/shard_map/pallas_call | solution.py:224
  38.9 9.7 %shard_map.95 = bf16[4096,128]{1,0:T(8,128)(2,1)} custom-call(s32[256]{0:T(256)} %bitcast.16, s32[256]{0:T(256)} %bitcast.18, s32[1]{0:T(128)} %bitcast.8.count_ref, bf16[256,128,128]{2,1,0:T(8,128)(2,1)} %bitcast.10, bf16[8192,128]{1,0:T(8,128)(2,1)} %bitcast.13), custom_call_target="tpu_custom_call" | custom-call | flops 1073741824 | bytes 11534336 | tf_op jit(solution)/shard_map/pallas_call | solution.py:60
  48.6 64.1 %shard_map.96 = (bf16[512,128]{1,0:T(8,128)(2,1)}, bf16[8,512,128]{2,1,0:T(8,128)(2,1)}, f32[128,256]{1,0:T(8,128)}) custom-call(bf16[8,512,128]{2,1,0:T(8,128)(2,1)} %bitcast.14, bf16[256,128]{1,0:T(8,128)(2,1)} %constant_dynamic-slice_fusion.1.w_ref, bf16[128,256]{1,0:T(8,128)(2,1)} %constant_dynamic-slice_fusion.wr_ref, bf16[512,128]{1,0:T(8,128)(2,1)} %cot_ref.1), custom_call_target="tpu_custom_call" | custom-call | tf_op jit(solution)/shard_map/pallas_call | solution.py:365
  112.7 1.6 broadcast_multiply_fusion
  114.3 9.9 %shard_map.97 = bf16[8192,128]{1,0:T(8,128)(2,1)} custom-call(s32[256]{0:T(256)} %bitcast.17, s32[256]{0:T(256)} %bitcast.19, s32[1]{0:T(128)} %bitcast.9.count_ref, bf16[256,128,128]{2,1,0:T(8,128)(2,1)} %bitcast.11, bf16[4096,128]{1,0:T(8,128)(2,1)} %bitcast.15), custom_call_target="tpu_custom_call" | custom-call | flops 1073741824 | bytes 11534336 | tf_op jit(solution)/shard_map/pallas_call | solution.py:60
  124.2 0.0 copy-start.1
  124.2 34.6 %shard_map.98 = bf16[512,128]{1,0:T(8,128)(2,1)} custom-call(bf16[2,8,512,128]{3,2,1,0:T(8,128)(2,1)} %bitcast.12), custom_call_target="tpu_custom_call" | custom-call | tf_op jit(solution)/shard_map/pallas_call | solution.py:279
  158.8 0.0 copy-done.1
  158.8 0.7 copy.13
  159.5 1.6 copy.14
Async XLA Ops:
  0.6 0.9 copy-start
  124.2 34.6 %copy-start.1 = (bf16[512,128]{1,0:T(8,128)(2,1)S(1)}, bf16[512,128]{1,0:T(8,128)(2,1)}, u32[]{:S(2)}) copy-start(bf16[512,128]{1,0:T(8,128)(2,1)} %get-tuple-element.12) | copy-start | bytes 393220

commit v17 on v16

--- a/solution.py
+++ b/solution.py
@@ -329,9 +329,7 @@
     for h in range(1, n_feat):
         hidden = hidden + jnp.dot(agg_ref[h], w_ref[pl.ds(h * half, half), :],
                                   preferred_element_type=jnp.float32)
-    negative = jnp.minimum(hidden, 0.0)
-    below = jnp.tanh(negative * 0.5) * (jnp.exp(negative) + 1.0)
-    hidden_ref[...] = jnp.where(hidden > 0, hidden, below).astype(hidden_ref.dtype)
+    hidden_ref[...] = hidden
     slope = jnp.where(hidden > 0, 1.0, jnp.exp(jnp.minimum(hidden, 0.0)))
     grad_out_ref[...] = (cot_ref[...].astype(jnp.float32) * slope).astype(grad_out_ref.dtype)
     feat_push(grad_out_ref, grad_ref, f_send, f_recv, 1)
@@ -365,7 +363,7 @@
     return pl.pallas_call(
         layer_kernel,
         out_shape=(
-            jax.ShapeDtypeStruct(block, jnp.bfloat16),
+            jax.ShapeDtypeStruct(block, jnp.float32),
             jax.ShapeDtypeStruct((n_col,) + block, jnp.bfloat16),
             term,
         ),
@@ -646,8 +644,10 @@
                                   row_blocks, transpose=False, remap=remap)
     weight_cols = lax.dynamic_slice_in_dim(weights, feat_index * feat_half, feat_half, 1)
     weight_rows = lax.dynamic_slice_in_dim(weights, feat_index * feat_half, feat_half, 0)
-    activated, spread_panel, weight_sum = layer_step(partial_value.reshape(n_coldev, -1, feat_half),
+    hidden, spread_panel, weight_sum = layer_step(partial_value.reshape(n_coldev, -1, feat_half),
                                                   weight_cols, weight_rows, cotangent, 1)
+    negative = jnp.minimum(hidden, 0.0)
+    activated = jnp.where(hidden > 0, hidden, jnp.expm1(negative)).astype(jnp.bfloat16)
     spread_panel = spread_panel.reshape(-1, feat_half)
     weight_grad = weight_sum * node_total ** (-0.5)
     back_partial = tile_products(local_tiles, block_rows, block_cols, count, spread_panel,

time: 161 us -> 158 us (0.981)
  the two profiles are of different devices: /device:TPU:1 before, /device:TPU:6 now
where the time goes in v17:
time: 158 us; the launch traced here: 157 us
  Pallas kernels  150 us (95%)
  other arithmetic  3.28 us (2%)
  local copies, waits for them, and re-layouts  3.07 us (2%)
    pallas_call x1, Pallas kernels, layer_step(): pl.pallas_call(layer_kernel, out_shape=(jax.ShapeDtypeStruct(block, jnp.f...  64.7 us
    pallas_call x1, Pallas kernels, row_scatter(): pl.pallas_call(functools.partial(row_scatter_kernel, chips), out_shape=ja...  36.4 us
    pallas_call x1, Pallas kernels, row_gather(): pl.pallas_call(functools.partial(row_gather_kernel, chips), out_shape=jax...  34.6 us
    pallas_call x2, Pallas kernels, tile_products(): pl.pallas_call(functools.partial(tile_kernel, transpose, remap), out_shap...  13.9 us

profile of v17, /device:TPU:6, one launch (start us, length us, event | category | flops | bytes accessed | tf_op | source)
XLA Modules:
  0.0 157.4 jit_solution(16701933586459093209)
XLA Ops:
  0.6 0.0 copy-start
  1.3 0.2 copy-done
  1.6 0.6 constant_dynamic-slice_fusion.wr_ref
  2.2 0.6 constant_dynamic-slice_fusion.1.w_ref
  2.8 34.6 %shard_map.94 = bf16[2,8,512,128]{3,2,1,0:T(8,128)(2,1)} custom-call(bf16[512,128]{1,0:T(8,128)(2,1)} %x_ref.1), custom_call_target="tpu_custom_call" | custom-call | tf_op jit(solution)/shard_map/pallas_call | solution.py:224
  37.5 6.9 %shard_map.95 = bf16[4096,128]{1,0:T(8,128)(2,1)} custom-call(s32[256]{0:T(256)} %bitcast.16, s32[256]{0:T(256)} %bitcast.18, s32[1]{0:T(128)} %bitcast.8.count_ref, bf16[256,128,128]{2,1,0:T(8,128)(2,1)} %bitcast.10, bf16[8192,128]{1,0:T(8,128)(2,1)} %bitcast.13), custom_call_target="tpu_custom_call" | custom-call | flops 1073741824 | bytes 11534336 | tf_op jit(solution)/shard_map/pallas_call | solution.py:60
  44.3 64.7 %shard_map.96 = (f32[512,128]{1,0:T(8,128)}, bf16[8,512,128]{2,1,0:T(8,128)(2,1)}, f32[128,256]{1,0:T(8,128)}) custom-call(bf16[8,512,128]{2,1,0:T(8,128)(2,1)} %bitcast.14, bf16[256,128]{1,0:T(8,128)(2,1)} %constant_dynamic-slice_fusion.1.w_ref, bf16[128,256]{1,0:T(8,128)(2,1)} %constant_dynamic-slice_fusion.wr_ref, bf16[512,128]{1,0:T(8,128)(2,1)} %cot_ref.1), custom_call_target="tpu_custom_call" | custom-call | tf_op jit(solution)/shard_map/pallas_call | solution.py:363
  109.0 1.7 %fusion = bf16[512,128]{1,0:T(8,128)(2,1)} fusion(f32[512,128]{1,0:T(8,128)} %get-tuple-element.6), kind=kLoop, calls=%fused_computation.1 | loop fusion | flops 262144 | bytes 393216 | tf_op jit(solution)/shard_map/convert_element_type | solution.py:650
  110.7 1.6 broadcast_multiply_fusion
  112.3 7.1 %shard_map.97 = bf16[8192,128]{1,0:T(8,128)(2,1)} custom-call(s32[256]{0:T(256)} %bitcast.17, s32[256]{0:T(256)} %bitcast.19, s32[1]{0:T(128)} %bitcast.9.count_ref, bf16[256,128,128]{2,1,0:T(8,128)(2,1)} %bitcast.11, bf16[4096,128]{1,0:T(8,128)(2,1)} %bitcast.15), custom_call_target="tpu_custom_call" | custom-call | flops 1073741824 | bytes 11534336 | tf_op jit(solution)/shard_map/pallas_call | solution.py:60
  119.4 36.4 %shard_map.98 = bf16[512,128]{1,0:T(8,128)(2,1)} custom-call(bf16[2,8,512,128]{3,2,1,0:T(8,128)(2,1)} %bitcast.12), custom_call_target="tpu_custom_call" | custom-call | tf_op jit(solution)/shard_map/pallas_call | solution.py:279
  155.8 1.6 copy.12
Async XLA Ops:
  0.6 0.9 copy-start

commit v18 on v14

--- a/solution.py
+++ b/solution.py
@@ -176,6 +176,10 @@
     return [member(lax.rem(me + d, chips)) for d in range(1, chips)], sibling
 
 
+def far_first(size):
+    return sorted(range(1, size), key=lambda d: -min(d, size - d))
+
+
 def row_gather_kernel(chips, x_ref, o_ref, send_sems, recv_sems, fwd_send, fwd_recv):
     z_me, z_member = group_of("row", 2, chips)
     c_me, core_member = group_of("row", 1, 2)
@@ -183,7 +187,7 @@
     peers, _ = pair_targets(chips)
     enter(peers + [sibling])
     copies = []
-    for d in range(1, chips):
+    for d in far_first(chips):
         peer = lax.rem(z_me + d, chips)
         copy = pltpu.make_async_remote_copy(
             src_ref=x_ref, dst_ref=o_ref.at[c_me, z_me], send_sem=send_sems.at[d],
@@ -245,8 +249,9 @@
             recv_sem=pair_recv_sems.at[k], device_id=sibling, device_id_type=pl.DeviceIdType.MESH)
         copy.start()
         copies.append(copy)
-    order = [lax.rem(z_me + d, chips) for d in range(1, chips)] + [z_me]
-    for d, k in enumerate(order, start=1):
+    offsets = far_first(chips)
+    order = [lax.rem(z_me + d, chips) for d in offsets] + [z_me]
+    for d, k in zip(offsets + [chips], order):
         incoming = pltpu.make_async_remote_copy(
             src_ref=pair_recv.at[k], dst_ref=pair_recv.at[k], send_sem=pair_send_sems.at[k],
             recv_sem=pair_recv_sems.at[k], device_id=sibling, device_id_type=pl.DeviceIdType.MESH)

time: 158 us -> 157 us (level)
    pallas_call x2, Pallas kernels: 17.1 us -> 15.2 us  [tile_products(): pl.pallas_call(functools.partial(tile_kernel, transpose), out_shape=jax.S...]
where the time goes in v18:
time: 157 us; the launch traced here: 156 us
  Pallas kernels  148 us (94%)
  other arithmetic  4.57 us (3%)
  local copies, waits for them, and re-layouts  2.85 us (2%)
    pallas_call x1, Pallas kernels, layer_step(): pl.pallas_call(layer_kernel, out_shape=(jax.ShapeDtypeStruct(block, jnp.f...  63.5 us
    pallas_call x1, Pallas kernels, row_gather(): pl.pallas_call(functools.partial(row_gather_kernel, chips), out_shape=jax...  36.7 us
    pallas_call x1, Pallas kernels, row_scatter(): pl.pallas_call(functools.partial(row_scatter_kernel, chips), out_shape=ja...  32.4 us
    pallas_call x2, Pallas kernels, tile_products(): pl.pallas_call(functools.partial(tile_kernel, transpose), out_shape=jax.S...  15.2 us

profile of v18, /device:TPU:1, one launch (start us, length us, event | category | flops | bytes accessed | tf_op | source)
XLA Modules:
  0.0 156.5 jit_solution(4193555368484632158)
XLA Ops:
  0.6 0.0 copy-start
  1.3 1.3 fusion.3.cols_ref
  2.6 0.0 copy-done
  2.6 0.6 constant_dynamic-slice_fusion.wr_ref
  3.3 0.6 constant_dynamic-slice_fusion.1.w_ref
  3.9 36.7 %shard_map.94 = bf16[2,8,512,128]{3,2,1,0:T(8,128)(2,1)} custom-call(bf16[512,128]{1,0:T(8,128)(2,1)} %x_ref.1), custom_call_target="tpu_custom_call" | custom-call | tf_op jit(solution)/shard_map/pallas_call | solution.py:228
  40.6 7.4 %shard_map.95 = bf16[4096,128]{1,0:T(8,128)(2,1)} custom-call(s32[256]{0:T(256)} %bitcast.16, s32[256]{0:T(256)} %fusion.3.cols_ref, s32[1]{0:T(128)} %bitcast.8.count_ref, bf16[256,128,128]{2,1,0:T(8,128)(2,1)} %bitcast.10, bf16[8192,128]{1,0:T(8,128)(2,1)} %bitcast.13), custom_call_target="tpu_custom_call" | custom-call | flops 1073741824 | bytes 11534336 | tf_op jit(solution)/shard_map/pallas_call | solution.py:60
  47.9 63.5 %shard_map.96 = (f32[512,128]{1,0:T(8,128)}, bf16[8,512,128]{2,1,0:T(8,128)(2,1)}, f32[128,256]{1,0:T(8,128)}) custom-call(bf16[8,512,128]{2,1,0:T(8,128)(2,1)} %bitcast.14, bf16[256,128]{1,0:T(8,128)(2,1)} %constant_dynamic-slice_fusion.1.w_ref, bf16[128,256]{1,0:T(8,128)(2,1)} %constant_dynamic-slice_fusion.wr_ref, bf16[512,128]{1,0:T(8,128)(2,1)} %cot_ref.1), custom_call_target="tpu_custom_call" | custom-call | tf_op jit(solution)/shard_map/pallas_call | solution.py:368
  111.5 1.7 %fusion = bf16[512,128]{1,0:T(8,128)(2,1)} fusion(f32[512,128]{1,0:T(8,128)} %get-tuple-element.6), kind=kLoop, calls=%fused_computation.1 | loop fusion | flops 262144 | bytes 393216 | tf_op jit(solution)/shard_map/convert_element_type | solution.py:652
  113.2 1.6 %broadcast_multiply_fusion = f32[128,256]{1,0:T(8,128)} fusion(f32[128,256]{1,0:T(8,128)} %get-tuple-element.8), kind=kLoop, calls=%fused_computation.2 | loop fusion | flops 32768 | bytes 262144 | tf_op jit(solution)/shard_map/mul | solution.py:654
  114.7 7.8 %shard_map.97 = bf16[8192,128]{1,0:T(8,128)(2,1)} custom-call(s32[256]{0:T(256)} %bitcast.17, s32[256]{0:T(256)} %fusion.3.cols_ref, s32[1]{0:T(128)} %bitcast.9.count_ref, bf16[256,128,128]{2,1,0:T(8,128)(2,1)} %bitcast.11, bf16[4096,128]{1,0:T(8,128)(2,1)} %bitcast.15), custom_call_target="tpu_custom_call" | custom-call | flops 1073741824 | bytes 11534336 | tf_op jit(solution)/shard_map/pallas_call | solution.py:60
  122.5 32.4 %shard_map.98 = bf16[512,128]{1,0:T(8,128)(2,1)} custom-call(bf16[2,8,512,128]{3,2,1,0:T(8,128)(2,1)} %bitcast.12), custom_call_target="tpu_custom_call" | custom-call | tf_op jit(solution)/shard_map/pallas_call | solution.py:284
  154.9 1.6 %copy.12 = bf16[512,128]{1,0:T(8,128)(2,1)} copy(bf16[512,128]{1,0:T(8,128)(2,1)} %shard_map.98) | data formatting | bytes 262144
Async XLA Ops:
  0.6 2.0 %copy-start = (bf16[256,256]{1,0:T(8,128)(2,1)S(1)}, bf16[256,256]{1,0:T(8,128)(2,1)}, u32[]{:S(2)}) copy-start(bf16[256,256]{1,0:T(8,128)(2,1)} %param.12) | copy-start | bytes 393220

commit v19 on v14

--- a/solution.py
+++ b/solution.py
@@ -310,7 +310,7 @@
         copy.wait_send()
 
 
-def layer_kernel(x_ref, w_ref, wr_ref, cot_ref, hidden_ref, panel_ref, sum_ref,
+def layer_kernel(scale, x_ref, w_ref, wr_ref, cot_ref, hidden_ref, panel_ref, sum_ref,
                  recv_ref, send_sems, recv_sems, summed_ref, agg_ref, grad_out_ref, grad_ref,
                  f_send, f_recv, term_ref, spread_ref, g_send, g_recv, *reduce_scratch):
     n_col = lax.axis_size("col")
@@ -345,14 +345,15 @@
     spread_ref[...] = spread.astype(spread_ref.dtype)
     copies = exchange_start("col", 1, n_col, "gather", spread_ref, panel_ref, g_send, g_recv)
     if radix:
-        reduce_radix(term_ref, sum_ref, *reduce_scratch)
+        reduce_radix(term_ref, sum_ref, *reduce_scratch, scale=scale)
     else:
         reduce_rounds(term_ref, sum_ref, *reduce_scratch)
+        sum_ref[...] = sum_ref[...] * scale
     exchange_finish("col", 1, n_col, "gather", spread_ref, panel_ref, panel_ref, g_send, g_recv,
                     copies)
 
 
-def layer_step(partials, weight_cols, weight_rows, cotangent, collective_id):
+def layer_step(partials, weight_cols, weight_rows, cotangent, collective_id, scale):
     n_col = lax.axis_size("col")
     n_feat = lax.axis_size("feat")
     block = partials.shape[1:]
@@ -361,7 +362,7 @@
     reduce_space = radix_scratch(term) if radix_fits(term) else reduce_scratch(term)
     vmem = pl.BlockSpec(memory_space=pltpu.VMEM)
     return pl.pallas_call(
-        layer_kernel,
+        functools.partial(layer_kernel, scale),
         out_shape=(
             jax.ShapeDtypeStruct(block, jnp.float32),
             jax.ShapeDtypeStruct((n_col,) + block, jnp.bfloat16),
@@ -516,7 +517,7 @@
     return total
 
 
-def reduce_radix(w_ref, o_ref, seg_recv, z_recv, x_recv, sems):
+def reduce_radix(w_ref, o_ref, seg_recv, z_recv, x_recv, sems, scale=1.0):
     _, z_group, x_group = radix_groups()
     me, size, member = first_group()
     seg = w_ref.shape[0] // size
@@ -542,7 +543,7 @@
         copy.wait_send()
     total = ordered_allreduce(z_group, total, z_recv, sems.at[2], sems.at[3])
     total = ordered_allreduce(x_group, total, x_recv, sems.at[4], sems.at[5])
-    o_ref[mine] = total
+    o_ref[mine] = total * scale
     copies = []
     for d in range(1, size):
         peer = lax.rem(me + d, size)
@@ -642,11 +643,12 @@
     weight_cols = lax.dynamic_slice_in_dim(weights, feat_index * feat_half, feat_half, 1)
     weight_rows = lax.dynamic_slice_in_dim(weights, feat_index * feat_half, feat_half, 0)
     hidden, spread_panel, weight_sum = layer_step(partial_value.reshape(n_coldev, -1, feat_half),
-                                                  weight_cols, weight_rows, cotangent, 1)
+                                                  weight_cols, weight_rows, cotangent, 1,
+                                                  node_total ** (-0.5))
     negative = jnp.minimum(hidden, 0.0)
     activated = jnp.where(hidden > 0, hidden, jnp.expm1(negative)).astype(jnp.bfloat16)
     spread_panel = spread_panel.reshape(-1, feat_half)
-    weight_grad = weight_sum * node_total ** (-0.5)
+    weight_grad = weight_sum
     back_partial = tile_products(local_tiles, block_rows, block_cols, count, spread_panel,
                                  col_blocks, transpose=True)
     if pair == 2:

time: 158 us -> 157 us (level)
  other arithmetic: 4.57 us -> 2.99 us
    pallas_call x2, Pallas kernels: 17.1 us -> 15.2 us  [tile_products(): pl.pallas_call(functools.partial(tile_kernel, transpose), out_shape=jax.S...]
where the time goes in v19:
time: 157 us; the launch traced here: 156 us
  Pallas kernels  148 us (94%)
  local copies, waits for them, and re-layouts  3.51 us (2%)
  other arithmetic  2.99 us (2%)
    pallas_call x1, Pallas kernels, layer_step(): pl.pallas_call(functools.partial(layer_kernel, scale), out_shape=(jax.Sha...  63.6 us
    pallas_call x1, Pallas kernels, row_gather(): pl.pallas_call(functools.partial(row_gather_kernel, chips), out_shape=jax...  36 us
    pallas_call x1, Pallas kernels, row_scatter(): pl.pallas_call(functools.partial(row_scatter_kernel, chips), out_shape=ja...  33.3 us
    pallas_call x2, Pallas kernels, tile_products(): pl.pallas_call(functools.partial(tile_kernel, transpose), out_shape=jax.S...  15.2 us

profile of v19, /device:TPU:1, one launch (start us, length us, event | category | flops | bytes accessed | tf_op | source)
XLA Modules:
  0.0 156.0 jit_solution(12619345841594998790)
XLA Ops:
  0.6 0.0 copy-start
  1.3 1.3 fusion.3.cols_ref
  2.6 0.0 copy-done
  2.6 0.6 constant_dynamic-slice_fusion.wr_ref
  3.2 0.6 constant_dynamic-slice_fusion.1.w_ref
  3.9 36.0 %shard_map.94 = bf16[2,8,512,128]{3,2,1,0:T(8,128)(2,1)} custom-call(bf16[512,128]{1,0:T(8,128)(2,1)} %x_ref.1), custom_call_target="tpu_custom_call" | custom-call | tf_op jit(solution)/shard_map/pallas_call | solution.py:224
  39.9 7.4 %shard_map.95 = bf16[4096,128]{1,0:T(8,128)(2,1)} custom-call(s32[256]{0:T(256)} %bitcast.16, s32[256]{0:T(256)} %fusion.3.cols_ref, s32[1]{0:T(128)} %bitcast.8.count_ref, bf16[256,128,128]{2,1,0:T(8,128)(2,1)} %bitcast.10, bf16[8192,128]{1,0:T(8,128)(2,1)} %bitcast.13), custom_call_target="tpu_custom_call" | custom-call | flops 1073741824 | bytes 11534336 | tf_op jit(solution)/shard_map/pallas_call | solution.py:60
  47.3 63.6 %shard_map.96 = (f32[512,128]{1,0:T(8,128)}, bf16[8,512,128]{2,1,0:T(8,128)(2,1)}, f32[128,256]{1,0:T(8,128)}) custom-call(bf16[8,512,128]{2,1,0:T(8,128)(2,1)} %bitcast.14, bf16[256,128]{1,0:T(8,128)(2,1)} %constant_dynamic-slice_fusion.1.w_ref, bf16[128,256]{1,0:T(8,128)(2,1)} %constant_dynamic-slice_fusion.wr_ref, bf16[512,128]{1,0:T(8,128)(2,1)} %cot_ref.1), custom_call_target="tpu_custom_call" | custom-call | tf_op jit(solution)/shard_map/pallas_call | solution.py:364
  110.9 1.7 %fusion = bf16[512,128]{1,0:T(8,128)(2,1)} fusion(f32[512,128]{1,0:T(8,128)} %get-tuple-element.6), kind=kLoop, calls=%fused_computation.1 | loop fusion | flops 262144 | bytes 393216 | tf_op jit(solution)/shard_map/convert_element_type | solution.py:649
  112.7 7.8 %shard_map.97 = bf16[8192,128]{1,0:T(8,128)(2,1)} custom-call(s32[256]{0:T(256)} %bitcast.17, s32[256]{0:T(256)} %fusion.3.cols_ref, s32[1]{0:T(128)} %bitcast.9.count_ref, bf16[256,128,128]{2,1,0:T(8,128)(2,1)} %bitcast.11, bf16[4096,128]{1,0:T(8,128)(2,1)} %bitcast.15), custom_call_target="tpu_custom_call" | custom-call | flops 1073741824 | bytes 11534336 | tf_op jit(solution)/shard_map/pallas_call | solution.py:60
  120.4 0.0 copy-start.1
  120.4 33.3 %shard_map.98 = bf16[512,128]{1,0:T(8,128)(2,1)} custom-call(bf16[2,8,512,128]{3,2,1,0:T(8,128)(2,1)} %bitcast.12), custom_call_target="tpu_custom_call" | custom-call | tf_op jit(solution)/shard_map/pallas_call | solution.py:279
  153.8 1.6 %copy.13 = bf16[512,128]{1,0:T(8,128)(2,1)} copy(bf16[512,128]{1,0:T(8,128)(2,1)} %shard_map.98) | data formatting | bytes 262144
  155.4 0.0 copy-done.1
  155.4 0.7 copy.14
Async XLA Ops:
  0.6 2.0 %copy-start = (bf16[256,256]{1,0:T(8,128)(2,1)S(1)}, bf16[256,256]{1,0:T(8,128)(2,1)}, u32[]{:S(2)}) copy-start(bf16[256,256]{1,0:T(8,128)(2,1)} %param.12) | copy-start | bytes 393220
  120.4 34.9 %copy-start.1 = (f32[128,256]{1,0:T(8,128)S(1)}, f32[128,256]{1,0:T(8,128)}, u32[]{:S(2)}) copy-start(f32[128,256]{1,0:T(8,128)} %get-tuple-element.14) | copy-start | bytes 393220

commit v20 on v17

--- a/solution.py
+++ b/solution.py
@@ -310,7 +310,7 @@
         copy.wait_send()
 
 
-def layer_kernel(x_ref, w_ref, wr_ref, cot_ref, hidden_ref, panel_ref, sum_ref,
+def layer_kernel(scale, x_ref, w_ref, wr_ref, cot_ref, hidden_ref, panel_ref, sum_ref,
                  recv_ref, send_sems, recv_sems, summed_ref, agg_ref, grad_out_ref, grad_ref,
                  f_send, f_recv, term_ref, spread_ref, g_send, g_recv, *reduce_scratch):
     n_col = lax.axis_size("col")
@@ -345,14 +345,15 @@
     spread_ref[...] = spread.astype(spread_ref.dtype)
     copies = exchange_start("col", 1, n_col, "gather", spread_ref, panel_ref, g_send, g_recv)
     if radix:
-        reduce_radix(term_ref, sum_ref, *reduce_scratch)
+        reduce_radix(term_ref, sum_ref, *reduce_scratch, scale=scale)
     else:
         reduce_rounds(term_ref, sum_ref, *reduce_scratch)
+        sum_ref[...] = sum_ref[...] * scale
     exchange_finish("col", 1, n_col, "gather", spread_ref, panel_ref, panel_ref, g_send, g_recv,
                     copies)
 
 
-def layer_step(partials, weight_cols, weight_rows, cotangent, collective_id):
+def layer_step(partials, weight_cols, weight_rows, cotangent, collective_id, scale):
     n_col = lax.axis_size("col")
     n_feat = lax.axis_size("feat")
     block = partials.shape[1:]
@@ -361,7 +362,7 @@
     reduce_space = radix_scratch(term) if radix_fits(term) else reduce_scratch(term)
     vmem = pl.BlockSpec(memory_space=pltpu.VMEM)
     return pl.pallas_call(
-        layer_kernel,
+        functools.partial(layer_kernel, scale),
         out_shape=(
             jax.ShapeDtypeStruct(block, jnp.float32),
             jax.ShapeDtypeStruct((n_col,) + block, jnp.bfloat16),
@@ -516,7 +517,7 @@
     return total
 
 
-def reduce_radix(w_ref, o_ref, seg_recv, z_recv, x_recv, sems):
+def reduce_radix(w_ref, o_ref, seg_recv, z_recv, x_recv, sems, scale=1.0):
     _, z_group, x_group = radix_groups()
     me, size, member = first_group()
     seg = w_ref.shape[0] // size
@@ -542,7 +543,7 @@
         copy.wait_send()
     total = ordered_allreduce(z_group, total, z_recv, sems.at[2], sems.at[3])
     total = ordered_allreduce(x_group, total, x_recv, sems.at[4], sems.at[5])
-    o_ref[mine] = total
+    o_ref[mine] = total * scale
     copies = []
     for d in range(1, size):
         peer = lax.rem(me + d, size)
@@ -645,11 +646,12 @@
     weight_cols = lax.dynamic_slice_in_dim(weights, feat_index * feat_half, feat_half, 1)
     weight_rows = lax.dynamic_slice_in_dim(weights, feat_index * feat_half, feat_half, 0)
     hidden, spread_panel, weight_sum = layer_step(partial_value.reshape(n_coldev, -1, feat_half),
-                                                  weight_cols, weight_rows, cotangent, 1)
+                                                  weight_cols, weight_rows, cotangent, 1,
+                                                  node_total ** (-0.5))
     negative = jnp.minimum(hidden, 0.0)
     activated = jnp.where(hidden > 0, hidden, jnp.expm1(negative)).astype(jnp.bfloat16)
     spread_panel = spread_panel.reshape(-1, feat_half)
-    weight_grad = weight_sum * node_total ** (-0.5)
+    weight_grad = weight_sum
     back_partial = tile_products(local_tiles, block_rows, block_cols, count, spread_panel,
                                  col_blocks, transpose=True, remap=remap)
     if pair == 2:

time: 158 us -> 159 us (level)
  the two profiles are of different devices: /device:TPU:6 before, /device:TPU:1 now
where the time goes in v20:
time: 159 us; the launch traced here: 156 us
  Pallas kernels  149 us (94%)
  local copies, waits for them, and re-layouts  3.73 us (2%)
  other arithmetic  1.71 us (1%)
    pallas_call x1, Pallas kernels, layer_step(): pl.pallas_call(functools.partial(layer_kernel, scale), out_shape=(jax.Sha...  64 us
    pallas_call x1, Pallas kernels, row_gather(): pl.pallas_call(functools.partial(row_gather_kernel, chips), out_shape=jax...  36 us
    pallas_call x1, Pallas kernels, row_scatter(): pl.pallas_call(functools.partial(row_scatter_kernel, chips), out_shape=ja...  29.3 us
    pallas_call x2, Pallas kernels, tile_products(): pl.pallas_call(functools.partial(tile_kernel, transpose, remap), out_shap...  19.6 us

profile of v20, /device:TPU:1, one launch (start us, length us, event | category | flops | bytes accessed | tf_op | source)
XLA Modules:
  0.0 155.8 jit_solution(15437546605601358620)
XLA Ops:
  0.6 0.0 copy-start
  1.3 0.2 copy-done
  1.6 0.6 constant_dynamic-slice_fusion.wr_ref
  2.2 0.6 constant_dynamic-slice_fusion.1.w_ref
  2.8 36.0 %shard_map.94 = bf16[2,8,512,128]{3,2,1,0:T(8,128)(2,1)} custom-call(bf16[512,128]{1,0:T(8,128)(2,1)} %x_ref.1), custom_call_target="tpu_custom_call" | custom-call | tf_op jit(solution)/shard_map/pallas_call | solution.py:224
  38.9 9.7 %shard_map.95 = bf16[4096,128]{1,0:T(8,128)(2,1)} custom-call(s32[256]{0:T(256)} %bitcast.16, s32[256]{0:T(256)} %bitcast.18, s32[1]{0:T(128)} %bitcast.8.count_ref, bf16[256,128,128]{2,1,0:T(8,128)(2,1)} %bitcast.10, bf16[8192,128]{1,0:T(8,128)(2,1)} %bitcast.13), custom_call_target="tpu_custom_call" | custom-call | flops 1073741824 | bytes 11534336 | tf_op jit(solution)/shard_map/pallas_call | solution.py:60
  48.6 64.0 %shard_map.96 = (f32[512,128]{1,0:T(8,128)}, bf16[8,512,128]{2,1,0:T(8,128)(2,1)}, f32[128,256]{1,0:T(8,128)}) custom-call(bf16[8,512,128]{2,1,0:T(8,128)(2,1)} %bitcast.14, bf16[256,128]{1,0:T(8,128)(2,1)} %constant_dynamic-slice_fusion.1.w_ref, bf16[128,256]{1,0:T(8,128)(2,1)} %constant_dynamic-slice_fusion.wr_ref, bf16[512,128]{1,0:T(8,128)(2,1)} %cot_ref.1), custom_call_target="tpu_custom_call" | custom-call | tf_op jit(solution)/shard_map/pallas_call | solution.py:364
  112.6 1.7 %fusion = bf16[512,128]{1,0:T(8,128)(2,1)} fusion(f32[512,128]{1,0:T(8,128)} %get-tuple-element.6), kind=kLoop, calls=%fused_computation.1 | loop fusion | flops 262144 | bytes 393216 | tf_op jit(solution)/shard_map/convert_element_type | solution.py:652
  114.3 9.9 %shard_map.97 = bf16[8192,128]{1,0:T(8,128)(2,1)} custom-call(s32[256]{0:T(256)} %bitcast.17, s32[256]{0:T(256)} %bitcast.19, s32[1]{0:T(128)} %bitcast.9.count_ref, bf16[256,128,128]{2,1,0:T(8,128)(2,1)} %bitcast.11, bf16[4096,128]{1,0:T(8,128)(2,1)} %bitcast.15), custom_call_target="tpu_custom_call" | custom-call | flops 1073741824 | bytes 11534336 | tf_op jit(solution)/shard_map/pallas_call | solution.py:60
  124.3 0.0 copy-start.1
  124.3 29.3 %shard_map.98 = bf16[512,128]{1,0:T(8,128)(2,1)} custom-call(bf16[2,8,512,128]{3,2,1,0:T(8,128)(2,1)} %bitcast.12), custom_call_target="tpu_custom_call" | custom-call | tf_op jit(solution)/shard_map/pallas_call | solution.py:279
  153.6 1.6 %copy.13 = bf16[512,128]{1,0:T(8,128)(2,1)} copy(bf16[512,128]{1,0:T(8,128)(2,1)} %shard_map.98) | data formatting | bytes 262144
  155.1 0.0 copy-done.1
  155.1 0.7 copy.14
Async XLA Ops:
  0.6 0.9 copy-start
  124.3 30.9 %copy-start.1 = (f32[128,256]{1,0:T(8,128)S(1)}, f32[128,256]{1,0:T(8,128)}, u32[]{:S(2)}) copy-start(f32[128,256]{1,0:T(8,128)} %get-tuple-element.14) | copy-start | bytes 393220
